TPU v7x, 32 devices: a whole 2x2x4 slice. The times are simulated.
32 devices in a mesh: section: 2 (over x), seq: 16 (over z, y, core).
Axes of the slice: x: 2, y: 2, z: 4, core: 2. Of those that a mesh axis runs over, the one named last changes fastest.
Arguments:
- latents: bfloat16 [4, 1024, 1024], P(None, 'seq'), may hold values from -6 to 6
- norm_gain: float32 [2, 1024], P('section'), may hold values from 0.1 to 1.9
- qkv_weight: bfloat16 [2, 1024, 3072], P('section', 'seq'), may hold values from -1 to 1
- proj_weight: bfloat16 [2, 1024, 1024], P('section', 'seq'), may hold values from -0.1875 to 0.1875
- merge_weight: bfloat16 [2, 1024, 1024], P('section', 'seq'), may hold values from -0.125 to 0.125
Outputs:
- denoised: bfloat16 [4, 1024, 1024], P(None, 'seq', 'section')
All inputs are finite; a program needn't handle non-finite values.
Results may differ from a plain program's by a relative error of at most 0.017.
Values may be sent and summed in bfloat16 or wider, within the bound.
No kernel may reach another device: no remote copies, remote signals or barrier semaphores. Data moves between devices by JAX's collectives and lax.ppermute only.
A program may use at most 64 MiB of HBM per device.

v0:
```python
import jax
import jax.numpy as jnp
from jax import lax
from jax.sharding import PartitionSpec as P

HEADS = 16
HEAD_DIM = 64


EPSILON = 1e-05


def partner(value, axis, bit):
    mask = 2**bit
    pairs = [(source, source ^ mask) for source in range(lax.axis_size(axis))]
    return lax.ppermute(value, axis, pairs)


def shifted(value, axis, steps):
    count = lax.axis_size(axis)
    initial, last = (max(0, -steps), min(count, count - steps))
    return lax.ppermute(value, axis, [(source, source + steps) for source in range(initial, last)])


def layer_norm(hidden, gain_row):
    values = hidden.astype(jnp.float32)
    center = values - jnp.mean(values, axis=-1, keepdims=True)
    spread = jnp.mean(center * center, axis=-1, keepdims=True)
    return (center * lax.rsqrt(spread + EPSILON) * gain_row).astype(jnp.bfloat16)


def body(latents, norm_gain, qkv_weight, proj_weight, merge_weight):
    seq_count = lax.axis_size("seq")
    section_count = lax.axis_size("section")
    my_section = lax.axis_index("section")
    midpoint = section_count // 2
    windows = latents.shape[0]
    tok_rows = latents.shape[1]
    features = latents.shape[2]
    repeat = max(seq_count // HEADS, 1)
    groups = seq_count // repeat
    head_cols = features * repeat // seq_count
    per_device = head_cols // HEAD_DIM
    part_rows = tok_rows // repeat
    scale_factor = HEAD_DIM ** (-0.5)
    w_qkv, w_proj, w_merge = (
        lax.all_gather(qkv_weight, "seq", axis=1, tiled=True),
        lax.all_gather(proj_weight, "seq", axis=1, tiled=True),
        lax.all_gather(merge_weight, "seq", axis=1, tiled=True),
    )
    w_qkv = w_qkv[0]
    w_proj = w_proj[0]
    w_merge = w_merge[0]
    gain_row = norm_gain[0]
    decoder = my_section >= midpoint
    encoder = my_section < midpoint
    query_shape = (seq_count, part_rows * head_cols)
    key_shape = (seq_count, tok_rows * head_cols)

    def to_heads(array_in, spread_copies):
        if spread_copies:
            grouped = array_in.reshape(tok_rows, groups, head_cols).transpose(1, 0, 2)
            grouped = grouped.reshape(groups, 1, tok_rows * head_cols)
            grouped = jnp.broadcast_to(grouped, (groups, repeat, tok_rows * head_cols))
            return grouped.reshape(seq_count, tok_rows * head_cols)
        grouped = array_in.reshape(part_rows, repeat, groups, head_cols).transpose(2, 1, 0, 3)
        return grouped.reshape(seq_count, part_rows * head_cols)

    def from_heads(array_in):
        grouped = array_in.reshape(groups, repeat, part_rows, head_cols).transpose(2, 1, 0, 3)
        return grouped.reshape(tok_rows, features)

    def project(carried):
        normed = layer_norm(carried, gain_row)
        packed = jnp.dot(normed, w_qkv, preferred_element_type=jnp.float32).astype(jnp.bfloat16)
        return (
            to_heads(packed[:, :features], False),
            to_heads(packed[:, features : 2 * features], True),
            to_heads(packed[:, 2 * features :], True),
        )

    def spare_heads():
        return (
            jnp.zeros(query_shape, jnp.bfloat16),
            jnp.zeros(key_shape, jnp.bfloat16),
            jnp.zeros(key_shape, jnp.bfloat16),
        )

    def attend(queries, keys_in, values_in):
        query_rows = queries.reshape(-1, per_device, HEAD_DIM)
        key_rows = keys_in.reshape(-1, per_device, HEAD_DIM)
        value_rows = values_in.reshape(-1, per_device, HEAD_DIM)
        block_rows = min(512, query_rows.shape[0])
        blocked = query_rows.reshape(-1, block_rows, per_device, HEAD_DIM)

        def one_block(query_block):
            scores = (
                jnp.einsum(
                    "qhd,khd->hqk", query_block, key_rows, preferred_element_type=jnp.float32
                )
                * scale_factor
            )
            row_max = jnp.max(scores, axis=-1, keepdims=True)
            weights = jnp.exp(scores - row_max)
            totals = jnp.sum(weights, axis=-1)
            probs = weights.astype(jnp.bfloat16)
            mixed = jnp.einsum(
                "hqk,khd->qhd", probs, value_rows, preferred_element_type=jnp.float32
            )
            return (mixed / totals.T[:, :, None]).astype(jnp.bfloat16)

        return lax.map(one_block, blocked).reshape(query_shape)

    def mirror_each(skip_term):
        for bit_no in range(section_count.bit_length() - 1):
            skip_term = partner(skip_term, "section", bit_no)
        return skip_term

    def tick(tick_no, loop_state):
        incoming, skip_store, result = loop_state
        window_no = tick_no - my_section
        active = (window_no >= 0) & (window_no < windows)
        chosen = jnp.clip(window_no, 0, windows - 1)
        fresh = lax.dynamic_index_in_dim(latents, chosen, 0, keepdims=False)
        entering = jnp.where(my_section == 0, fresh, incoming)
        skip_slot = lax.dynamic_index_in_dim(skip_store, chosen, 0, keepdims=False)
        carried = lax.cond(
            active & decoder,
            lambda: (
                jnp.dot(entering, w_merge, preferred_element_type=jnp.float32)
                + skip_slot.astype(jnp.float32)
            ).astype(jnp.bfloat16),
            lambda: entering,
        )
        queries, keys_in, values_in = lax.cond(active, lambda: project(carried), spare_heads)
        queries, keys_in, values_in = (
            lax.all_to_all(queries, "seq", split_axis=0, concat_axis=0, tiled=True),
            lax.all_to_all(keys_in, "seq", split_axis=0, concat_axis=0, tiled=True),
            lax.all_to_all(values_in, "seq", split_axis=0, concat_axis=0, tiled=True),
        )
        attended = lax.cond(
            active,
            lambda: attend(queries, keys_in, values_in),
            lambda: jnp.zeros(query_shape, jnp.bfloat16),
        )
        attended = lax.all_to_all(attended, "seq", split_axis=0, concat_axis=0, tiled=True)
        leaving = lax.cond(
            active,
            lambda: (
                carried.astype(jnp.float32)
                + jnp.dot(from_heads(attended), w_proj, preferred_element_type=jnp.float32)
            ).astype(jnp.bfloat16),
            lambda: carried,
        )
        skip_term = lax.cond(
            active & encoder,
            lambda: jnp.dot(leaving, w_merge, preferred_element_type=jnp.float32).astype(
                jnp.bfloat16
            ),
            lambda: jnp.zeros_like(leaving),
        )
        arrived = mirror_each(skip_term)
        source_no = tick_no - (section_count - 1 - my_section)
        landing = decoder & (source_no >= 0) & (source_no < windows)
        target = jnp.clip(source_no, 0, windows - 1)
        updated = lax.dynamic_update_index_in_dim(skip_store, arrived, target, 0)
        skip_store = jnp.where(landing, updated, skip_store)
        incoming = shifted(leaving, "section", 1)
        finished = lax.dynamic_update_index_in_dim(result, leaving.astype(jnp.float32), chosen, 0)
        result = jnp.where(active & (my_section == section_count - 1), finished, result)
        return (incoming, skip_store, result)

    loop_state = (
        jnp.zeros(latents.shape[1:], jnp.bfloat16),
        jnp.zeros_like(latents),
        jnp.zeros(latents.shape, jnp.float32),
    )
    loop_state = lax.fori_loop(0, windows + section_count - 1, tick, loop_state)
    result = loop_state[2]
    return lax.psum_scatter(result.astype(jnp.bfloat16), "section", scatter_dimension=2, tiled=True)


def solution(mesh):
    placed = (
        P(None, "seq", None),
        P("section", None),
        P("section", "seq", None),
        P("section", "seq", None),
        P("section", "seq", None),
    )
    return jax.shard_map(
        body, mesh=mesh, in_specs=placed, out_specs=P(None, "seq", "section"), check_vma=False
    )
```

profile of v0, /device:TPU:0, one launch (start us, length us, event | category | flops | bytes accessed | tf_op | source)
XLA Modules:
  0.0 594.8 jit_solution(4779026322006849936)
XLA Ops:
  8.8 44.9 %all-gather.4.cloned.1.call-done = bf16[1,1024,1024]{2,1,0:T(8,128)(2,1)} async-done(((bf16[1,64,1024]{2,1,0:T(8,128)(2,1)}), bf16[1,1024,1024]{2,1,0:T(8,128)(2,1)}) %all-gather.4.cloned.1.call-update) | async-done | bytes 2097168 | tf_op jit(solution)/shard_map/all_gather | solution.py:49
  53.7 42.4 %all-gather.8.cloned.1.call-done = bf16[1,1024,1024]{2,1,0:T(8,128)(2,1)} async-done(((bf16[1,64,1024]{2,1,0:T(8,128)(2,1)}), bf16[1,1024,1024]{2,1,0:T(8,128)(2,1)}) %all-gather.8.cloned.1.call-update) | async-done | bytes 2097168 | tf_op jit(solution)/shard_map/all_gather | solution.py:48
  96.1 62.4 %all-gather.6.cloned.1.call-done = bf16[1,1024,3072]{2,1,0:T(8,128)(2,1)} async-done(((bf16[1,64,3072]{2,1,0:T(8,128)(2,1)}), bf16[1,1024,3072]{2,1,0:T(8,128)(2,1)}) %all-gather.6.cloned.1.call-update) | async-done | bytes 6291472 | tf_op jit(solution)/shard_map/all_gather | solution.py:47
  159.5 414.5 %while.28 = (s32[]{:T(128)}, bf16[64,1024]{1,0:T(8,128)(2,1)S(1)}, bf16[4,64,1024]{2,1,0:T(8,128)(2,1)S(1)}, bf16[4,64,1024]{2,1,0:T(8,128)(2,1)}, s32[]{:T(128)...) while((s32[]{:T(128)}, bf16[64,1024]{1,0:T(8,128)(2,1)S(1)}, ...), condition=%wide.region_17.18_spmd, body=%wide.region_0.17_spmd.sunk | while | flops 945355840 | bytes 44074696 | solution.py:178
  161.1 8.0 %conditional.12 = (bf16[16,4096]{1,0:T(8,128)(2,1)S(1)}, bf16[16,4096]{1,0:T(8,128)(2,1)S(1)}, bf16[16,4096]{1,0:T(8,128)(2,1)S(1)}) conditional(s32[]{:T(128)} %convert_element_type.121, () %tuple.109, (bf16[64,1024]{1,0:T(8,128)(2,1)}, f32[1,1024]{1,0:T(1,128)S(1)}, bf16[1024,3072]{1,0:T(8,128)(2,1)}) %tuple.147), branch_computations={%region_3.3_spmd, %region_4.6_spmd} | conditional | flops 403570752 | bytes 10230040 | solution.py:135
  176.4 5.9 all-to-all-done
  197.5 7.6 %all-to-all-done.2 = bf16[16,2,2048]{2,1,0:T(2,128)(2,1)S(1)} async-done(((bf16[16,2,2048]{2,1,0:T(2,128)(2,1)}), bf16[16,2,2048]{2,1,0:T(2,128)(2,1)S(1)}, u32[]{:S(2)}, u32[]{:S(2)}) %all-to-all-start.2) | async-done | bytes 131104 | tf_op jit(solution)/shard_map/while/body/eval_jaxpr/all_to_all | solution.py:139
  205.3 7.2 %conditional.13 = (bf16[16,4096]{1,0:T(8,128)(2,1)S(1)}) conditional(s32[]{:T(128)} %convert_element_type.121, () %tuple.112, (bf16[16,1,4096]{2,1,0:T(2,128)(2,1)S(1)}, bf16[16,1,4096]{2,1,0:T(2,128)(2,1)S(1)}, bf16[16,1,4096]{2,1,0:T(2,128)(2,1)S(1)}) %tuple.113), branch_computations={%region_7.7_spmd, %region_8.12_spmd} | conditional | flops 138476544 | bytes 9578643 | solution.py:141
  217.9 7.8 %all-to-all-done.3 = bf16[16,2,2048]{2,1,0:T(2,128)(2,1)S(1)} async-done(((bf16[16,2,2048]{2,1,0:T(2,128)(2,1)}), bf16[16,2,2048]{2,1,0:T(2,128)(2,1)S(1)}, u32[]{:S(2)}, u32[]{:S(2)}) %all-to-all-start.3) | async-done | bytes 131104 | tf_op jit(solution)/shard_map/while/body/eval_jaxpr/all_to_all | solution.py:146
  239.8 8.0 %conditional.12 = (bf16[16,4096]{1,0:T(8,128)(2,1)S(1)}, bf16[16,4096]{1,0:T(8,128)(2,1)S(1)}, bf16[16,4096]{1,0:T(8,128)(2,1)S(1)}) conditional(s32[]{:T(128)} %convert_element_type.121, () %tuple.109, (bf16[64,1024]{1,0:T(8,128)(2,1)}, f32[1,1024]{1,0:T(1,128)S(1)}, bf16[1024,3072]{1,0:T(8,128)(2,1)}) %tuple.147), branch_computations={%region_3.3_spmd, %region_4.6_spmd} | conditional | flops 403570752 | bytes 10230040 | solution.py:135
  255.1 5.9 all-to-all-done
  276.2 7.6 %all-to-all-done.2 = bf16[16,2,2048]{2,1,0:T(2,128)(2,1)S(1)} async-done(((bf16[16,2,2048]{2,1,0:T(2,128)(2,1)}), bf16[16,2,2048]{2,1,0:T(2,128)(2,1)S(1)}, u32[]{:S(2)}, u32[]{:S(2)}) %all-to-all-start.2) | async-done | bytes 131104 | tf_op jit(solution)/shard_map/while/body/eval_jaxpr/all_to_all | solution.py:139
  284.0 7.2 %conditional.13 = (bf16[16,4096]{1,0:T(8,128)(2,1)S(1)}) conditional(s32[]{:T(128)} %convert_element_type.121, () %tuple.112, (bf16[16,1,4096]{2,1,0:T(2,128)(2,1)S(1)}, bf16[16,1,4096]{2,1,0:T(2,128)(2,1)S(1)}, bf16[16,1,4096]{2,1,0:T(2,128)(2,1)S(1)}) %tuple.113), branch_computations={%region_7.7_spmd, %region_8.12_spmd} | conditional | flops 138476544 | bytes 9578643 | solution.py:141
  296.6 7.8 %all-to-all-done.3 = bf16[16,2,2048]{2,1,0:T(2,128)(2,1)S(1)} async-done(((bf16[16,2,2048]{2,1,0:T(2,128)(2,1)}), bf16[16,2,2048]{2,1,0:T(2,128)(2,1)S(1)}, u32[]{:S(2)}, u32[]{:S(2)}) %all-to-all-start.3) | async-done | bytes 131104 | tf_op jit(solution)/shard_map/while/body/eval_jaxpr/all_to_all | solution.py:146
  309.1 7.0 %collective-permute-start = (bf16[64,1024]{1,0:T(8,128)(2,1)}, bf16[64,1024]{1,0:T(8,128)(2,1)S(1)}, u32[]{:S(2)}, u32[]{:S(2)}) collective-permute-start(bf16[64,1024]{1,0:T(8,128)(2,1)} %get-tuple-element.591), channel_id=1, source_target_pairs={{0,16},{1,17},{2,18},{3,19},{4,20},{5,21},{6,22},{7,23},{8,24},{9,... | collective-permute-start | bytes 393224 | tf_op jit(solution)/shard_map/while/body/eval_jaxpr/ppermute | solution.py:22
  324.3 8.0 %conditional.12 = (bf16[16,4096]{1,0:T(8,128)(2,1)S(1)}, bf16[16,4096]{1,0:T(8,128)(2,1)S(1)}, bf16[16,4096]{1,0:T(8,128)(2,1)S(1)}) conditional(s32[]{:T(128)} %convert_element_type.121, () %tuple.109, (bf16[64,1024]{1,0:T(8,128)(2,1)}, f32[1,1024]{1,0:T(1,128)S(1)}, bf16[1024,3072]{1,0:T(8,128)(2,1)}) %tuple.147), branch_computations={%region_3.3_spmd, %region_4.6_spmd} | conditional | flops 403570752 | bytes 10230040 | solution.py:135
  339.6 5.9 all-to-all-done
  360.7 7.6 %all-to-all-done.2 = bf16[16,2,2048]{2,1,0:T(2,128)(2,1)S(1)} async-done(((bf16[16,2,2048]{2,1,0:T(2,128)(2,1)}), bf16[16,2,2048]{2,1,0:T(2,128)(2,1)S(1)}, u32[]{:S(2)}, u32[]{:S(2)}) %all-to-all-start.2) | async-done | bytes 131104 | tf_op jit(solution)/shard_map/while/body/eval_jaxpr/all_to_all | solution.py:139
  368.4 7.2 %conditional.13 = (bf16[16,4096]{1,0:T(8,128)(2,1)S(1)}) conditional(s32[]{:T(128)} %convert_element_type.121, () %tuple.112, (bf16[16,1,4096]{2,1,0:T(2,128)(2,1)S(1)}, bf16[16,1,4096]{2,1,0:T(2,128)(2,1)S(1)}, bf16[16,1,4096]{2,1,0:T(2,128)(2,1)S(1)}) %tuple.113), branch_computations={%region_7.7_spmd, %region_8.12_spmd} | conditional | flops 138476544 | bytes 9578643 | solution.py:141
  381.1 7.8 %all-to-all-done.3 = bf16[16,2,2048]{2,1,0:T(2,128)(2,1)S(1)} async-done(((bf16[16,2,2048]{2,1,0:T(2,128)(2,1)}), bf16[16,2,2048]{2,1,0:T(2,128)(2,1)S(1)}, u32[]{:S(2)}, u32[]{:S(2)}) %all-to-all-start.3) | async-done | bytes 131104 | tf_op jit(solution)/shard_map/while/body/eval_jaxpr/all_to_all | solution.py:146
  393.5 6.8 %collective-permute-start = (bf16[64,1024]{1,0:T(8,128)(2,1)}, bf16[64,1024]{1,0:T(8,128)(2,1)S(1)}, u32[]{:S(2)}, u32[]{:S(2)}) collective-permute-start(bf16[64,1024]{1,0:T(8,128)(2,1)} %get-tuple-element.591), channel_id=1, source_target_pairs={{0,16},{1,17},{2,18},{3,19},{4,20},{5,21},{6,22},{7,23},{8,24},{9,... | collective-permute-start | bytes 393224 | tf_op jit(solution)/shard_map/while/body/eval_jaxpr/ppermute | solution.py:22
  408.5 8.0 %conditional.12 = (bf16[16,4096]{1,0:T(8,128)(2,1)S(1)}, bf16[16,4096]{1,0:T(8,128)(2,1)S(1)}, bf16[16,4096]{1,0:T(8,128)(2,1)S(1)}) conditional(s32[]{:T(128)} %convert_element_type.121, () %tuple.109, (bf16[64,1024]{1,0:T(8,128)(2,1)}, f32[1,1024]{1,0:T(1,128)S(1)}, bf16[1024,3072]{1,0:T(8,128)(2,1)}) %tuple.147), branch_computations={%region_3.3_spmd, %region_4.6_spmd} | conditional | flops 403570752 | bytes 10230040 | solution.py:135
  423.8 5.9 all-to-all-done
  444.9 7.6 %all-to-all-done.2 = bf16[16,2,2048]{2,1,0:T(2,128)(2,1)S(1)} async-done(((bf16[16,2,2048]{2,1,0:T(2,128)(2,1)}), bf16[16,2,2048]{2,1,0:T(2,128)(2,1)S(1)}, u32[]{:S(2)}, u32[]{:S(2)}) %all-to-all-start.2) | async-done | bytes 131104 | tf_op jit(solution)/shard_map/while/body/eval_jaxpr/all_to_all | solution.py:139
  452.6 7.2 %conditional.13 = (bf16[16,4096]{1,0:T(8,128)(2,1)S(1)}) conditional(s32[]{:T(128)} %convert_element_type.121, () %tuple.112, (bf16[16,1,4096]{2,1,0:T(2,128)(2,1)S(1)}, bf16[16,1,4096]{2,1,0:T(2,128)(2,1)S(1)}, bf16[16,1,4096]{2,1,0:T(2,128)(2,1)S(1)}) %tuple.113), branch_computations={%region_7.7_spmd, %region_8.12_spmd} | conditional | flops 138476544 | bytes 9578643 | solution.py:141
  465.3 7.8 %all-to-all-done.3 = bf16[16,2,2048]{2,1,0:T(2,128)(2,1)S(1)} async-done(((bf16[16,2,2048]{2,1,0:T(2,128)(2,1)}), bf16[16,2,2048]{2,1,0:T(2,128)(2,1)S(1)}, u32[]{:S(2)}, u32[]{:S(2)}) %all-to-all-start.3) | async-done | bytes 131104 | tf_op jit(solution)/shard_map/while/body/eval_jaxpr/all_to_all | solution.py:146
  477.7 6.8 %collective-permute-start = (bf16[64,1024]{1,0:T(8,128)(2,1)}, bf16[64,1024]{1,0:T(8,128)(2,1)S(1)}, u32[]{:S(2)}, u32[]{:S(2)}) collective-permute-start(bf16[64,1024]{1,0:T(8,128)(2,1)} %get-tuple-element.591), channel_id=1, source_target_pairs={{0,16},{1,17},{2,18},{3,19},{4,20},{5,21},{6,22},{7,23},{8,24},{9,... | collective-permute-start | bytes 393224 | tf_op jit(solution)/shard_map/while/body/eval_jaxpr/ppermute | solution.py:22
  500.1 5.9 all-to-all-done
  521.2 7.6 %all-to-all-done.2 = bf16[16,2,2048]{2,1,0:T(2,128)(2,1)S(1)} async-done(((bf16[16,2,2048]{2,1,0:T(2,128)(2,1)}), bf16[16,2,2048]{2,1,0:T(2,128)(2,1)S(1)}, u32[]{:S(2)}, u32[]{:S(2)}) %all-to-all-start.2) | async-done | bytes 131104 | tf_op jit(solution)/shard_map/while/body/eval_jaxpr/all_to_all | solution.py:139
  534.4 7.8 %all-to-all-done.3 = bf16[16,2,2048]{2,1,0:T(2,128)(2,1)S(1)} async-done(((bf16[16,2,2048]{2,1,0:T(2,128)(2,1)}), bf16[16,2,2048]{2,1,0:T(2,128)(2,1)S(1)}, u32[]{:S(2)}, u32[]{:S(2)}) %all-to-all-start.3) | async-done | bytes 131104 | tf_op jit(solution)/shard_map/while/body/eval_jaxpr/all_to_all | solution.py:146
  544.1 24.6 %collective-permute-start = (bf16[64,1024]{1,0:T(8,128)(2,1)}, bf16[64,1024]{1,0:T(8,128)(2,1)S(1)}, u32[]{:S(2)}, u32[]{:S(2)}) collective-permute-start(bf16[64,1024]{1,0:T(8,128)(2,1)} %get-tuple-element.591), channel_id=1, source_target_pairs={{0,16},{1,17},{2,18},{3,19},{4,20},{5,21},{6,22},{7,23},{8,24},{9,... | collective-permute-start | bytes 393224 | tf_op jit(solution)/shard_map/while/body/eval_jaxpr/ppermute | solution.py:22
  574.0 14.3 %reduce-scatter.2.cloned.1.call-done = bf16[4,64,512]{2,1,0:T(8,128)(2,1)} async-done(((bf16[4,64,1024]{2,1,0:T(8,128)(2,1)}), bf16[4,64,512]{2,1,0:T(8,128)(2,1)}) %reduce-scatter.2.cloned.1.call-update) | async-done | bytes 262160 | tf_op jit(solution)/shard_map/reduce_scatter | solution.py:180
  (354 shorter events, 301.1 us)
Async XLA Ops:
  6.5 47.2 %all-gather.4.cloned.1.call-start = ((), (), s32[]{:S(2)}) async-start(), calls=%async_computation.5 | async-start | bytes 2228224 | tf_op jit(solution)/shard_map/all_gather | solution.py:49
  7.3 88.8 %all-gather.8.cloned.1.call-start = ((), (), s32[]{:S(2)}) async-start(), calls=%async_computation.7 | async-start | bytes 2228224 | tf_op jit(solution)/shard_map/all_gather | solution.py:48
  8.0 150.5 %all-gather.6.cloned.1.call-start = ((), (), s32[]{:S(2)}) async-start(), calls=%async_computation.6 | async-start | bytes 6684672 | tf_op jit(solution)/shard_map/all_gather | solution.py:47
  8.7 579.5 %reduce-scatter.2.cloned.1.call-start = ((), (), s32[]{:S(2)}) async-start(), calls=%async_computation.8 | async-start | bytes 786432 | tf_op jit(solution)/shard_map/reduce_scatter | solution.py:180
  171.0 11.4 %all-to-all-start = ((bf16[16,2,2048]{2,1,0:T(2,128)(2,1)}), bf16[16,2,2048]{2,1,0:T(2,128)(2,1)S(1)}, u32[]{:S(2)}, u32[]{:S(2)}) async-start(bf16[16,2,2048]{2,1,0:T(2,128)(2,1)} %reshape.146), calls=%async_computation | async-start | bytes 262144 | tf_op jit(solution)/shard_map/while/body/eval_jaxpr/all_to_all | solution.py:137
  182.4 11.4 %all-to-all-start.1 = ((bf16[16,2,2048]{2,1,0:T(2,128)(2,1)}), bf16[16,2,2048]{2,1,0:T(2,128)(2,1)S(1)}, u32[]{:S(2)}, u32[]{:S(2)}) async-start(bf16[16,2,2048]{2,1,0:T(2,128)(2,1)} %reshape.148), calls=%async_computation.1 | async-start | bytes 262144 | tf_op jit(solution)/shard_map/while/body/eval_jaxpr/all_to_all | solution.py:138
  193.8 11.4 %all-to-all-start.2 = ((bf16[16,2,2048]{2,1,0:T(2,128)(2,1)}), bf16[16,2,2048]{2,1,0:T(2,128)(2,1)S(1)}, u32[]{:S(2)}, u32[]{:S(2)}) async-start(bf16[16,2,2048]{2,1,0:T(2,128)(2,1)} %reshape.150), calls=%async_computation.2 | async-start | bytes 262144 | tf_op jit(solution)/shard_map/while/body/eval_jaxpr/all_to_all | solution.py:139
  214.4 11.4 %all-to-all-start.3 = ((bf16[16,2,2048]{2,1,0:T(2,128)(2,1)}), bf16[16,2,2048]{2,1,0:T(2,128)(2,1)S(1)}, u32[]{:S(2)}, u32[]{:S(2)}) async-start(bf16[16,2,2048]{2,1,0:T(2,128)(2,1)} %reshape.152), calls=%async_computation.3 | async-start | bytes 262144 | tf_op jit(solution)/shard_map/while/body/eval_jaxpr/all_to_all | solution.py:146
  230.4 7.8 %collective-permute-start = (bf16[64,1024]{1,0:T(8,128)(2,1)}, bf16[64,1024]{1,0:T(8,128)(2,1)S(1)}, u32[]{:S(2)}, u32[]{:S(2)}) collective-permute-start(bf16[64,1024]{1,0:T(8,128)(2,1)} %get-tuple-element.591), channel_id=1, source_target_pairs={{0,16},{1,17},{2,18},{3,19},{4,20},{5,21},{6,22},{7,23},{8,24},{9,... | collective-permute-start | bytes 393224 | tf_op jit(solution)/shard_map/while/body/eval_jaxpr/ppermute | solution.py:22
  233.1 5.0 collective-permute-start.1
  249.7 11.4 %all-to-all-start = ((bf16[16,2,2048]{2,1,0:T(2,128)(2,1)}), bf16[16,2,2048]{2,1,0:T(2,128)(2,1)S(1)}, u32[]{:S(2)}, u32[]{:S(2)}) async-start(bf16[16,2,2048]{2,1,0:T(2,128)(2,1)} %reshape.146), calls=%async_computation | async-start | bytes 262144 | tf_op jit(solution)/shard_map/while/body/eval_jaxpr/all_to_all | solution.py:137
  261.1 11.4 %all-to-all-start.1 = ((bf16[16,2,2048]{2,1,0:T(2,128)(2,1)}), bf16[16,2,2048]{2,1,0:T(2,128)(2,1)S(1)}, u32[]{:S(2)}, u32[]{:S(2)}) async-start(bf16[16,2,2048]{2,1,0:T(2,128)(2,1)} %reshape.148), calls=%async_computation.1 | async-start | bytes 262144 | tf_op jit(solution)/shard_map/while/body/eval_jaxpr/all_to_all | solution.py:138
  272.5 11.4 %all-to-all-start.2 = ((bf16[16,2,2048]{2,1,0:T(2,128)(2,1)}), bf16[16,2,2048]{2,1,0:T(2,128)(2,1)S(1)}, u32[]{:S(2)}, u32[]{:S(2)}) async-start(bf16[16,2,2048]{2,1,0:T(2,128)(2,1)} %reshape.150), calls=%async_computation.2 | async-start | bytes 262144 | tf_op jit(solution)/shard_map/while/body/eval_jaxpr/all_to_all | solution.py:139
  293.1 11.4 %all-to-all-start.3 = ((bf16[16,2,2048]{2,1,0:T(2,128)(2,1)}), bf16[16,2,2048]{2,1,0:T(2,128)(2,1)S(1)}, u32[]{:S(2)}, u32[]{:S(2)}) async-start(bf16[16,2,2048]{2,1,0:T(2,128)(2,1)} %reshape.152), calls=%async_computation.3 | async-start | bytes 262144 | tf_op jit(solution)/shard_map/while/body/eval_jaxpr/all_to_all | solution.py:146
  309.1 13.6 %collective-permute-start = (bf16[64,1024]{1,0:T(8,128)(2,1)}, bf16[64,1024]{1,0:T(8,128)(2,1)S(1)}, u32[]{:S(2)}, u32[]{:S(2)}) collective-permute-start(bf16[64,1024]{1,0:T(8,128)(2,1)} %get-tuple-element.591), channel_id=1, source_target_pairs={{0,16},{1,17},{2,18},{3,19},{4,20},{5,21},{6,22},{7,23},{8,24},{9,... | collective-permute-start | bytes 393224 | tf_op jit(solution)/shard_map/while/body/eval_jaxpr/ppermute | solution.py:22
  317.6 5.0 collective-permute-start.1
  334.1 11.4 %all-to-all-start = ((bf16[16,2,2048]{2,1,0:T(2,128)(2,1)}), bf16[16,2,2048]{2,1,0:T(2,128)(2,1)S(1)}, u32[]{:S(2)}, u32[]{:S(2)}) async-start(bf16[16,2,2048]{2,1,0:T(2,128)(2,1)} %reshape.146), calls=%async_computation | async-start | bytes 262144 | tf_op jit(solution)/shard_map/while/body/eval_jaxpr/all_to_all | solution.py:137
  345.5 11.4 %all-to-all-start.1 = ((bf16[16,2,2048]{2,1,0:T(2,128)(2,1)}), bf16[16,2,2048]{2,1,0:T(2,128)(2,1)S(1)}, u32[]{:S(2)}, u32[]{:S(2)}) async-start(bf16[16,2,2048]{2,1,0:T(2,128)(2,1)} %reshape.148), calls=%async_computation.1 | async-start | bytes 262144 | tf_op jit(solution)/shard_map/while/body/eval_jaxpr/all_to_all | solution.py:138
  356.9 11.4 %all-to-all-start.2 = ((bf16[16,2,2048]{2,1,0:T(2,128)(2,1)}), bf16[16,2,2048]{2,1,0:T(2,128)(2,1)S(1)}, u32[]{:S(2)}, u32[]{:S(2)}) async-start(bf16[16,2,2048]{2,1,0:T(2,128)(2,1)} %reshape.150), calls=%async_computation.2 | async-start | bytes 262144 | tf_op jit(solution)/shard_map/while/body/eval_jaxpr/all_to_all | solution.py:139
  377.6 11.4 %all-to-all-start.3 = ((bf16[16,2,2048]{2,1,0:T(2,128)(2,1)}), bf16[16,2,2048]{2,1,0:T(2,128)(2,1)S(1)}, u32[]{:S(2)}, u32[]{:S(2)}) async-start(bf16[16,2,2048]{2,1,0:T(2,128)(2,1)} %reshape.152), calls=%async_computation.3 | async-start | bytes 262144 | tf_op jit(solution)/shard_map/while/body/eval_jaxpr/all_to_all | solution.py:146
  393.5 13.3 %collective-permute-start = (bf16[64,1024]{1,0:T(8,128)(2,1)}, bf16[64,1024]{1,0:T(8,128)(2,1)S(1)}, u32[]{:S(2)}, u32[]{:S(2)}) collective-permute-start(bf16[64,1024]{1,0:T(8,128)(2,1)} %get-tuple-element.591), channel_id=1, source_target_pairs={{0,16},{1,17},{2,18},{3,19},{4,20},{5,21},{6,22},{7,23},{8,24},{9,... | collective-permute-start | bytes 393224 | tf_op jit(solution)/shard_map/while/body/eval_jaxpr/ppermute | solution.py:22
  418.3 11.4 %all-to-all-start = ((bf16[16,2,2048]{2,1,0:T(2,128)(2,1)}), bf16[16,2,2048]{2,1,0:T(2,128)(2,1)S(1)}, u32[]{:S(2)}, u32[]{:S(2)}) async-start(bf16[16,2,2048]{2,1,0:T(2,128)(2,1)} %reshape.146), calls=%async_computation | async-start | bytes 262144 | tf_op jit(solution)/shard_map/while/body/eval_jaxpr/all_to_all | solution.py:137
  429.7 11.4 %all-to-all-start.1 = ((bf16[16,2,2048]{2,1,0:T(2,128)(2,1)}), bf16[16,2,2048]{2,1,0:T(2,128)(2,1)S(1)}, u32[]{:S(2)}, u32[]{:S(2)}) async-start(bf16[16,2,2048]{2,1,0:T(2,128)(2,1)} %reshape.148), calls=%async_computation.1 | async-start | bytes 262144 | tf_op jit(solution)/shard_map/while/body/eval_jaxpr/all_to_all | solution.py:138
  441.1 11.4 %all-to-all-start.2 = ((bf16[16,2,2048]{2,1,0:T(2,128)(2,1)}), bf16[16,2,2048]{2,1,0:T(2,128)(2,1)S(1)}, u32[]{:S(2)}, u32[]{:S(2)}) async-start(bf16[16,2,2048]{2,1,0:T(2,128)(2,1)} %reshape.150), calls=%async_computation.2 | async-start | bytes 262144 | tf_op jit(solution)/shard_map/while/body/eval_jaxpr/all_to_all | solution.py:139
  461.7 11.4 %all-to-all-start.3 = ((bf16[16,2,2048]{2,1,0:T(2,128)(2,1)}), bf16[16,2,2048]{2,1,0:T(2,128)(2,1)S(1)}, u32[]{:S(2)}, u32[]{:S(2)}) async-start(bf16[16,2,2048]{2,1,0:T(2,128)(2,1)} %reshape.152), calls=%async_computation.3 | async-start | bytes 262144 | tf_op jit(solution)/shard_map/while/body/eval_jaxpr/all_to_all | solution.py:146
  477.7 13.3 %collective-permute-start = (bf16[64,1024]{1,0:T(8,128)(2,1)}, bf16[64,1024]{1,0:T(8,128)(2,1)S(1)}, u32[]{:S(2)}, u32[]{:S(2)}) collective-permute-start(bf16[64,1024]{1,0:T(8,128)(2,1)} %get-tuple-element.591), channel_id=1, source_target_pairs={{0,16},{1,17},{2,18},{3,19},{4,20},{5,21},{6,22},{7,23},{8,24},{9,... | collective-permute-start | bytes 393224 | tf_op jit(solution)/shard_map/while/body/eval_jaxpr/ppermute | solution.py:22
  494.6 11.4 %all-to-all-start = ((bf16[16,2,2048]{2,1,0:T(2,128)(2,1)}), bf16[16,2,2048]{2,1,0:T(2,128)(2,1)S(1)}, u32[]{:S(2)}, u32[]{:S(2)}) async-start(bf16[16,2,2048]{2,1,0:T(2,128)(2,1)} %reshape.146), calls=%async_computation | async-start | bytes 262144 | tf_op jit(solution)/shard_map/while/body/eval_jaxpr/all_to_all | solution.py:137
  506.0 11.4 %all-to-all-start.1 = ((bf16[16,2,2048]{2,1,0:T(2,128)(2,1)}), bf16[16,2,2048]{2,1,0:T(2,128)(2,1)S(1)}, u32[]{:S(2)}, u32[]{:S(2)}) async-start(bf16[16,2,2048]{2,1,0:T(2,128)(2,1)} %reshape.148), calls=%async_computation.1 | async-start | bytes 262144 | tf_op jit(solution)/shard_map/while/body/eval_jaxpr/all_to_all | solution.py:138
  517.4 11.4 %all-to-all-start.2 = ((bf16[16,2,2048]{2,1,0:T(2,128)(2,1)}), bf16[16,2,2048]{2,1,0:T(2,128)(2,1)S(1)}, u32[]{:S(2)}, u32[]{:S(2)}) async-start(bf16[16,2,2048]{2,1,0:T(2,128)(2,1)} %reshape.150), calls=%async_computation.2 | async-start | bytes 262144 | tf_op jit(solution)/shard_map/while/body/eval_jaxpr/all_to_all | solution.py:139
  530.9 11.4 %all-to-all-start.3 = ((bf16[16,2,2048]{2,1,0:T(2,128)(2,1)}), bf16[16,2,2048]{2,1,0:T(2,128)(2,1)S(1)}, u32[]{:S(2)}, u32[]{:S(2)}) async-start(bf16[16,2,2048]{2,1,0:T(2,128)(2,1)} %reshape.152), calls=%async_computation.3 | async-start | bytes 262144 | tf_op jit(solution)/shard_map/while/body/eval_jaxpr/all_to_all | solution.py:146
  544.1 29.9 %collective-permute-start = (bf16[64,1024]{1,0:T(8,128)(2,1)}, bf16[64,1024]{1,0:T(8,128)(2,1)S(1)}, u32[]{:S(2)}, u32[]{:S(2)}) collective-permute-start(bf16[64,1024]{1,0:T(8,128)(2,1)} %get-tuple-element.591), channel_id=1, source_target_pairs={{0,16},{1,17},{2,18},{3,19},{4,20},{5,21},{6,22},{7,23},{8,24},{9,... | collective-permute-start | bytes 393224 | tf_op jit(solution)/shard_map/while/body/eval_jaxpr/ppermute | solution.py:22
  568.7 5.2 collective-permute-start.1
  (12 other events, 37.7 us)
Sparse Core Ops, SparseCore 0:
  9.5 44.1 all-gather.3
  55.9 40.1 all-gather.7
  98.4 60.1 all-gather.5
  574.1 14.1 reduce-scatter.1
where the time goes:
time: 597 us; the launch traced here: 595 us
  waiting for transfers between devices  320 us (54%)
  starting transfers between devices  117 us (20%)
  other arithmetic  50.4 us (8%)
  local copies, waits for them, and re-layouts  50.1 us (8%)
  matrix products  42 us (7%)
  between operations  13.2 us (2%)
    all_gather x1, waiting for transfers between devices, body(): lax.all_gather(qkv_weight, 'seq', axis=1, tiled=True)  62.4 us
    ppermute x5, starting transfers between devices, shifted(): lax.ppermute(value, axis, [(source, source + steps) for source in range(i...  46.5 us
    all_gather x1, waiting for transfers between devices, body(): lax.all_gather(merge_weight, 'seq', axis=1, tiled=True)  44.9 us
    all_gather x1, waiting for transfers between devices, body(): lax.all_gather(proj_weight, 'seq', axis=1, tiled=True)  42.4 us
    all_to_all x5, waiting for transfers between devices, tick(): lax.all_to_all(attended, 'seq', split_axis=0, concat_axis=0, tiled=True)  39.2 us
    all_to_all x5, waiting for transfers between devices, tick(): lax.all_to_all(values_in, 'seq', split_axis=0, concat_axis=0, tiled=True)  38.1 us
    all_to_all x5, waiting for transfers between devices, tick(): lax.all_to_all(queries, 'seq', split_axis=0, concat_axis=0, tiled=True)  29.7 us
    all_to_all x5, waiting for transfers between devices, tick(): lax.all_to_all(keys_in, 'seq', split_axis=0, concat_axis=0, tiled=True)  29.6 us
  transfers between devices with their start and end apart: 34, of which 29 were waited for; matrix products, arithmetic and copies ran while one was open for 6% of the time, Pallas kernels for 0%

commit v1 on v0

--- a/solution.py
+++ b/solution.py
@@ -1,6 +1,8 @@
 import jax
 import jax.numpy as jnp
 from jax import lax
+from jax.experimental import pallas as pl
+from jax.experimental.pallas import tpu as pltpu
 from jax.sharding import PartitionSpec as P
 
 HEADS = 16
@@ -180,6 +182,443 @@
     return lax.psum_scatter(result.astype(jnp.bfloat16), "section", scatter_dimension=2, tiled=True)
 
 
+class Plan:
+    def __init__(self, sections, seq_count, windows, tok_rows, features):
+        self.sections = sections
+        self.seq_count = seq_count
+        self.windows = windows
+        self.tok_rows = tok_rows
+        self.features = features
+        self.inner = seq_count // windows
+        self.slots = sections * self.inner
+        self.half = tok_rows // sections
+        self.shard = windows * self.half
+        self.tokens = self.slots * self.shard
+        self.cols = features // self.slots
+        self.half_cols = features // sections
+        self.w_rows = features // seq_count
+        self.group = self.inner * self.w_rows
+        self.chips = [(mx, mi) for mx in range(sections) for mi in range(0, self.inner, 2)]
+
+    @staticmethod
+    def fits(sections, seq_count, windows, tok_rows, features):
+        if sections != 2 or windows & (windows - 1) or seq_count % (2 * windows):
+            return False
+        inner = seq_count // windows
+        if inner & (inner - 1) or features % (sections * inner * 2 * HEAD_DIM):
+            return False
+        return features == HEADS * HEAD_DIM and tok_rows % 32 == 0
+
+    def mask(self, mx=0, mz=0, mi=0):
+        return mx * self.seq_count + mz * self.inner + mi
+
+
+def attention(qkv, out, cols, rows_q):
+    tokens = qkv.shape[0]
+    lane_head = lax.broadcasted_iota(jnp.int32, (1, cols), 1) // HEAD_DIM
+
+    def one_block(block_no, carry):
+        rows = pl.ds(pl.multiple_of(block_no * rows_q, rows_q), rows_q)
+        query = qkv[rows, 0:cols]
+        keys_in = qkv[:, cols : 2 * cols]
+        values_in = qkv[:, 2 * cols : 3 * cols]
+        mixed = jnp.zeros((rows_q, cols), jnp.float32)
+        for head in range(cols // HEAD_DIM):
+            mine = lane_head == head
+            picked = jnp.where(mine, query, jnp.zeros_like(query))
+            scores = lax.dot_general(
+                picked, keys_in, (((1,), (1,)), ((), ())), preferred_element_type=jnp.float32
+            )
+            row_max = jnp.max(scores, axis=-1, keepdims=True)
+            weights = jnp.exp(scores - row_max)
+            totals = jnp.sum(weights, axis=-1, keepdims=True)
+            part = jnp.dot(
+                weights.astype(jnp.bfloat16), values_in, preferred_element_type=jnp.float32
+            )
+            mixed = jnp.where(mine, part / totals, mixed)
+        out[rows, :] = mixed.astype(jnp.bfloat16)
+        return carry
+
+    lax.fori_loop(0, tokens // rows_q, one_block, 0)
+
+
+def project_rows(normed, w_qkv, cols):
+    packed = jnp.dot(normed, w_qkv, preferred_element_type=jnp.float32)
+    lane = lax.broadcasted_iota(jnp.int32, (1, packed.shape[1]), 1)
+    packed = packed.astype(jnp.bfloat16)
+    return jnp.where(lane < cols, packed * jnp.bfloat16(HEAD_DIM ** (-0.5)), packed)
+
+
+def slot_of(plan, where, mx, mi):
+    return (where[0] ^ mx) * plan.inner + (where[2] ^ mi)
+
+
+def aligned(index, size):
+    return pl.ds(pl.multiple_of(index * size, size), size)
+
+
+def start_all(copies):
+    for copy in copies:
+        copy.start()
+    for copy in copies:
+        copy.wait()
+
+
+def prepare_kernel(plan, where, latents, qkv_weight, proj_weight, merge_weight, *rest):
+    shares = rest[: plan.windows]
+    keep, give, cross, sems = rest[plan.windows :]
+    copies = []
+
+    def add(source, target):
+        copies.append(pltpu.make_async_copy(source, target, sems.at[len(copies)]))
+
+    for core, target in ((1, give), (0, keep)):
+        for chip_no, (mx, mi) in enumerate(plan.chips):
+            slot = slot_of(plan, where, mx, mi ^ core)
+            for part in range(3):
+                add(
+                    qkv_weight.at[0, :, aligned(part * plan.slots + slot, plan.cols)],
+                    target.at[chip_no, :, part * plan.cols : (part + 1) * plan.cols],
+                )
+    width = plan.half_cols
+    for part, matrix in enumerate((proj_weight, merge_weight)):
+        add(
+            matrix.at[0, :, aligned(where[0] ^ 1, width)],
+            cross.at[:, part * width : (part + 1) * width],
+        )
+    for mz in range(plan.windows):
+        add(latents.at[where[1] ^ mz, aligned(where[0], plan.half), :], shares[mz])
+    start_all(copies)
+
+
+def pair_kernel(plan, keep, given, *outs):
+    rows = plan.w_rows
+    for chip_no, out in enumerate(outs):
+        out[0:rows, :] = keep[chip_no]
+        out[rows:, :] = given[chip_no]
+
+
+def sort_kernel(plan, where, *refs):
+    count = len(plan.chips)
+    pieces, outs = (refs[:count], refs[count:])
+    rows = 2 * plan.w_rows
+    for section in range(plan.sections):
+
+        @pl.when(where[0] == section)
+        def _():
+            for piece, (mx, mi) in zip(pieces, plan.chips):
+                start = mi * plan.w_rows
+                outs[section ^ mx][start : start + rows, :] = piece[...]
+
+
+def merge_kernel(plan, where, proj_weight, merge_weight, crossed, mats, last):
+    width = plan.half_cols
+    for section in range(plan.sections):
+
+        @pl.when(where[0] == section)
+        def _():
+            lanes = slice(section * width, (section + 1) * width)
+            mine = proj_weight[0, :, lanes]
+            others = crossed[:, 0:width]
+            mats[:, 0:width] = mine if section == 0 else others
+            last[...] = others if section == 0 else mine
+            total = merge_weight[0, :, lanes].astype(jnp.float32)
+            total = total + crossed[:, width:].astype(jnp.float32)
+            mats[:, width:] = total.astype(jnp.bfloat16)
+
+
+def stack_kernel(*refs):
+    start = 0
+    for piece in refs[:-1]:
+        rows = piece.shape[0]
+        refs[-1][start : start + rows, :] = piece[...]
+        start += rows
+
+
+def gather_weights(plan, where, pieces, target):
+    rows = plan.w_rows
+    for mz, piece in enumerate(pieces):
+        for mi in range(plan.inner):
+            shard = (where[1] ^ mz) * plan.inner + (where[2] ^ mi)
+            target[aligned(shard, rows), :] = piece[mi * rows : (mi + 1) * rows, :]
+
+
+def plane_order(plan):
+    return [(mx, mi ^ core) for core in range(2) for mx, mi in plan.chips]
+
+
+def first_kernel(plan, where, gain, *rest):
+    hidden_in = rest[: plan.slots]
+    pieces = rest[plan.slots : plan.slots + plan.windows]
+    out, w_qkv, qkv = rest[plan.slots + plan.windows :]
+    gather_weights(plan, where, pieces, w_qkv)
+    for piece, (mx, mi) in zip(hidden_in, plane_order(plan)):
+        normed = layer_norm(piece[...], gain[...])
+        rows = aligned(slot_of(plan, where, mx, mi), plan.shard)
+        qkv[rows, :] = project_rows(normed, w_qkv[...], plan.cols)
+    attention(qkv, out, plan.cols, min(256, plan.tokens))
+
+
+def second_kernel(plan, where, gain, *rest):
+    slots, windows = (plan.slots, plan.windows)
+    hidden_in, rest = (rest[:slots], rest[slots:])
+    attended_in, rest = (rest[:slots], rest[slots:])
+    mats_in, rest = (rest[:slots], rest[slots:])
+    pieces, rest = (rest[:windows], rest[windows:])
+    outs, rest = (rest[: plan.inner // 2], rest[plan.inner // 2 :])
+    kept, att, mats, w_qkv, joined, qkv, mixed = rest
+    order = plane_order(plan)
+    for piece, (mx, mi) in zip(attended_in, order):
+        att[:, aligned(slot_of(plan, where, mx, mi), plan.cols)] = piece[...]
+    rows = plan.w_rows
+    for piece, (mx, mi) in zip(mats_in, order):
+        for mz in range(windows):
+            shard = (where[1] ^ mz) * plan.inner + (where[2] ^ mi)
+            mats[where[0] ^ mx, aligned(shard, rows), :] = piece[mz * rows : (mz + 1) * rows, :]
+    gather_weights(plan, where, pieces, w_qkv)
+    width = plan.half_cols
+    for piece, (mx, mi) in zip(hidden_in, order):
+        part = aligned(slot_of(plan, where, mx, mi), plan.shard)
+        attended = att[part, :]
+        hidden = jnp.concatenate(
+            [
+                jnp.dot(attended, mats[side, :, 0:width], preferred_element_type=jnp.float32)
+                for side in range(plan.sections)
+            ],
+            axis=1,
+        )
+        hidden = (piece[...].astype(jnp.float32) + hidden).astype(jnp.bfloat16)
+        merged = jnp.concatenate(
+            [
+                jnp.dot(hidden, mats[side, :, width:], preferred_element_type=jnp.float32)
+                for side in range(plan.sections)
+            ],
+            axis=1,
+        ).astype(jnp.bfloat16)
+        joined[part, :] = merged
+        normed = layer_norm(merged, gain[...])
+        qkv[part, :] = project_rows(normed, w_qkv[...], plan.cols)
+    attention(qkv, mixed, plan.cols, min(256, plan.tokens))
+    lanes = aligned(where[0], width)
+    for side in range(plan.sections):
+        for mi in range(plan.inner):
+            part = aligned(side * plan.inner + (where[2] ^ mi), plan.shard)
+            start = ((mi % 2) * plan.sections + side) * plan.shard
+            outs[mi // 2][start : start + plan.shard, :] = mixed[part, :]
+            if mi == 0:
+                kept[side * plan.shard : (side + 1) * plan.shard, :] = joined[part, lanes]
+
+
+def third_kernel(plan, where, kept, *rest):
+    chips, rest = (rest[: len(plan.chips)], rest[len(plan.chips) :])
+    swapped, mats_in = (rest[0], rest[1 : 1 + plan.inner])
+    outs, (att, mat) = (rest[1 + plan.inner : -2], rest[-2:])
+    rows = plan.sections * plan.shard
+    for chip_no, (mx, mi) in enumerate(plan.chips):
+        for core in range(2):
+            lanes = aligned(slot_of(plan, where, mx, mi ^ core), plan.cols)
+            if core == 0:
+                att[:, lanes] = chips[chip_no][0:rows, :]
+            else:
+                att[:, lanes] = swapped[chip_no * rows : (chip_no + 1) * rows, :]
+    rows = plan.w_rows
+    order = [mi ^ core for core in range(2) for mi in range(0, plan.inner, 2)]
+    for piece, mi in zip(mats_in, order):
+        for mz in range(plan.windows):
+            shard = (where[1] ^ mz) * plan.inner + (where[2] ^ mi)
+            mat[aligned(shard, rows), :] = piece[mz * rows : (mz + 1) * rows, :]
+    result = jnp.dot(att[...], mat[...], preferred_element_type=jnp.float32)
+    result = (kept[...].astype(jnp.float32) + result).astype(jnp.bfloat16)
+    for side in range(plan.sections):
+        for mz in range(plan.windows):
+            start = side * plan.shard + mz * plan.half
+            outs[mz][side * plan.half : (side + 1) * plan.half, :] = result[
+                start : start + plan.half, :
+            ]
+
+
+def place_kernel(plan, where, *refs):
+    for mz in range(plan.windows):
+        refs[-1][where[1] ^ mz] = refs[mz][...]
+
+
+def halves_kernel(plan, *refs):
+    rows = plan.sections * plan.shard
+    for chip_no, piece in enumerate(refs[:-1]):
+        refs[-1][chip_no * rows : (chip_no + 1) * rows, :] = piece[rows:, :]
+
+
+def plane_body(latents, norm_gain, qkv_weight, proj_weight, merge_weight):
+    plan = Plan(
+        lax.axis_size("section"), lax.axis_size("seq"), latents.shape[0], *latents.shape[1:]
+    )
+    windows, inner, shard, cols = (plan.windows, plan.inner, plan.shard, plan.cols)
+    section = lax.axis_index("section")
+    position = lax.axis_index("seq")
+    window, place = (position // inner, position % inner)
+    lane = lax.iota(jnp.int32, 3)
+    where = jnp.where(lane == 0, section, jnp.where(lane == 1, window, place)).astype(jnp.int32)
+    devices = plan.sections * plan.seq_count
+    bf16 = jnp.bfloat16
+    smem = pl.BlockSpec(memory_space=pltpu.SMEM)
+    anywhere = pl.BlockSpec(memory_space=pl.ANY)
+    vmem = pl.BlockSpec(memory_space=pltpu.VMEM)
+    tokens, features, width = (plan.tokens, plan.features, plan.half_cols)
+
+    def swap(value, mask):
+        pairs = [(source, source ^ mask) for source in range(devices)]
+        return lax.ppermute(value, ("section", "seq"), pairs)
+
+    def call(kernel, outs, ins, scratch=(), specs=None, flops=0, limit=40):
+        shapes = tuple(jax.ShapeDtypeStruct(shape, bf16) for shape in outs)
+        moved = sum(2 * value.size for value in ins)
+        return pl.pallas_call(
+            kernel,
+            out_shape=shapes,
+            in_specs=specs or [vmem] * len(ins),
+            out_specs=tuple(vmem for _ in shapes),
+            scratch_shapes=list(scratch),
+            cost_estimate=pl.CostEstimate(
+                flops=flops, bytes_accessed=moved, transcendentals=0
+            ),
+            compiler_params=pltpu.CompilerParams(vmem_limit_bytes=limit << 20),
+        )(*ins)
+
+    def stack(pieces):
+        rows = sum(piece.shape[0] for piece in pieces)
+        return call(stack_kernel, [(rows, pieces[0].shape[1])], pieces, limit=8)[0]
+
+    def z_gather(value):
+        far = swap(value, plan.mask(mz=2))
+        near = swap(value, plan.mask(mz=1))
+        return [value, near, far, swap(far, plan.mask(mz=1))]
+
+    def chip_gather(value):
+        return [value] + [
+            swap(value, plan.mask(mx=mx, mi=mi))
+            for chip_no, (mx, mi) in enumerate(plan.chips)
+            if chip_no
+        ]
+
+    def core_gather(pieces):
+        return pieces + [swap(piece, plan.mask(mi=1)) for piece in pieces]
+
+    n_parts = 6 * len(plan.chips)
+    prepared = call(
+        lambda *refs: prepare_kernel(plan, *refs),
+        [(plan.half, features)] * windows
+        + [(len(plan.chips), plan.w_rows, 3 * cols)] * 2
+        + [(plan.w_rows, 2 * width)],
+        [where, latents, qkv_weight, proj_weight, merge_weight],
+        [pltpu.SemaphoreType.DMA((n_parts + 2 + windows,))],
+        [smem] + [anywhere] * 4,
+        limit=8,
+    )
+    shares, (keep, give, cross) = (prepared[:windows], prepared[windows:])
+    given = swap(give, plan.mask(mi=1))
+    crossed = swap(cross, plan.mask(mx=1))
+    other_gain = swap(norm_gain, plan.mask(mx=1))
+    gain_a = jnp.where(section == 0, norm_gain, other_gain)
+    gain_b = jnp.where(section == 0, other_gain, norm_gain)
+    shares = [shares[0]] + [swap(shares[mz], plan.mask(mz=mz)) for mz in range(1, windows)]
+    outgoing = call(
+        lambda *refs: pair_kernel(plan, *refs),
+        [(2 * plan.w_rows, 3 * cols)] * len(plan.chips),
+        [keep, given],
+        limit=8,
+    )
+    incoming = [outgoing[0]] + [
+        swap(outgoing[chip_no], plan.mask(mx=mx, mi=mi))
+        for chip_no, (mx, mi) in enumerate(plan.chips)
+        if chip_no
+    ]
+    mats, last = call(
+        lambda *refs: merge_kernel(plan, *refs),
+        [(plan.w_rows, 2 * width), (plan.w_rows, width)],
+        [where, proj_weight, merge_weight, crossed],
+        (),
+        [smem] + [vmem] * 3,
+        limit=8,
+    )
+    mats = z_gather(mats)
+    hidden = chip_gather(stack(shares))
+    hidden = core_gather(hidden)
+    rows_a, rows_b = call(
+        lambda *refs: sort_kernel(plan, *refs),
+        [(plan.group, 3 * cols)] * 2,
+        [where] + incoming,
+        (),
+        [smem] + [vmem] * len(incoming),
+        limit=8,
+    )
+    pieces_a = z_gather(rows_a)
+    mats = chip_gather(stack(mats))
+    pieces_b = [rows_b] + [swap(rows_b, plan.mask(mz=mz)) for mz in range(1, windows)]
+    last = [last] + [swap(last, plan.mask(mz=mz)) for mz in range(1, windows)]
+
+    (attended,) = call(
+        lambda *refs: first_kernel(plan, *refs),
+        [(tokens, cols)],
+        [where, gain_a] + hidden + pieces_a,
+        [pltpu.VMEM((features, 3 * cols), bf16), pltpu.VMEM((tokens, 3 * cols), bf16)],
+        [smem] + [vmem] * (1 + len(hidden) + windows),
+        flops=10_000_000_000,
+    )
+    attended = core_gather(chip_gather(attended))
+    mats = core_gather(mats)
+    last = stack(last)
+    last = [last] + [swap(last, plan.mask(mi=mi)) for mi in range(2, inner, 2)]
+    last = core_gather(last)
+    *attended, kept = call(
+        lambda *refs: second_kernel(plan, *refs),
+        [(2 * plan.sections * shard, cols)] * (inner // 2) + [(plan.sections * shard, width)],
+        [where, gain_b] + hidden + attended + mats + pieces_b,
+        [
+            pltpu.VMEM((tokens, features), bf16),
+            pltpu.VMEM((plan.sections, features, 2 * width), bf16),
+            pltpu.VMEM((features, 3 * cols), bf16),
+            pltpu.VMEM((tokens, features), bf16),
+            pltpu.VMEM((tokens, 3 * cols), bf16),
+            pltpu.VMEM((tokens, cols), bf16),
+        ],
+        [smem] + [vmem] * (1 + 3 * plan.slots + windows),
+        flops=18_000_000_000,
+    )
+    back = [attended[0]] + [
+        swap(attended[mi // 2], plan.mask(mx=mx, mi=mi))
+        for chip_no, (mx, mi) in enumerate(plan.chips)
+        if chip_no
+    ]
+    (halves,) = call(
+        lambda *refs: halves_kernel(plan, *refs),
+        [(len(plan.chips) * plan.sections * shard, cols)],
+        back,
+        limit=8,
+    )
+    swapped = swap(halves, plan.mask(mi=1))
+    outcome = call(
+        lambda *refs: third_kernel(plan, *refs),
+        [(plan.tok_rows, width)] * windows,
+        [where, kept] + back + [swapped] + last,
+        [
+            pltpu.VMEM((plan.sections * shard, features), bf16),
+            pltpu.VMEM((features, width), bf16),
+        ],
+        [smem] + [vmem] * (2 + len(back) + inner),
+        flops=1_000_000_000,
+        limit=16,
+    )
+    outcome = [outcome[0]] + [swap(outcome[mz], plan.mask(mz=mz)) for mz in range(1, windows)]
+    return call(
+        lambda *refs: place_kernel(plan, *refs),
+        [(windows, plan.tok_rows, width)],
+        [where] + outcome,
+        (),
+        [smem] + [vmem] * windows,
+        limit=8,
+    )[0]
+
+
 def solution(mesh):
     placed = (
         P(None, "seq", None),
@@ -188,6 +627,25 @@
         P("section", "seq", None),
         P("section", "seq", None),
     )
-    return jax.shard_map(
-        body, mesh=mesh, in_specs=placed, out_specs=P(None, "seq", "section"), check_vma=False
-    )
+
+    def plane_step(*arguments):
+        return plane_body(*arguments)
+
+    def step(latents, *weights):
+        fits = Plan.fits(
+            mesh.shape["section"],
+            mesh.shape["seq"],
+            latents.shape[0],
+            latents.shape[1] // mesh.shape["seq"],
+            latents.shape[2],
+        )
+        mapped = jax.shard_map(
+            plane_step if fits else body,
+            mesh=mesh,
+            in_specs=placed,
+            out_specs=P(None, "seq", "section"),
+            check_vma=False,
+        )
+        return mapped(latents, *weights)
+
+    return step

time: 597 us -> 158 us (0.26)
  waiting for transfers between devices: 320 us -> 72 us
  starting transfers between devices: 117 us -> 54.1 us
  other arithmetic: 50.4 us -> 0.01 us
  local copies, waits for them, and re-layouts: 50.1 us -> 3.85 us
  matrix products: 42 us -> 0 us
  Pallas kernels: 0 us -> 27.3 us
  between operations: 13.2 us -> 0.23 us
    all_gather x3 -> x0, waiting for transfers between devices: 150 us -> none  [the longest x1 62.4 us: body(): lax.all_gather(qkv_weight, 'seq', axis=1, tiled=True)]
    all_to_all x20 -> x0, waiting for transfers between devices: 137 us -> none  [the longest x5 39.2 us: tick(): lax.all_to_all(attended, 'seq', split_axis=0, concat_axis=0, tiled=True)]
    all_to_all x20 -> x0, starting transfers between devices: 70.2 us -> none  [the longest x5 17.6 us: tick(): lax.all_to_all(keys_in, 'seq', split_axis=0, concat_axis=0, tiled=True)]
    ppermute x10 -> x52, waiting for transfers between devices: 16.9 us -> 72 us  [swap(): return lax.ppermute(value, ('section', 'seq'), pairs)]
    dot_general x28 -> x0, matrix products: 42 us -> none  [the longest x4 16.6 us: project(): jnp.dot(normed, w_qkv, preferred_element_type=jnp.float32)]
    pallas_call x0 -> x12, Pallas kernels: none -> 27.3 us  [call(): pl.pallas_call(kernel, out_shape=shapes, in_specs=specs or [vmem] * len(i...]
    while x76 -> x0, local copies, waits for them, and re-layouts: 20.1 us -> none
    select_n x15 -> x2, other arithmetic: 16.1 us -> 0.01 us  [the longest x1 0.01 us: plane_body(): gain_a = jnp.where(section == 0, norm_gain, other_gain)]
  transfers between devices with their start and end apart: 34 -> 52, of which waited for: 29 -> 17; matrix products, arithmetic and copies ran while one was open for 6% -> 0% of each run, Pallas kernels for 0% -> 15%
where the time goes in v1:
time: 158 us
  waiting for transfers between devices  72 us (46%)
  starting transfers between devices  54.1 us (34%)
  Pallas kernels  27.3 us (17%)
  local copies, waits for them, and re-layouts  3.85 us (2%)
    ppermute x52, waiting for transfers between devices, swap(): return lax.ppermute(value, ('section', 'seq'), pairs)  72 us
    ppermute x52, starting transfers between devices, swap(): return lax.ppermute(value, ('section', 'seq'), pairs)  54.1 us
    pallas_call x12, Pallas kernels, call(): pl.pallas_call(kernel, out_shape=shapes, in_specs=specs or [vmem] * len(i...  27.3 us
    unnamed x10, local copies, waits for them, and re-layouts  3.85 us
  transfers between devices with their start and end apart: 52, of which 17 were waited for; matrix products, arithmetic and copies ran while one was open for 0% of the time, Pallas kernels for 15%

profile of v1, /device:TPU:0, one launch (start us, length us, event | category | flops | bytes accessed | tf_op | source)
XLA Modules:
  0.0 157.6 jit_solution(14737199988942819899)
XLA Ops:
  5.9 2.6 %collective-permute-start.25 = (bf16[64,1024]{1,0:T(8,128)(2,1)S(1)}, bf16[64,1024]{1,0:T(8,128)(2,1)S(1)}, u32[]{:S(2)}, u32[]{:S(2)}) collective-permute-start(bf16[64,1024]{1,0:T(8,128)(2,1)S(1)} %get-tuple-element.38), channel_id=1, source_target_pairs={{0,16},{1,17},{2,18},{3,19},{4,20},{5,21},{6,22},{7,23},{8,24},{9,... | collective-permute-start | bytes 393224 | tf_op jit(solution)/shard_map/ppermute | solution.py:470
  8.5 1.6 %collective-permute-start.1 = (bf16[32,1024]{1,0:T(8,128)(2,1)S(1)}, bf16[32,1024]{1,0:T(8,128)(2,1)S(1)}, u32[]{:S(2)}, u32[]{:S(2)}) collective-permute-start(bf16[32,1024]{1,0:T(8,128)(2,1)S(1)} %get-tuple-element.28), channel_id=1, source_target_pairs={{0,4},{1,5},{2,6},{3,7},{4,0},{5,1},{6,2},{7,3},{8,12},{9,13},{10,... | collective-permute-start | bytes 196616 | tf_op jit(solution)/shard_map/ppermute | solution.py:470
  10.0 2.6 %collective-permute-start.2 = (bf16[32,1024]{1,0:T(8,128)(2,1)S(1)}, bf16[32,1024]{1,0:T(8,128)(2,1)S(1)}, u32[]{:S(2)}, u32[]{:S(2)}) collective-permute-start(bf16[32,1024]{1,0:T(8,128)(2,1)S(1)} %get-tuple-element.29), channel_id=1, source_target_pairs={{0,8},{1,9},{2,10},{3,11},{4,12},{5,13},{6,14},{7,15},{8,0},{9,1},... | collective-permute-start | bytes 196616 | tf_op jit(solution)/shard_map/ppermute | solution.py:470
  13.2 3.3 %collective-permute-start.3 = (bf16[32,1024]{1,0:T(8,128)(2,1)S(1)}, bf16[32,1024]{1,0:T(8,128)(2,1)S(1)}, u32[]{:S(2)}, u32[]{:S(2)}) collective-permute-start(bf16[32,1024]{1,0:T(8,128)(2,1)S(1)} %get-tuple-element.30), channel_id=1, source_target_pairs={{0,12},{1,13},{2,14},{3,15},{4,8},{5,9},{6,10},{7,11},{8,4},{9,5},... | collective-permute-start | bytes 196616 | tf_op jit(solution)/shard_map/ppermute | solution.py:470
  18.2 1.9 %collective-permute-start.44 = (bf16[64,512]{1,0:T(8,128)(2,1)S(1)}, bf16[64,512]{1,0:T(8,128)(2,1)S(1)}, u32[]{:S(2)}, u32[]{:S(2)}) collective-permute-start(bf16[64,512]{1,0:T(8,128)(2,1)S(1)} %get-tuple-element.44.refs_0_), channel_id=1, source_target_pairs={{0,8},{1,9},{2,10},{3,11},{4,12},{5,13},{6,14},{7,15},{8,0},{9,1},... | collective-permute-start | bytes 196616 | tf_op jit(solution)/shard_map/ppermute | solution.py:470
  21.6 1.6 %collective-permute-start.12 = (bf16[128,384]{1,0:T(8,128)(2,1)S(1)}, bf16[128,384]{1,0:T(8,128)(2,1)S(1)}, u32[]{:S(2)}, u32[]{:S(2)}) collective-permute-start(bf16[128,384]{1,0:T(8,128)(2,1)S(1)} %get-tuple-element.34), channel_id=1, source_target_pairs={{0,2},{1,3},{2,0},{3,1},{4,6},{5,7},{6,4},{7,5},{8,10},{9,11},{10,... | collective-permute-start | bytes 294920 | tf_op jit(solution)/shard_map/ppermute | solution.py:470
  24.7 4.6 %collective-permute-done.44.refs_2_ = bf16[64,512]{1,0:T(8,128)(2,1)S(1)} collective-permute-done((bf16[64,512]{1,0:T(8,128)(2,1)S(1)}, bf16[64,512]{1,0:T(8,128)(2,1)S(1)}, u32[]{:S(2)}, u32[]{:S(2)}) %collective-permute-start.44) | collective-permute-done | bytes 65568 | tf_op jit(solution)/shard_map/ppermute | solution.py:470
  29.3 2.4 %collective-permute-start.6 = (bf16[128,1024]{1,0:T(8,128)(2,1)S(1)}, bf16[128,1024]{1,0:T(8,128)(2,1)S(1)}, u32[]{:S(2)}, u32[]{:S(2)}) collective-permute-start(bf16[128,1024]{1,0:T(8,128)(2,1)S(1)} %shard_map.56.refs_2_), channel_id=1, source_target_pairs={{0,18},{1,19},{2,16},{3,17},{4,22},{5,23},{6,20},{7,21},{8,26},{9,... | collective-permute-start | bytes 786440 | tf_op jit(solution)/shard_map/ppermute | solution.py:470
  32.8 2.4 %collective-permute-start.14 = (bf16[128,384]{1,0:T(8,128)(2,1)S(1)}, bf16[128,384]{1,0:T(8,128)(2,1)S(1)}, u32[]{:S(2)}, u32[]{:S(2)}) collective-permute-start(bf16[128,384]{1,0:T(8,128)(2,1)S(1)} %get-tuple-element.36), channel_id=1, source_target_pairs={{0,18},{1,19},{2,16},{3,17},{4,22},{5,23},{6,20},{7,21},{8,26},{9,... | collective-permute-start | bytes 294920 | tf_op jit(solution)/shard_map/ppermute | solution.py:470
  35.4 10.4 %collective-permute-done.14.refs_4_ = bf16[128,384]{1,0:T(8,128)(2,1)S(1)} collective-permute-done((bf16[128,384]{1,0:T(8,128)(2,1)S(1)}, bf16[128,384]{1,0:T(8,128)(2,1)S(1)}, u32[]{:S(2)}, u32[]{:S(2)}) %collective-permute-start.14) | collective-permute-done | bytes 98336 | tf_op jit(solution)/shard_map/ppermute | solution.py:470
  46.5 3.2 %collective-permute-start.15 = (bf16[256,384]{1,0:T(8,128)(2,1)S(1)}, bf16[256,384]{1,0:T(8,128)(2,1)}, u32[]{:S(2)}, u32[]{:S(2)}) collective-permute-start(bf16[256,384]{1,0:T(8,128)(2,1)S(1)} %get-tuple-element.37.refs_10_), channel_id=1, source_target_pairs={{0,4},{1,5},{2,6},{3,7},{4,0},{5,1},{6,2},{7,3},{8,12},{9,13},{10,... | collective-permute-start | bytes 589832 | tf_op jit(solution)/shard_map/ppermute | solution.py:470
  49.7 2.0 %collective-permute-start.28 = (bf16[64,1024]{1,0:T(8,128)(2,1)S(1)}, bf16[64,1024]{1,0:T(8,128)(2,1)S(1)}, u32[]{:S(2)}, u32[]{:S(2)}) collective-permute-start(bf16[64,1024]{1,0:T(8,128)(2,1)S(1)} %collective-permute-done.27.refs_2_), channel_id=1, source_target_pairs={{0,4},{1,5},{2,6},{3,7},{4,0},{5,1},{6,2},{7,3},{8,12},{9,13},{10,... | collective-permute-start | bytes 393224 | tf_op jit(solution)/shard_map/ppermute | solution.py:470
  51.7 14.5 %collective-permute-done.28.refs_3_ = bf16[64,1024]{1,0:T(8,128)(2,1)S(1)} collective-permute-done((bf16[64,1024]{1,0:T(8,128)(2,1)S(1)}, bf16[64,1024]{1,0:T(8,128)(2,1)S(1)}, u32[]{:S(2)}, u32[]{:S(2)}) %collective-permute-start.28) | collective-permute-done | bytes 131104 | tf_op jit(solution)/shard_map/ppermute | solution.py:470
  67.0 1.8 %collective-permute-start.17 = (bf16[256,384]{1,0:T(8,128)(2,1)}, bf16[256,384]{1,0:T(8,128)(2,1)S(1)}, u32[]{:S(2)}, u32[]{:S(2)}) collective-permute-start(bf16[256,384]{1,0:T(8,128)(2,1)} %collective-permute-done.16.refs_12_), channel_id=1, source_target_pairs={{0,4},{1,5},{2,6},{3,7},{4,0},{5,1},{6,2},{7,3},{8,12},{9,13},{10,... | collective-permute-start | bytes 589832 | tf_op jit(solution)/shard_map/ppermute | solution.py:470
  68.8 8.9 %collective-permute-done.37.refs_28_ = bf16[256,384]{1,0:T(8,128)(2,1)S(1)} collective-permute-done((bf16[256,384]{1,0:T(8,128)(2,1)S(1)}, bf16[256,384]{1,0:T(8,128)(2,1)S(1)}, u32[]{:S(2)}, u32[]{:S(2)}) %collective-permute-start.37) | collective-permute-done | bytes 196640 | tf_op jit(solution)/shard_map/ppermute | solution.py:470
  77.7 2.3 %collective-permute-start.38 = (bf16[256,384]{1,0:T(8,128)(2,1)S(1)}, bf16[256,384]{1,0:T(8,128)(2,1)S(1)}, u32[]{:S(2)}, u32[]{:S(2)}) collective-permute-start(bf16[256,384]{1,0:T(8,128)(2,1)S(1)} %get-tuple-element.40.refs_26_), channel_id=1, source_target_pairs={{0,12},{1,13},{2,14},{3,15},{4,8},{5,9},{6,10},{7,11},{8,4},{9,5},... | collective-permute-start | bytes 589832 | tf_op jit(solution)/shard_map/ppermute | solution.py:470
  80.0 1.5 collective-permute-start.29
  83.5 7.7 %shard_map.59.refs_10_ = bf16[1024,128]{1,0:T(8,128)(2,1)S(1)} custom-call(s32[3]{0:T(128)S(1)} %compare_select_fusion.1.refs_0_, f32[1,1024]{1,0:T(1,128)S(1)} %get-tuple-element.49.refs_1_, bf16[128,1024]{1,0:T(8,128)(2,1)S(1)} %shard_map.56.refs_2_, bf16[128,1024]{1,0:T(8,128)(2,1)S(1)} %collective-permute-done.4.refs_3_, ...), custom_call_target="tpu_custom_call" | custom-call | flops 10000000000 | bytes 2885638 | tf_op jit(solution)/shard_map/pallas_call | solution.py:475
  91.2 1.6 %collective-permute-start.18 = (bf16[1024,128]{1,0:T(8,128)(2,1)S(1)}, bf16[1024,128]{1,0:T(8,128)(2,1)S(1)}, u32[]{:S(2)}, u32[]{:S(2)}) collective-permute-start(bf16[1024,128]{1,0:T(8,128)(2,1)S(1)} %shard_map.59.refs_10_), channel_id=1, source_target_pairs={{0,2},{1,3},{2,0},{3,1},{4,6},{5,7},{6,4},{7,5},{8,10},{9,11},{10,... | collective-permute-start | bytes 786440 | tf_op jit(solution)/shard_map/ppermute | solution.py:470
  97.7 9.8 %collective-permute-done.31.refs_21_ = bf16[256,1024]{1,0:T(8,128)(2,1)S(1)} collective-permute-done((bf16[256,1024]{1,0:T(8,128)(2,1)S(1)}, bf16[256,1024]{1,0:T(8,128)(2,1)S(1)}, u32[]{:S(2)}, u32[]{:S(2)}) %collective-permute-start.31) | collective-permute-done | bytes 524320 | tf_op jit(solution)/shard_map/ppermute | solution.py:470
  108.0 3.1 %collective-permute-done.18.refs_11_ = bf16[1024,128]{1,0:T(8,128)(2,1)S(1)} collective-permute-done((bf16[1024,128]{1,0:T(8,128)(2,1)S(1)}, bf16[1024,128]{1,0:T(8,128)(2,1)S(1)}, u32[]{:S(2)}, u32[]{:S(2)}) %collective-permute-start.18) | collective-permute-done | bytes 262176 | tf_op jit(solution)/shard_map/ppermute | solution.py:470
  111.2 2.0 %collective-permute-done.19.refs_12_ = bf16[1024,128]{1,0:T(8,128)(2,1)S(1)} collective-permute-done((bf16[1024,128]{1,0:T(8,128)(2,1)S(1)}, bf16[1024,128]{1,0:T(8,128)(2,1)S(1)}, u32[]{:S(2)}, u32[]{:S(2)}) %collective-permute-start.19) | collective-permute-done | bytes 262176 | tf_op jit(solution)/shard_map/ppermute | solution.py:470
  113.2 4.0 %collective-permute-done.20.refs_13_ = bf16[1024,128]{1,0:T(8,128)(2,1)S(1)} collective-permute-done((bf16[1024,128]{1,0:T(8,128)(2,1)S(1)}, bf16[1024,128]{1,0:T(8,128)(2,1)S(1)}, u32[]{:S(2)}, u32[]{:S(2)}) %collective-permute-start.20) | collective-permute-done | bytes 262176 | tf_op jit(solution)/shard_map/ppermute | solution.py:470
  117.8 1.7 %collective-permute-done.23.refs_16_ = bf16[1024,128]{1,0:T(8,128)(2,1)S(1)} collective-permute-done((bf16[1024,128]{1,0:T(8,128)(2,1)S(1)}, bf16[1024,128]{1,0:T(8,128)(2,1)S(1)}, u32[]{:S(2)}, u32[]{:S(2)}) %collective-permute-start.23) | collective-permute-done | bytes 262176 | tf_op jit(solution)/shard_map/ppermute | solution.py:470
  119.5 1.5 collective-permute-start.46
  121.0 14.4 %shard_map.62 = (bf16[512,128]{1,0:T(8,128)(2,1)S(1)}, bf16[512,128]{1,0:T(8,128)(2,1)S(1)}, bf16[256,512]{1,0:T(8,128)(2,1)S(1)}) custom-call(s32[3]{0:T(128)S(1)} %compare_select_fusion.1.refs_0_, f32[1,1024]{1,0:T(1,128)S(1)} %get-tuple-element.50.refs_1_, bf16[128,1024]{1,0:T(8,128)(2,1)S(1)} %shard_map.56.refs_2_, ...), custom_call_target="tpu_custom_call" | custom-call | flops 17999998976 | bytes 9177094 | tf_op jit(solution)/shard_map/pallas_call | solution.py:475
  136.0 1.5 collective-permute-start.40
  141.9 2.9 %collective-permute-done.41.refs_3_.refs_5_ = bf16[512,128]{1,0:T(8,128)(2,1)S(1)} collective-permute-done((bf16[512,128]{1,0:T(8,128)(2,1)S(1)}, bf16[512,128]{1,0:T(8,128)(2,1)S(1)}, u32[]{:S(2)}, u32[]{:S(2)}) %collective-permute-start.41) | collective-permute-done | bytes 131104 | tf_op jit(solution)/shard_map/ppermute | solution.py:470
  144.9 1.5 collective-permute-done.42.refs_6_
  147.7 2.1 %collective-permute-start.50 = (bf16[64,512]{1,0:T(8,128)(2,1)S(1)}, bf16[64,512]{1,0:T(8,128)(2,1)S(1)}, u32[]{:S(2)}, u32[]{:S(2)}) collective-permute-start(bf16[64,512]{1,0:T(8,128)(2,1)S(1)} %get-tuple-element.47), channel_id=1, source_target_pairs={{0,8},{1,9},{2,10},{3,11},{4,12},{5,13},{6,14},{7,15},{8,0},{9,1},... | collective-permute-start | bytes 196616 | tf_op jit(solution)/shard_map/ppermute | solution.py:470
  149.8 2.3 %collective-permute-start.51 = (bf16[64,512]{1,0:T(8,128)(2,1)S(1)}, bf16[64,512]{1,0:T(8,128)(2,1)S(1)}, u32[]{:S(2)}, u32[]{:S(2)}) collective-permute-start(bf16[64,512]{1,0:T(8,128)(2,1)S(1)} %get-tuple-element.48), channel_id=1, source_target_pairs={{0,12},{1,13},{2,14},{3,15},{4,8},{5,9},{6,10},{7,11},{8,4},{9,5},... | collective-permute-start | bytes 196616 | tf_op jit(solution)/shard_map/ppermute | solution.py:470
  152.8 3.5 %collective-permute-done.50.refs_3_ = bf16[64,512]{1,0:T(8,128)(2,1)S(1)} collective-permute-done((bf16[64,512]{1,0:T(8,128)(2,1)S(1)}, bf16[64,512]{1,0:T(8,128)(2,1)S(1)}, u32[]{:S(2)}, u32[]{:S(2)}) %collective-permute-start.50) | collective-permute-done | bytes 65568 | tf_op jit(solution)/shard_map/ppermute | solution.py:470
  (96 shorter events, 30.4 us)
Async XLA Ops:
  5.3 14.8 %collective-permute-start.11 = (bf16[4,64,384]{2,1,0:T(8,128)(2,1)S(1)}, bf16[4,64,384]{2,1,0:T(8,128)(2,1)S(1)}, u32[]{:S(2)}, u32[]{:S(2)}) collective-permute-start(bf16[4,64,384]{2,1,0:T(8,128)(2,1)S(1)} %get-tuple-element.32), channel_id=1, source_target_pairs={{0,1},{1,0},{2,3},{3,2},{4,5},{5,4},{6,7},{7,6},{8,9},{9,8},{10,11... | collective-permute-start | bytes 589832 | tf_op jit(solution)/shard_map/ppermute | solution.py:470
  8.5 8.7 %collective-permute-start.1 = (bf16[32,1024]{1,0:T(8,128)(2,1)S(1)}, bf16[32,1024]{1,0:T(8,128)(2,1)S(1)}, u32[]{:S(2)}, u32[]{:S(2)}) collective-permute-start(bf16[32,1024]{1,0:T(8,128)(2,1)S(1)} %get-tuple-element.28), channel_id=1, source_target_pairs={{0,4},{1,5},{2,6},{3,7},{4,0},{5,1},{6,2},{7,3},{8,12},{9,13},{10,... | collective-permute-start | bytes 196616 | tf_op jit(solution)/shard_map/ppermute | solution.py:470
  17.0 15.2 %collective-permute-start.27 = (bf16[64,1024]{1,0:T(8,128)(2,1)S(1)}, bf16[64,1024]{1,0:T(8,128)(2,1)S(1)}, u32[]{:S(2)}, u32[]{:S(2)}) collective-permute-start(bf16[64,1024]{1,0:T(8,128)(2,1)S(1)} %get-tuple-element.39.refs_0_), channel_id=1, source_target_pairs={{0,8},{1,9},{2,10},{3,11},{4,12},{5,13},{6,14},{7,15},{8,0},{9,1},... | collective-permute-start | bytes 393224 | tf_op jit(solution)/shard_map/ppermute | solution.py:470
  18.2 11.1 %collective-permute-start.44 = (bf16[64,512]{1,0:T(8,128)(2,1)S(1)}, bf16[64,512]{1,0:T(8,128)(2,1)S(1)}, u32[]{:S(2)}, u32[]{:S(2)}) collective-permute-start(bf16[64,512]{1,0:T(8,128)(2,1)S(1)} %get-tuple-element.44.refs_0_), channel_id=1, source_target_pairs={{0,8},{1,9},{2,10},{3,11},{4,12},{5,13},{6,14},{7,15},{8,0},{9,1},... | collective-permute-start | bytes 196616 | tf_op jit(solution)/shard_map/ppermute | solution.py:470
  20.1 11.7 %collective-permute-start.45 = (bf16[64,512]{1,0:T(8,128)(2,1)S(1)}, bf16[64,512]{1,0:T(8,128)(2,1)S(1)}, u32[]{:S(2)}, u32[]{:S(2)}) collective-permute-start(bf16[64,512]{1,0:T(8,128)(2,1)S(1)} %get-tuple-element.44.refs_0_), channel_id=1, source_target_pairs={{0,12},{1,13},{2,14},{3,15},{4,8},{5,9},{6,10},{7,11},{8,4},{9,5},... | collective-permute-start | bytes 196616 | tf_op jit(solution)/shard_map/ppermute | solution.py:470
  21.6 11.2 %collective-permute-start.12 = (bf16[128,384]{1,0:T(8,128)(2,1)S(1)}, bf16[128,384]{1,0:T(8,128)(2,1)S(1)}, u32[]{:S(2)}, u32[]{:S(2)}) collective-permute-start(bf16[128,384]{1,0:T(8,128)(2,1)S(1)} %get-tuple-element.34), channel_id=1, source_target_pairs={{0,2},{1,3},{2,0},{3,1},{4,6},{5,7},{6,4},{7,5},{8,10},{9,11},{10,... | collective-permute-start | bytes 294920 | tf_op jit(solution)/shard_map/ppermute | solution.py:470
  23.2 12.0 %collective-permute-start.13 = (bf16[128,384]{1,0:T(8,128)(2,1)S(1)}, bf16[128,384]{1,0:T(8,128)(2,1)S(1)}, u32[]{:S(2)}, u32[]{:S(2)}) collective-permute-start(bf16[128,384]{1,0:T(8,128)(2,1)S(1)} %get-tuple-element.35), channel_id=1, source_target_pairs={{0,16},{1,17},{2,18},{3,19},{4,20},{5,21},{6,22},{7,23},{8,24},{9,... | collective-permute-start | bytes 294920 | tf_op jit(solution)/shard_map/ppermute | solution.py:470
  29.3 17.2 %collective-permute-start.6 = (bf16[128,1024]{1,0:T(8,128)(2,1)S(1)}, bf16[128,1024]{1,0:T(8,128)(2,1)S(1)}, u32[]{:S(2)}, u32[]{:S(2)}) collective-permute-start(bf16[128,1024]{1,0:T(8,128)(2,1)S(1)} %shard_map.56.refs_2_), channel_id=1, source_target_pairs={{0,18},{1,19},{2,16},{3,17},{4,22},{5,23},{6,20},{7,21},{8,26},{9,... | collective-permute-start | bytes 786440 | tf_op jit(solution)/shard_map/ppermute | solution.py:470
  31.8 17.9 %collective-permute-start.4 = (bf16[128,1024]{1,0:T(8,128)(2,1)S(1)}, bf16[128,1024]{1,0:T(8,128)(2,1)S(1)}, u32[]{:S(2)}, u32[]{:S(2)}) collective-permute-start(bf16[128,1024]{1,0:T(8,128)(2,1)S(1)} %shard_map.56.refs_2_), channel_id=1, source_target_pairs={{0,2},{1,3},{2,0},{3,1},{4,6},{5,7},{6,4},{7,5},{8,10},{9,11},{10,... | collective-permute-start | bytes 786440 | tf_op jit(solution)/shard_map/ppermute | solution.py:470
  32.3 17.4 %collective-permute-start.5 = (bf16[128,1024]{1,0:T(8,128)(2,1)S(1)}, bf16[128,1024]{1,0:T(8,128)(2,1)S(1)}, u32[]{:S(2)}, u32[]{:S(2)}) collective-permute-start(bf16[128,1024]{1,0:T(8,128)(2,1)S(1)} %shard_map.56.refs_2_), channel_id=1, source_target_pairs={{0,16},{1,17},{2,18},{3,19},{4,20},{5,21},{6,22},{7,23},{8,24},{9,... | collective-permute-start | bytes 786440 | tf_op jit(solution)/shard_map/ppermute | solution.py:470
  32.8 13.0 %collective-permute-start.14 = (bf16[128,384]{1,0:T(8,128)(2,1)S(1)}, bf16[128,384]{1,0:T(8,128)(2,1)S(1)}, u32[]{:S(2)}, u32[]{:S(2)}) collective-permute-start(bf16[128,384]{1,0:T(8,128)(2,1)S(1)} %get-tuple-element.36), channel_id=1, source_target_pairs={{0,18},{1,19},{2,16},{3,17},{4,22},{5,23},{6,20},{7,21},{8,26},{9,... | collective-permute-start | bytes 294920 | tf_op jit(solution)/shard_map/ppermute | solution.py:470
  35.3 11.1 %collective-permute-start.26 = (bf16[64,1024]{1,0:T(8,128)(2,1)S(1)}, bf16[64,1024]{1,0:T(8,128)(2,1)S(1)}, u32[]{:S(2)}, u32[]{:S(2)}) collective-permute-start(bf16[64,1024]{1,0:T(8,128)(2,1)S(1)} %get-tuple-element.39.refs_0_), channel_id=1, source_target_pairs={{0,4},{1,5},{2,6},{3,7},{4,0},{5,1},{6,2},{7,3},{8,12},{9,13},{10,... | collective-permute-start | bytes 393224 | tf_op jit(solution)/shard_map/ppermute | solution.py:470
  46.4 19.8 %collective-permute-start.16 = (bf16[256,384]{1,0:T(8,128)(2,1)S(1)}, bf16[256,384]{1,0:T(8,128)(2,1)}, u32[]{:S(2)}, u32[]{:S(2)}) collective-permute-start(bf16[256,384]{1,0:T(8,128)(2,1)S(1)} %get-tuple-element.37.refs_10_), channel_id=1, source_target_pairs={{0,8},{1,9},{2,10},{3,11},{4,12},{5,13},{6,14},{7,15},{8,0},{9,1},... | collective-permute-start | bytes 589832 | tf_op jit(solution)/shard_map/ppermute | solution.py:470
  46.5 20.2 %collective-permute-start.15 = (bf16[256,384]{1,0:T(8,128)(2,1)S(1)}, bf16[256,384]{1,0:T(8,128)(2,1)}, u32[]{:S(2)}, u32[]{:S(2)}) collective-permute-start(bf16[256,384]{1,0:T(8,128)(2,1)S(1)} %get-tuple-element.37.refs_10_), channel_id=1, source_target_pairs={{0,4},{1,5},{2,6},{3,7},{4,0},{5,1},{6,2},{7,3},{8,12},{9,13},{10,... | collective-permute-start | bytes 589832 | tf_op jit(solution)/shard_map/ppermute | solution.py:470
  49.6 17.4 %collective-permute-start.36 = (bf16[256,384]{1,0:T(8,128)(2,1)S(1)}, bf16[256,384]{1,0:T(8,128)(2,1)S(1)}, u32[]{:S(2)}, u32[]{:S(2)}) collective-permute-start(bf16[256,384]{1,0:T(8,128)(2,1)S(1)} %get-tuple-element.40.refs_26_), channel_id=1, source_target_pairs={{0,4},{1,5},{2,6},{3,7},{4,0},{5,1},{6,2},{7,3},{8,12},{9,13},{10,... | collective-permute-start | bytes 589832 | tf_op jit(solution)/shard_map/ppermute | solution.py:470
  49.7 16.4 %collective-permute-start.28 = (bf16[64,1024]{1,0:T(8,128)(2,1)S(1)}, bf16[64,1024]{1,0:T(8,128)(2,1)S(1)}, u32[]{:S(2)}, u32[]{:S(2)}) collective-permute-start(bf16[64,1024]{1,0:T(8,128)(2,1)S(1)} %collective-permute-done.27.refs_2_), channel_id=1, source_target_pairs={{0,4},{1,5},{2,6},{3,7},{4,0},{5,1},{6,2},{7,3},{8,12},{9,13},{10,... | collective-permute-start | bytes 393224 | tf_op jit(solution)/shard_map/ppermute | solution.py:470
  51.7 28.3 %collective-permute-start.10 = (bf16[128,1024]{1,0:T(8,128)(2,1)S(1)}, bf16[128,1024]{1,0:T(8,128)(2,1)S(1)}, u32[]{:S(2)}, u32[]{:S(2)}) collective-permute-start(bf16[128,1024]{1,0:T(8,128)(2,1)S(1)} %collective-permute-done.6.refs_5_), channel_id=1, source_target_pairs={{0,1},{1,0},{2,3},{3,2},{4,5},{5,4},{6,7},{7,6},{8,9},{9,8},{10,11... | collective-permute-start | bytes 786440 | tf_op jit(solution)/shard_map/ppermute | solution.py:470
  66.1 15.4 %collective-permute-start.8 = (bf16[128,1024]{1,0:T(8,128)(2,1)S(1)}, bf16[128,1024]{1,0:T(8,128)(2,1)S(1)}, u32[]{:S(2)}, u32[]{:S(2)}) collective-permute-start(bf16[128,1024]{1,0:T(8,128)(2,1)S(1)} %collective-permute-done.4.refs_3_), channel_id=1, source_target_pairs={{0,1},{1,0},{2,3},{3,2},{4,5},{5,4},{6,7},{7,6},{8,9},{9,8},{10,11... | collective-permute-start | bytes 786440 | tf_op jit(solution)/shard_map/ppermute | solution.py:470
  66.1 16.9 %collective-permute-start.9 = (bf16[128,1024]{1,0:T(8,128)(2,1)S(1)}, bf16[128,1024]{1,0:T(8,128)(2,1)S(1)}, u32[]{:S(2)}, u32[]{:S(2)}) collective-permute-start(bf16[128,1024]{1,0:T(8,128)(2,1)S(1)} %collective-permute-done.5.refs_4_), channel_id=1, source_target_pairs={{0,1},{1,0},{2,3},{3,2},{4,5},{5,4},{6,7},{7,6},{8,9},{9,8},{10,11... | collective-permute-start | bytes 786440 | tf_op jit(solution)/shard_map/ppermute | solution.py:470
  66.7 11.1 %collective-permute-start.37 = (bf16[256,384]{1,0:T(8,128)(2,1)S(1)}, bf16[256,384]{1,0:T(8,128)(2,1)S(1)}, u32[]{:S(2)}, u32[]{:S(2)}) collective-permute-start(bf16[256,384]{1,0:T(8,128)(2,1)S(1)} %get-tuple-element.40.refs_26_), channel_id=1, source_target_pairs={{0,8},{1,9},{2,10},{3,11},{4,12},{5,13},{6,14},{7,15},{8,0},{9,1},... | collective-permute-start | bytes 589832 | tf_op jit(solution)/shard_map/ppermute | solution.py:470
  67.0 16.5 %collective-permute-start.17 = (bf16[256,384]{1,0:T(8,128)(2,1)}, bf16[256,384]{1,0:T(8,128)(2,1)S(1)}, u32[]{:S(2)}, u32[]{:S(2)}) collective-permute-start(bf16[256,384]{1,0:T(8,128)(2,1)} %collective-permute-done.16.refs_12_), channel_id=1, source_target_pairs={{0,4},{1,5},{2,6},{3,7},{4,0},{5,1},{6,2},{7,3},{8,12},{9,13},{10,... | collective-permute-start | bytes 589832 | tf_op jit(solution)/shard_map/ppermute | solution.py:470
  77.7 13.5 %collective-permute-start.38 = (bf16[256,384]{1,0:T(8,128)(2,1)S(1)}, bf16[256,384]{1,0:T(8,128)(2,1)S(1)}, u32[]{:S(2)}, u32[]{:S(2)}) collective-permute-start(bf16[256,384]{1,0:T(8,128)(2,1)S(1)} %get-tuple-element.40.refs_26_), channel_id=1, source_target_pairs={{0,12},{1,13},{2,14},{3,15},{4,8},{5,9},{6,10},{7,11},{8,4},{9,5},... | collective-permute-start | bytes 589832 | tf_op jit(solution)/shard_map/ppermute | solution.py:470
  80.0 13.9 %collective-permute-start.29 = (bf16[256,1024]{1,0:T(8,128)(2,1)S(1)}, bf16[256,1024]{1,0:T(8,128)(2,1)S(1)}, u32[]{:S(2)}, u32[]{:S(2)}) collective-permute-start(bf16[256,1024]{1,0:T(8,128)(2,1)S(1)} %shard_map.61.refs_18_), channel_id=1, source_target_pairs={{0,2},{1,3},{2,0},{3,1},{4,6},{5,7},{6,4},{7,5},{8,10},{9,11},{10,... | collective-permute-start | bytes 1572872 | tf_op jit(solution)/shard_map/ppermute | solution.py:470
  81.5 14.8 %collective-permute-start.30 = (bf16[256,1024]{1,0:T(8,128)(2,1)S(1)}, bf16[256,1024]{1,0:T(8,128)(2,1)S(1)}, u32[]{:S(2)}, u32[]{:S(2)}) collective-permute-start(bf16[256,1024]{1,0:T(8,128)(2,1)S(1)} %shard_map.61.refs_18_), channel_id=1, source_target_pairs={{0,16},{1,17},{2,18},{3,19},{4,20},{5,21},{6,22},{7,23},{8,24},{9,... | collective-permute-start | bytes 1572872 | tf_op jit(solution)/shard_map/ppermute | solution.py:470
  83.0 24.5 %collective-permute-start.31 = (bf16[256,1024]{1,0:T(8,128)(2,1)S(1)}, bf16[256,1024]{1,0:T(8,128)(2,1)S(1)}, u32[]{:S(2)}, u32[]{:S(2)}) collective-permute-start(bf16[256,1024]{1,0:T(8,128)(2,1)S(1)} %shard_map.61.refs_18_), channel_id=1, source_target_pairs={{0,18},{1,19},{2,16},{3,17},{4,22},{5,23},{6,20},{7,21},{8,26},{9,... | collective-permute-start | bytes 1572872 | tf_op jit(solution)/shard_map/ppermute | solution.py:470
  83.5 24.0 %collective-permute-start.32 = (bf16[256,1024]{1,0:T(8,128)(2,1)S(1)}, bf16[256,1024]{1,0:T(8,128)(2,1)S(1)}, u32[]{:S(2)}, u32[]{:S(2)}) collective-permute-start(bf16[256,1024]{1,0:T(8,128)(2,1)S(1)} %shard_map.61.refs_18_), channel_id=1, source_target_pairs={{0,1},{1,0},{2,3},{3,2},{4,5},{5,4},{6,7},{7,6},{8,9},{9,8},{10,11... | collective-permute-start | bytes 1572872 | tf_op jit(solution)/shard_map/ppermute | solution.py:470
  91.2 20.0 %collective-permute-start.18 = (bf16[1024,128]{1,0:T(8,128)(2,1)S(1)}, bf16[1024,128]{1,0:T(8,128)(2,1)S(1)}, u32[]{:S(2)}, u32[]{:S(2)}) collective-permute-start(bf16[1024,128]{1,0:T(8,128)(2,1)S(1)} %shard_map.59.refs_10_), channel_id=1, source_target_pairs={{0,2},{1,3},{2,0},{3,1},{4,6},{5,7},{6,4},{7,5},{8,10},{9,11},{10,... | collective-permute-start | bytes 786440 | tf_op jit(solution)/shard_map/ppermute | solution.py:470
  93.9 19.3 %collective-permute-start.19 = (bf16[1024,128]{1,0:T(8,128)(2,1)S(1)}, bf16[1024,128]{1,0:T(8,128)(2,1)S(1)}, u32[]{:S(2)}, u32[]{:S(2)}) collective-permute-start(bf16[1024,128]{1,0:T(8,128)(2,1)S(1)} %shard_map.59.refs_10_), channel_id=1, source_target_pairs={{0,16},{1,17},{2,18},{3,19},{4,20},{5,21},{6,22},{7,23},{8,24},{9,... | collective-permute-start | bytes 786440 | tf_op jit(solution)/shard_map/ppermute | solution.py:470
  96.3 20.9 %collective-permute-start.20 = (bf16[1024,128]{1,0:T(8,128)(2,1)S(1)}, bf16[1024,128]{1,0:T(8,128)(2,1)S(1)}, u32[]{:S(2)}, u32[]{:S(2)}) collective-permute-start(bf16[1024,128]{1,0:T(8,128)(2,1)S(1)} %shard_map.59.refs_10_), channel_id=1, source_target_pairs={{0,18},{1,19},{2,16},{3,17},{4,22},{5,23},{6,20},{7,21},{8,26},{9,... | collective-permute-start | bytes 786440 | tf_op jit(solution)/shard_map/ppermute | solution.py:470
  107.5 9.7 %collective-permute-start.21 = (bf16[1024,128]{1,0:T(8,128)(2,1)S(1)}, bf16[1024,128]{1,0:T(8,128)(2,1)S(1)}, u32[]{:S(2)}, u32[]{:S(2)}) collective-permute-start(bf16[1024,128]{1,0:T(8,128)(2,1)S(1)} %shard_map.59.refs_10_), channel_id=1, source_target_pairs={{0,1},{1,0},{2,3},{3,2},{4,5},{5,4},{6,7},{7,6},{8,9},{9,8},{10,11... | collective-permute-start | bytes 786440 | tf_op jit(solution)/shard_map/ppermute | solution.py:470
  107.5 13.5 %collective-permute-start.33 = (bf16[256,1024]{1,0:T(8,128)(2,1)S(1)}, bf16[256,1024]{1,0:T(8,128)(2,1)S(1)}, u32[]{:S(2)}, u32[]{:S(2)}) collective-permute-start(bf16[256,1024]{1,0:T(8,128)(2,1)S(1)} %collective-permute-done.29.refs_19_), channel_id=1, source_target_pairs={{0,1},{1,0},{2,3},{3,2},{4,5},{5,4},{6,7},{7,6},{8,9},{9,8},{10,11... | collective-permute-start | bytes 1572872 | tf_op jit(solution)/shard_map/ppermute | solution.py:470
  119.5 19.5 %collective-permute-start.46 = (bf16[256,512]{1,0:T(8,128)(2,1)S(1)}, bf16[256,512]{1,0:T(8,128)(2,1)S(1)}, u32[]{:S(2)}, u32[]{:S(2)}) collective-permute-start(bf16[256,512]{1,0:T(8,128)(2,1)S(1)} %shard_map.64.refs_7_), channel_id=1, source_target_pairs={{0,2},{1,3},{2,0},{3,1},{4,6},{5,7},{6,4},{7,5},{8,10},{9,11},{10,... | collective-permute-start | bytes 786440 | tf_op jit(solution)/shard_map/ppermute | solution.py:470
  (25 other events, 127.6 us)

commit v2 on v1

--- a/solution.py
+++ b/solution.py
@@ -257,74 +257,90 @@
     return pl.ds(pl.multiple_of(index * size, size), size)
 
 
-def start_all(copies):
-    for copy in copies:
-        copy.start()
-    for copy in copies:
-        copy.wait()
-
-
-def prepare_kernel(plan, where, latents, qkv_weight, proj_weight, merge_weight, *rest):
+def prepare_kernel(plan, where, latents, gain, qkv_weight, proj_weight, merge_weight, *rest):
     shares = rest[: plan.windows]
-    keep, give, cross, sems = rest[plan.windows :]
+    keep, give, cross, held, sems = rest[plan.windows :]
     copies = []
 
     def add(source, target):
         copies.append(pltpu.make_async_copy(source, target, sems.at[len(copies)]))
 
-    for core, target in ((1, give), (0, keep)):
-        for chip_no, (mx, mi) in enumerate(plan.chips):
-            slot = slot_of(plan, where, mx, mi ^ core)
-            for part in range(3):
-                add(
-                    qkv_weight.at[0, :, aligned(part * plan.slots + slot, plan.cols)],
-                    target.at[chip_no, :, part * plan.cols : (part + 1) * plan.cols],
-                )
-    width = plan.half_cols
+    for part in range(3):
+        add(
+            qkv_weight.at[0, :, part * plan.features : (part + 1) * plan.features],
+            held.at[part],
+        )
+    width, rows = (plan.half_cols, plan.w_rows)
     for part, matrix in enumerate((proj_weight, merge_weight)):
         add(
             matrix.at[0, :, aligned(where[0] ^ 1, width)],
-            cross.at[:, part * width : (part + 1) * width],
+            cross.at[part * rows : (part + 1) * rows, :],
         )
     for mz in range(plan.windows):
         add(latents.at[where[1] ^ mz, aligned(where[0], plan.half), :], shares[mz])
-    start_all(copies)
-
-
-def pair_kernel(plan, keep, given, *outs):
+    for copy in copies:
+        copy.start()
+    first_row = (where[1] * plan.inner + where[2]) * rows
+    row = first_row + lax.broadcasted_iota(jnp.int32, (rows, plan.features), 0)
+    lane = lax.broadcasted_iota(jnp.int32, (rows, plan.features), 1)
+    factors = jnp.where(row == lane, gain[...], jnp.zeros((1, plan.features), jnp.float32))
+    factors = jnp.sum(factors, axis=1, keepdims=True)
+    for copy in copies[:3]:
+        copy.wait()
+    for core, target in ((1, give), (0, keep)):
+        for chip_no, (mx, mi) in enumerate(plan.chips):
+            lanes = aligned(slot_of(plan, where, mx, mi ^ core), plan.cols)
+            for part in range(3):
+                scaled = held[part, :, lanes].astype(jnp.float32) * factors
+                target[chip_no, :, part * plan.cols : (part + 1) * plan.cols] = scaled.astype(
+                    jnp.bfloat16
+                )
+    for copy in copies[3:]:
+        copy.wait()
+
+
+def pair_kernel(plan, keep, given, cross, *outs):
     rows = plan.w_rows
-    for chip_no, out in enumerate(outs):
-        out[0:rows, :] = keep[chip_no]
-        out[rows:, :] = given[chip_no]
-
-
-def sort_kernel(plan, where, *refs):
+    for chip_no, (out, chip) in enumerate(zip(outs, plan.chips)):
+        out[0:rows, 0 : 3 * plan.cols] = keep[chip_no]
+        out[rows:, 0 : 3 * plan.cols] = given[chip_no]
+        if chip == (1, 0):
+            out[:, 3 * plan.cols :] = cross[...]
+
+
+def sort_kernel(plan, where, proj_weight, merge_weight, *refs):
     count = len(plan.chips)
-    pieces, outs = (refs[:count], refs[count:])
-    rows = 2 * plan.w_rows
+    pieces, (rows_a, rows_b, mats) = (refs[:count], refs[count:])
+    rows, width, cols = (plan.w_rows, plan.half_cols, 3 * plan.cols)
+    lone = width // plan.inner
+    crossed = pieces[plan.chips.index((1, 0))]
     for section in range(plan.sections):
 
         @pl.when(where[0] == section)
         def _():
+            outs = (rows_a, rows_b)
             for piece, (mx, mi) in zip(pieces, plan.chips):
-                start = mi * plan.w_rows
-                outs[section ^ mx][start : start + rows, :] = piece[...]
-
-
-def merge_kernel(plan, where, proj_weight, merge_weight, crossed, mats, last):
-    width = plan.half_cols
-    for section in range(plan.sections):
-
-        @pl.when(where[0] == section)
-        def _():
+                part = slice(mi * rows, (mi + 2) * rows)
+                outs[section ^ mx][part, 0:cols] = piece[:, 0:cols]
             lanes = slice(section * width, (section + 1) * width)
             mine = proj_weight[0, :, lanes]
-            others = crossed[:, 0:width]
+            others = crossed[0:rows, cols:]
             mats[:, 0:width] = mine if section == 0 else others
-            last[...] = others if section == 0 else mine
+            last = others if section == 0 else mine
+            for mi in range(plan.inner):
+                rows_b[mi * rows : (mi + 1) * rows, cols:] = last[:, mi * lone : (mi + 1) * lone]
             total = merge_weight[0, :, lanes].astype(jnp.float32)
-            total = total + crossed[:, width:].astype(jnp.float32)
+            total = total + crossed[rows:, cols:].astype(jnp.float32)
             mats[:, width:] = total.astype(jnp.bfloat16)
+
+
+def last_kernel(plan, *refs):
+    rows, lone = (plan.w_rows, plan.half_cols // plan.inner)
+    for mz, piece in enumerate(refs[:-1]):
+        for mi in range(plan.inner):
+            refs[-1][mz * rows : (mz + 1) * rows, mi * lone : (mi + 1) * lone] = piece[
+                mi * rows : (mi + 1) * rows, 3 * plan.cols :
+            ]
 
 
 def stack_kernel(*refs):
@@ -340,34 +356,58 @@
     for mz, piece in enumerate(pieces):
         for mi in range(plan.inner):
             shard = (where[1] ^ mz) * plan.inner + (where[2] ^ mi)
-            target[aligned(shard, rows), :] = piece[mi * rows : (mi + 1) * rows, :]
+            target[aligned(shard, rows), :] = piece[
+                mi * rows : (mi + 1) * rows, 0 : 3 * plan.cols
+            ]
 
 
 def plane_order(plan):
     return [(mx, mi ^ core) for core in range(2) for mx, mi in plan.chips]
 
 
-def first_kernel(plan, where, gain, *rest):
+def normalize(values):
+    center = values - jnp.mean(values, axis=-1, keepdims=True)
+    spread = jnp.mean(center * center, axis=-1, keepdims=True)
+    return (center * lax.rsqrt(spread + EPSILON)).astype(jnp.bfloat16)
+
+
+def row_blocks(plan, one_block):
+    size = min(512, plan.tokens)
+
+    def step(block_no, carry):
+        one_block(aligned(block_no, size))
+        return carry
+
+    lax.fori_loop(0, plan.tokens // size, step, 0)
+
+
+def first_kernel(plan, where, *rest):
     hidden_in = rest[: plan.slots]
     pieces = rest[plan.slots : plan.slots + plan.windows]
-    out, w_qkv, qkv = rest[plan.slots + plan.windows :]
+    out, w_qkv, normed, qkv = rest[plan.slots + plan.windows :]
     gather_weights(plan, where, pieces, w_qkv)
     for piece, (mx, mi) in zip(hidden_in, plane_order(plan)):
-        normed = layer_norm(piece[...], gain[...])
         rows = aligned(slot_of(plan, where, mx, mi), plan.shard)
-        qkv[rows, :] = project_rows(normed, w_qkv[...], plan.cols)
+        normed[rows, :] = normalize(piece[...].astype(jnp.float32))
+
+    def one_block(rows):
+        qkv[rows, :] = project_rows(normed[rows, :], w_qkv[...], plan.cols)
+
+    row_blocks(plan, one_block)
     attention(qkv, out, plan.cols, min(256, plan.tokens))
 
 
-def second_kernel(plan, where, gain, *rest):
+def second_kernel(plan, where, *rest):
     slots, windows = (plan.slots, plan.windows)
     hidden_in, rest = (rest[:slots], rest[slots:])
     attended_in, rest = (rest[:slots], rest[slots:])
     mats_in, rest = (rest[:slots], rest[slots:])
     pieces, rest = (rest[:windows], rest[windows:])
     outs, rest = (rest[: plan.inner // 2], rest[plan.inner // 2 :])
-    kept, att, mats, w_qkv, joined, qkv, mixed = rest
+    kept, hid, att, mats, w_qkv, joined, qkv, mixed = rest
     order = plane_order(plan)
+    for piece, (mx, mi) in zip(hidden_in, order):
+        hid[aligned(slot_of(plan, where, mx, mi), plan.shard), :] = piece[...]
     for piece, (mx, mi) in zip(attended_in, order):
         att[:, aligned(slot_of(plan, where, mx, mi), plan.cols)] = piece[...]
     rows = plan.w_rows
@@ -377,8 +417,8 @@
             mats[where[0] ^ mx, aligned(shard, rows), :] = piece[mz * rows : (mz + 1) * rows, :]
     gather_weights(plan, where, pieces, w_qkv)
     width = plan.half_cols
-    for piece, (mx, mi) in zip(hidden_in, order):
-        part = aligned(slot_of(plan, where, mx, mi), plan.shard)
+
+    def one_block(part):
         attended = att[part, :]
         hidden = jnp.concatenate(
             [
@@ -387,17 +427,21 @@
             ],
             axis=1,
         )
-        hidden = (piece[...].astype(jnp.float32) + hidden).astype(jnp.bfloat16)
+        hidden = (hid[part, :].astype(jnp.float32) + hidden).astype(jnp.bfloat16)
         merged = jnp.concatenate(
             [
                 jnp.dot(hidden, mats[side, :, width:], preferred_element_type=jnp.float32)
                 for side in range(plan.sections)
             ],
             axis=1,
-        ).astype(jnp.bfloat16)
+        )
+        merged = merged.astype(jnp.bfloat16)
         joined[part, :] = merged
-        normed = layer_norm(merged, gain[...])
-        qkv[part, :] = project_rows(normed, w_qkv[...], plan.cols)
+        qkv[part, :] = project_rows(
+            normalize(merged.astype(jnp.float32)), w_qkv[...], plan.cols
+        )
+
+    row_blocks(plan, one_block)
     attention(qkv, mixed, plan.cols, min(256, plan.tokens))
     lanes = aligned(where[0], width)
     for side in range(plan.sections):
@@ -461,7 +505,7 @@
     devices = plan.sections * plan.seq_count
     bf16 = jnp.bfloat16
     smem = pl.BlockSpec(memory_space=pltpu.SMEM)
-    anywhere = pl.BlockSpec(memory_space=pl.ANY)
+    hbm = pl.BlockSpec(memory_space=pltpu.HBM)
     vmem = pl.BlockSpec(memory_space=pltpu.VMEM)
     tokens, features, width = (plan.tokens, plan.features, plan.half_cols)
 
@@ -489,9 +533,11 @@
         return call(stack_kernel, [(rows, pieces[0].shape[1])], pieces, limit=8)[0]
 
     def z_gather(value):
-        far = swap(value, plan.mask(mz=2))
-        near = swap(value, plan.mask(mz=1))
-        return [value, near, far, swap(far, plan.mask(mz=1))]
+        pieces = [value]
+        for mz in range(1, windows):
+            low = mz & -mz
+            pieces.append(swap(pieces[mz - low], plan.mask(mz=low)))
+        return pieces
 
     def chip_gather(value):
         return [value] + [
@@ -503,28 +549,29 @@
     def core_gather(pieces):
         return pieces + [swap(piece, plan.mask(mi=1)) for piece in pieces]
 
-    n_parts = 6 * len(plan.chips)
     prepared = call(
         lambda *refs: prepare_kernel(plan, *refs),
         [(plan.half, features)] * windows
         + [(len(plan.chips), plan.w_rows, 3 * cols)] * 2
-        + [(plan.w_rows, 2 * width)],
-        [where, latents, qkv_weight, proj_weight, merge_weight],
-        [pltpu.SemaphoreType.DMA((n_parts + 2 + windows,))],
-        [smem] + [anywhere] * 4,
+        + [(2 * plan.w_rows, width)],
+        [where, latents, norm_gain, qkv_weight, proj_weight, merge_weight],
+        [
+            pltpu.VMEM((3, plan.w_rows, features), bf16),
+            pltpu.SemaphoreType.DMA((5 + windows,)),
+        ],
+        [smem, hbm, vmem, hbm, hbm, hbm],
         limit=8,
     )
     shares, (keep, give, cross) = (prepared[:windows], prepared[windows:])
     given = swap(give, plan.mask(mi=1))
-    crossed = swap(cross, plan.mask(mx=1))
-    other_gain = swap(norm_gain, plan.mask(mx=1))
-    gain_a = jnp.where(section == 0, norm_gain, other_gain)
-    gain_b = jnp.where(section == 0, other_gain, norm_gain)
     shares = [shares[0]] + [swap(shares[mz], plan.mask(mz=mz)) for mz in range(1, windows)]
     outgoing = call(
         lambda *refs: pair_kernel(plan, *refs),
-        [(2 * plan.w_rows, 3 * cols)] * len(plan.chips),
-        [keep, given],
+        [
+            (2 * plan.w_rows, 3 * cols + (width if chip == (1, 0) else 0))
+            for chip in plan.chips
+        ],
+        [keep, given, cross],
         limit=8,
     )
     incoming = [outgoing[0]] + [
@@ -532,48 +579,48 @@
         for chip_no, (mx, mi) in enumerate(plan.chips)
         if chip_no
     ]
-    mats, last = call(
-        lambda *refs: merge_kernel(plan, *refs),
-        [(plan.w_rows, 2 * width), (plan.w_rows, width)],
-        [where, proj_weight, merge_weight, crossed],
-        (),
-        [smem] + [vmem] * 3,
-        limit=8,
-    )
-    mats = z_gather(mats)
     hidden = chip_gather(stack(shares))
     hidden = core_gather(hidden)
-    rows_a, rows_b = call(
+    rows_a, rows_b, mats = call(
         lambda *refs: sort_kernel(plan, *refs),
-        [(plan.group, 3 * cols)] * 2,
-        [where] + incoming,
+        [
+            (plan.group, 3 * cols),
+            (plan.group, 3 * cols + width // inner),
+            (plan.w_rows, 2 * width),
+        ],
+        [where, proj_weight, merge_weight] + incoming,
         (),
-        [smem] + [vmem] * len(incoming),
+        [smem] + [vmem] * (2 + len(incoming)),
         limit=8,
     )
+    mats = z_gather(mats)
     pieces_a = z_gather(rows_a)
+    pieces_b = z_gather(rows_b)
     mats = chip_gather(stack(mats))
-    pieces_b = [rows_b] + [swap(rows_b, plan.mask(mz=mz)) for mz in range(1, windows)]
-    last = [last] + [swap(last, plan.mask(mz=mz)) for mz in range(1, windows)]
 
     (attended,) = call(
         lambda *refs: first_kernel(plan, *refs),
         [(tokens, cols)],
-        [where, gain_a] + hidden + pieces_a,
-        [pltpu.VMEM((features, 3 * cols), bf16), pltpu.VMEM((tokens, 3 * cols), bf16)],
-        [smem] + [vmem] * (1 + len(hidden) + windows),
+        [where] + hidden + pieces_a,
+        [
+            pltpu.VMEM((features, 3 * cols), bf16),
+            pltpu.VMEM((tokens, features), bf16),
+            pltpu.VMEM((tokens, 3 * cols), bf16),
+        ],
+        [smem] + [vmem] * (len(hidden) + windows),
         flops=10_000_000_000,
     )
     attended = core_gather(chip_gather(attended))
     mats = core_gather(mats)
-    last = stack(last)
+    (last,) = call(lambda *refs: last_kernel(plan, *refs), [(plan.group, width)], pieces_b, limit=8)
     last = [last] + [swap(last, plan.mask(mi=mi)) for mi in range(2, inner, 2)]
     last = core_gather(last)
     *attended, kept = call(
         lambda *refs: second_kernel(plan, *refs),
         [(2 * plan.sections * shard, cols)] * (inner // 2) + [(plan.sections * shard, width)],
-        [where, gain_b] + hidden + attended + mats + pieces_b,
+        [where] + hidden + attended + mats + pieces_b,
         [
+            pltpu.VMEM((tokens, features), bf16),
             pltpu.VMEM((tokens, features), bf16),
             pltpu.VMEM((plan.sections, features, 2 * width), bf16),
             pltpu.VMEM((features, 3 * cols), bf16),
@@ -581,7 +628,7 @@
             pltpu.VMEM((tokens, 3 * cols), bf16),
             pltpu.VMEM((tokens, cols), bf16),
         ],
-        [smem] + [vmem] * (1 + 3 * plan.slots + windows),
+        [smem] + [vmem] * (3 * plan.slots + windows),
         flops=18_000_000_000,
     )
     back = [attended[0]] + [
@@ -632,13 +679,14 @@
         return plane_body(*arguments)
 
     def step(latents, *weights):
-        fits = Plan.fits(
+        sizes = (
             mesh.shape["section"],
             mesh.shape["seq"],
             latents.shape[0],
             latents.shape[1] // mesh.shape["seq"],
             latents.shape[2],
         )
+        fits = Plan.fits(*sizes)
         mapped = jax.shard_map(
             plane_step if fits else body,
             mesh=mesh,

time: 158 us -> 151 us (0.956)
  starting transfers between devices: 54.1 us -> 42.4 us
  waiting for transfers between devices: 72 us -> 78.8 us
  Pallas kernels: 27.3 us -> 24.9 us
    ppermute x52 -> x47, starting transfers between devices: 54.1 us -> 42.4 us  [swap(): return lax.ppermute(value, ('section', 'seq'), pairs)]
    ppermute x52 -> x47, waiting for transfers between devices: 72 us -> 78.8 us  [swap(): return lax.ppermute(value, ('section', 'seq'), pairs)]
    pallas_call x12 -> x11, Pallas kernels: 27.3 us -> 24.9 us  [call(): pl.pallas_call(kernel, out_shape=shapes, in_specs=specs or [vmem] * len(i...]
    unnamed x10 -> x14, local copies, waits for them, and re-layouts: 3.85 us -> 4.53 us
  transfers between devices with their start and end apart: 52 -> 47, of which waited for: 17 -> 22; matrix products, arithmetic and copies ran while one was open for 0% -> 0% of each run, Pallas kernels for 15% -> 14%
where the time goes in v2:
time: 151 us
  waiting for transfers between devices  78.8 us (52%)
  starting transfers between devices  42.4 us (28%)
  Pallas kernels  24.9 us (16%)
  local copies, waits for them, and re-layouts  4.53 us (3%)
    ppermute x47, waiting for transfers between devices, swap(): return lax.ppermute(value, ('section', 'seq'), pairs)  78.8 us
    ppermute x47, starting transfers between devices, swap(): return lax.ppermute(value, ('section', 'seq'), pairs)  42.4 us
    pallas_call x11, Pallas kernels, call(): pl.pallas_call(kernel, out_shape=shapes, in_specs=specs or [vmem] * len(i...  24.9 us
    unnamed x14, local copies, waits for them, and re-layouts  4.53 us
  transfers between devices with their start and end apart: 47, of which 22 were waited for; matrix products, arithmetic and copies ran while one was open for 0% of the time, Pallas kernels for 14%

profile of v2, /device:TPU:0, one launch (start us, length us, event | category | flops | bytes accessed | tf_op | source)
XLA Modules:
  0.0 150.7 jit_solution(554564116151284870)
XLA Ops:
  6.4 2.6 %collective-permute-start = (bf16[32,1024]{1,0:T(8,128)(2,1)S(1)}, bf16[32,1024]{1,0:T(8,128)(2,1)S(1)}, u32[]{:S(2)}, u32[]{:S(2)}) collective-permute-start(bf16[32,1024]{1,0:T(8,128)(2,1)S(1)} %get-tuple-element.27), channel_id=1, source_target_pairs={{0,4},{1,5},{2,6},{3,7},{4,0},{5,1},{6,2},{7,3},{8,12},{9,13},{10,... | collective-permute-start | bytes 196616 | tf_op jit(solution)/shard_map/ppermute | solution.py:514
  9.0 2.6 %collective-permute-start.1 = (bf16[32,1024]{1,0:T(8,128)(2,1)S(1)}, bf16[32,1024]{1,0:T(8,128)(2,1)S(1)}, u32[]{:S(2)}, u32[]{:S(2)}) collective-permute-start(bf16[32,1024]{1,0:T(8,128)(2,1)S(1)} %get-tuple-element.28), channel_id=1, source_target_pairs={{0,8},{1,9},{2,10},{3,11},{4,12},{5,13},{6,14},{7,15},{8,0},{9,1},... | collective-permute-start | bytes 196616 | tf_op jit(solution)/shard_map/ppermute | solution.py:514
  11.7 5.0 %collective-permute-done.1.refs_2_ = bf16[32,1024]{1,0:T(8,128)(2,1)S(1)} collective-permute-done((bf16[32,1024]{1,0:T(8,128)(2,1)S(1)}, bf16[32,1024]{1,0:T(8,128)(2,1)S(1)}, u32[]{:S(2)}, u32[]{:S(2)}) %collective-permute-start.1) | collective-permute-done | bytes 65568 | tf_op jit(solution)/shard_map/ppermute | solution.py:514
  17.7 1.6 %collective-permute-start.3 = (bf16[128,1024]{1,0:T(8,128)(2,1)S(1)}, bf16[128,1024]{1,0:T(8,128)(2,1)S(1)}, u32[]{:S(2)}, u32[]{:S(2)}) collective-permute-start(bf16[128,1024]{1,0:T(8,128)(2,1)S(1)} %shard_map.56.refs_1_), channel_id=1, source_target_pairs={{0,2},{1,3},{2,0},{3,1},{4,6},{5,7},{6,4},{7,5},{8,10},{9,11},{10,... | collective-permute-start | bytes 786440 | tf_op jit(solution)/shard_map/ppermute | solution.py:514
  19.9 2.4 %collective-permute-start.13 = (bf16[128,384]{1,0:T(8,128)(2,1)S(1)}, bf16[128,384]{1,0:T(8,128)(2,1)S(1)}, u32[]{:S(2)}, u32[]{:S(2)}) collective-permute-start(bf16[128,384]{1,0:T(8,128)(2,1)S(1)} %get-tuple-element.36), channel_id=1, source_target_pairs={{0,18},{1,19},{2,16},{3,17},{4,22},{5,23},{6,20},{7,21},{8,26},{9,... | collective-permute-start | bytes 294920 | tf_op jit(solution)/shard_map/ppermute | solution.py:514
  24.4 4.6 %collective-permute-done.11.refs_4_ = bf16[128,384]{1,0:T(8,128)(2,1)S(1)} collective-permute-done((bf16[128,384]{1,0:T(8,128)(2,1)S(1)}, bf16[128,384]{1,0:T(8,128)(2,1)S(1)}, u32[]{:S(2)}, u32[]{:S(2)}) %collective-permute-start.11) | collective-permute-done | bytes 98336 | tf_op jit(solution)/shard_map/ppermute | solution.py:514
  29.0 2.4 %collective-permute-start.5 = (bf16[128,1024]{1,0:T(8,128)(2,1)S(1)}, bf16[128,1024]{1,0:T(8,128)(2,1)S(1)}, u32[]{:S(2)}, u32[]{:S(2)}) collective-permute-start(bf16[128,1024]{1,0:T(8,128)(2,1)S(1)} %shard_map.56.refs_1_), channel_id=1, source_target_pairs={{0,18},{1,19},{2,16},{3,17},{4,22},{5,23},{6,20},{7,21},{8,26},{9,... | collective-permute-start | bytes 786440 | tf_op jit(solution)/shard_map/ppermute | solution.py:514
  32.6 2.4 %collective-permute-start.15 = (bf16[256,384]{1,0:T(8,128)(2,1)S(1)}, bf16[256,384]{1,0:T(8,128)(2,1)S(1)}, u32[]{:S(2)}, u32[]{:S(2)}) collective-permute-start(bf16[256,384]{1,0:T(8,128)(2,1)S(1)} %get-tuple-element.37.refs_9_), channel_id=1, source_target_pairs={{0,8},{1,9},{2,10},{3,11},{4,12},{5,13},{6,14},{7,15},{8,0},{9,1},... | collective-permute-start | bytes 589832 | tf_op jit(solution)/shard_map/ppermute | solution.py:514
  35.0 2.0 %collective-permute-done.4.refs_3_ = bf16[128,1024]{1,0:T(8,128)(2,1)S(1)} collective-permute-done((bf16[128,1024]{1,0:T(8,128)(2,1)S(1)}, bf16[128,1024]{1,0:T(8,128)(2,1)S(1)}, u32[]{:S(2)}, u32[]{:S(2)}) %collective-permute-start.4) | collective-permute-done | bytes 262176 | tf_op jit(solution)/shard_map/ppermute | solution.py:514
  37.1 3.0 %collective-permute-done.5.refs_4_ = bf16[128,1024]{1,0:T(8,128)(2,1)S(1)} collective-permute-done((bf16[128,1024]{1,0:T(8,128)(2,1)S(1)}, bf16[128,1024]{1,0:T(8,128)(2,1)S(1)}, u32[]{:S(2)}, u32[]{:S(2)}) %collective-permute-start.5) | collective-permute-done | bytes 262176 | tf_op jit(solution)/shard_map/ppermute | solution.py:514
  40.1 2.4 %collective-permute-start.35 = (bf16[256,512]{1,0:T(8,128)(2,1)S(1)}, bf16[256,512]{1,0:T(8,128)(2,1)S(1)}, u32[]{:S(2)}, u32[]{:S(2)}) collective-permute-start(bf16[256,512]{1,0:T(8,128)(2,1)S(1)} %get-tuple-element.39.refs_25_.refs_0_), channel_id=1, source_target_pairs={{0,8},{1,9},{2,10},{3,11},{4,12},{5,13},{6,14},{7,15},{8,0},{9,1},... | collective-permute-start | bytes 786440 | tf_op jit(solution)/shard_map/ppermute | solution.py:514
  42.5 2.8 %collective-permute-done.15.refs_11_ = bf16[256,384]{1,0:T(8,128)(2,1)S(1)} collective-permute-done((bf16[256,384]{1,0:T(8,128)(2,1)S(1)}, bf16[256,384]{1,0:T(8,128)(2,1)S(1)}, u32[]{:S(2)}, u32[]{:S(2)}) %collective-permute-start.15) | collective-permute-done | bytes 196640 | tf_op jit(solution)/shard_map/ppermute | solution.py:514
  45.3 2.0 %collective-permute-start.34 = (bf16[256,512]{1,0:T(8,128)(2,1)S(1)}, bf16[256,512]{1,0:T(8,128)(2,1)S(1)}, u32[]{:S(2)}, u32[]{:S(2)}) collective-permute-start(bf16[256,512]{1,0:T(8,128)(2,1)S(1)} %get-tuple-element.39.refs_25_.refs_0_), channel_id=1, source_target_pairs={{0,4},{1,5},{2,6},{3,7},{4,0},{5,1},{6,2},{7,3},{8,12},{9,13},{10,... | collective-permute-start | bytes 786440 | tf_op jit(solution)/shard_map/ppermute | solution.py:514
  47.7 8.9 %collective-permute-done.35.refs_27_.refs_2_ = bf16[256,512]{1,0:T(8,128)(2,1)S(1)} collective-permute-done((bf16[256,512]{1,0:T(8,128)(2,1)S(1)}, bf16[256,512]{1,0:T(8,128)(2,1)S(1)}, u32[]{:S(2)}, u32[]{:S(2)}) %collective-permute-start.35) | collective-permute-done | bytes 262176 | tf_op jit(solution)/shard_map/ppermute | solution.py:514
  56.6 5.3 %collective-permute-done.16.refs_12_ = bf16[256,384]{1,0:T(8,128)(2,1)S(1)} collective-permute-done((bf16[256,384]{1,0:T(8,128)(2,1)S(1)}, bf16[256,384]{1,0:T(8,128)(2,1)S(1)}, u32[]{:S(2)}, u32[]{:S(2)}) %collective-permute-start.16) | collective-permute-done | bytes 196640 | tf_op jit(solution)/shard_map/ppermute | solution.py:514
  61.9 7.6 %shard_map.59.refs_9_ = bf16[1024,128]{1,0:T(8,128)(2,1)S(1)} custom-call(s32[3]{0:T(128)S(1)} %compare_select_fusion.1.refs_0_, bf16[128,1024]{1,0:T(8,128)(2,1)S(1)} %shard_map.56.refs_1_, bf16[128,1024]{1,0:T(8,128)(2,1)S(1)} %collective-permute-done.3.refs_2_, bf16[128,1024]{1,0:T(8,128)(2,1)S(1)} %collective-permute-done.4.refs_3_, ...), custom_call_target="tpu_custom_call" | custom-call | flops 10000000000 | bytes 2883590 | tf_op jit(solution)/shard_map/pallas_call | solution.py:519
  70.5 2.0 %collective-permute-start.26 = (bf16[64,1024]{1,0:T(8,128)(2,1)S(1)}, bf16[64,1024]{1,0:T(8,128)(2,1)S(1)}, u32[]{:S(2)}, u32[]{:S(2)}) collective-permute-start(bf16[64,1024]{1,0:T(8,128)(2,1)S(1)} %collective-permute-done.25.refs_2_), channel_id=1, source_target_pairs={{0,4},{1,5},{2,6},{3,7},{4,0},{5,1},{6,2},{7,3},{8,12},{9,13},{10,... | collective-permute-start | bytes 393224 | tf_op jit(solution)/shard_map/ppermute | solution.py:514
  72.5 4.3 %collective-permute-done.24.refs_1_ = bf16[64,1024]{1,0:T(8,128)(2,1)S(1)} collective-permute-done((bf16[64,1024]{1,0:T(8,128)(2,1)S(1)}, bf16[64,1024]{1,0:T(8,128)(2,1)S(1)}, u32[]{:S(2)}, u32[]{:S(2)}) %collective-permute-start.24) | collective-permute-done | bytes 131104 | tf_op jit(solution)/shard_map/ppermute | solution.py:514
  78.4 1.8 %collective-permute-start.19 = (bf16[1024,128]{1,0:T(8,128)(2,1)S(1)}, bf16[1024,128]{1,0:T(8,128)(2,1)S(1)}, u32[]{:S(2)}, u32[]{:S(2)}) collective-permute-start(bf16[1024,128]{1,0:T(8,128)(2,1)S(1)} %shard_map.59.refs_9_), channel_id=1, source_target_pairs={{0,18},{1,19},{2,16},{3,17},{4,22},{5,23},{6,20},{7,21},{8,26},{9,... | collective-permute-start | bytes 786440 | tf_op jit(solution)/shard_map/ppermute | solution.py:514
  82.0 1.8 %collective-permute-start.29 = (bf16[256,1024]{1,0:T(8,128)(2,1)S(1)}, bf16[256,1024]{1,0:T(8,128)(2,1)S(1)}, u32[]{:S(2)}, u32[]{:S(2)}) collective-permute-start(bf16[256,1024]{1,0:T(8,128)(2,1)S(1)} %shard_map.60.refs_17_), channel_id=1, source_target_pairs={{0,18},{1,19},{2,16},{3,17},{4,22},{5,23},{6,20},{7,21},{8,26},{9,... | collective-permute-start | bytes 1572872 | tf_op jit(solution)/shard_map/ppermute | solution.py:514
  83.7 2.3 %collective-permute-done.18.refs_11_ = bf16[1024,128]{1,0:T(8,128)(2,1)S(1)} collective-permute-done((bf16[1024,128]{1,0:T(8,128)(2,1)S(1)}, bf16[1024,128]{1,0:T(8,128)(2,1)S(1)}, u32[]{:S(2)}, u32[]{:S(2)}) %collective-permute-start.18) | collective-permute-done | bytes 262176 | tf_op jit(solution)/shard_map/ppermute | solution.py:514
  86.0 6.1 %collective-permute-done.19.refs_12_ = bf16[1024,128]{1,0:T(8,128)(2,1)S(1)} collective-permute-done((bf16[1024,128]{1,0:T(8,128)(2,1)S(1)}, bf16[1024,128]{1,0:T(8,128)(2,1)S(1)}, u32[]{:S(2)}, u32[]{:S(2)}) %collective-permute-start.19) | collective-permute-done | bytes 262176 | tf_op jit(solution)/shard_map/ppermute | solution.py:514
  92.7 6.0 %collective-permute-done.27.refs_18_ = bf16[256,1024]{1,0:T(8,128)(2,1)S(1)} collective-permute-done((bf16[256,1024]{1,0:T(8,128)(2,1)S(1)}, bf16[256,1024]{1,0:T(8,128)(2,1)S(1)}, u32[]{:S(2)}, u32[]{:S(2)}) %collective-permute-start.27) | collective-permute-done | bytes 524320 | tf_op jit(solution)/shard_map/ppermute | solution.py:514
  98.7 4.2 %collective-permute-done.28.refs_19_ = bf16[256,1024]{1,0:T(8,128)(2,1)S(1)} collective-permute-done((bf16[256,1024]{1,0:T(8,128)(2,1)S(1)}, bf16[256,1024]{1,0:T(8,128)(2,1)S(1)}, u32[]{:S(2)}, u32[]{:S(2)}) %collective-permute-start.28) | collective-permute-done | bytes 524320 | tf_op jit(solution)/shard_map/ppermute | solution.py:514
  102.9 8.8 %collective-permute-done.29.refs_20_ = bf16[256,1024]{1,0:T(8,128)(2,1)S(1)} collective-permute-done((bf16[256,1024]{1,0:T(8,128)(2,1)S(1)}, bf16[256,1024]{1,0:T(8,128)(2,1)S(1)}, u32[]{:S(2)}, u32[]{:S(2)}) %collective-permute-start.29) | collective-permute-done | bytes 524320 | tf_op jit(solution)/shard_map/ppermute | solution.py:514
  112.3 1.6 %collective-permute-done.22.refs_15_ = bf16[1024,128]{1,0:T(8,128)(2,1)S(1)} collective-permute-done((bf16[1024,128]{1,0:T(8,128)(2,1)S(1)}, bf16[1024,128]{1,0:T(8,128)(2,1)S(1)}, u32[]{:S(2)}, u32[]{:S(2)}) %collective-permute-start.22) | collective-permute-done | bytes 262176 | tf_op jit(solution)/shard_map/ppermute | solution.py:514
  114.8 12.7 %shard_map.61 = (bf16[512,128]{1,0:T(8,128)(2,1)S(1)}, bf16[512,128]{1,0:T(8,128)(2,1)S(1)}, bf16[256,512]{1,0:T(8,128)(2,1)S(1)}) custom-call(s32[3]{0:T(128)S(1)} %compare_select_fusion.1.refs_0_, bf16[128,1024]{1,0:T(8,128)(2,1)S(1)} %shard_map.56.refs_1_, bf16[128,1024]{1,0:T(8,128)(2,1)S(1)} %collective-permute-done.3.refs_2_, ...), custom_call_target="tpu_custom_call" | custom-call | flops 17999998976 | bytes 9437190 | tf_op jit(solution)/shard_map/pallas_call | solution.py:519
  132.9 2.3 %collective-permute-done.38.refs_2_.refs_4_ = bf16[512,128]{1,0:T(8,128)(2,1)S(1)} collective-permute-done((bf16[512,128]{1,0:T(8,128)(2,1)S(1)}, bf16[512,128]{1,0:T(8,128)(2,1)S(1)}, u32[]{:S(2)}, u32[]{:S(2)}) %collective-permute-start.38) | collective-permute-done | bytes 131104 | tf_op jit(solution)/shard_map/ppermute | solution.py:514
  135.2 1.7 %collective-permute-done.39.refs_3_.refs_5_ = bf16[512,128]{1,0:T(8,128)(2,1)S(1)} collective-permute-done((bf16[512,128]{1,0:T(8,128)(2,1)S(1)}, bf16[512,128]{1,0:T(8,128)(2,1)S(1)}, u32[]{:S(2)}, u32[]{:S(2)}) %collective-permute-start.39) | collective-permute-done | bytes 131104 | tf_op jit(solution)/shard_map/ppermute | solution.py:514
  139.6 1.7 %collective-permute-start.44 = (bf16[64,512]{1,0:T(8,128)(2,1)S(1)}, bf16[64,512]{1,0:T(8,128)(2,1)S(1)}, u32[]{:S(2)}, u32[]{:S(2)}) collective-permute-start(bf16[64,512]{1,0:T(8,128)(2,1)S(1)} %get-tuple-element.44), channel_id=1, source_target_pairs={{0,4},{1,5},{2,6},{3,7},{4,0},{5,1},{6,2},{7,3},{8,12},{9,13},{10,... | collective-permute-start | bytes 196616 | tf_op jit(solution)/shard_map/ppermute | solution.py:514
  142.3 1.8 %collective-permute-start.46 = (bf16[64,512]{1,0:T(8,128)(2,1)S(1)}, bf16[64,512]{1,0:T(8,128)(2,1)S(1)}, u32[]{:S(2)}, u32[]{:S(2)}) collective-permute-start(bf16[64,512]{1,0:T(8,128)(2,1)S(1)} %get-tuple-element.46), channel_id=1, source_target_pairs={{0,12},{1,13},{2,14},{3,15},{4,8},{5,9},{6,10},{7,11},{8,4},{9,5},... | collective-permute-start | bytes 196616 | tf_op jit(solution)/shard_map/ppermute | solution.py:514
  144.1 5.3 %collective-permute-done.45.refs_3_ = bf16[64,512]{1,0:T(8,128)(2,1)S(1)} collective-permute-done((bf16[64,512]{1,0:T(8,128)(2,1)S(1)}, bf16[64,512]{1,0:T(8,128)(2,1)S(1)}, u32[]{:S(2)}, u32[]{:S(2)}) %collective-permute-start.45) | collective-permute-done | bytes 65568 | tf_op jit(solution)/shard_map/ppermute | solution.py:514
  (88 shorter events, 28.3 us)
Async XLA Ops:
  5.8 13.5 %collective-permute-start.10 = (bf16[4,64,384]{2,1,0:T(8,128)(2,1)S(1)}, bf16[4,64,384]{2,1,0:T(8,128)(2,1)S(1)}, u32[]{:S(2)}, u32[]{:S(2)}) collective-permute-start(bf16[4,64,384]{2,1,0:T(8,128)(2,1)S(1)} %get-tuple-element.31), channel_id=1, source_target_pairs={{0,1},{1,0},{2,3},{3,2},{4,5},{5,4},{6,7},{7,6},{8,9},{9,8},{10,11... | collective-permute-start | bytes 589832 | tf_op jit(solution)/shard_map/ppermute | solution.py:514
  9.0 7.7 %collective-permute-start.1 = (bf16[32,1024]{1,0:T(8,128)(2,1)S(1)}, bf16[32,1024]{1,0:T(8,128)(2,1)S(1)}, u32[]{:S(2)}, u32[]{:S(2)}) collective-permute-start(bf16[32,1024]{1,0:T(8,128)(2,1)S(1)} %get-tuple-element.28), channel_id=1, source_target_pairs={{0,8},{1,9},{2,10},{3,11},{4,12},{5,13},{6,14},{7,15},{8,0},{9,1},... | collective-permute-start | bytes 196616 | tf_op jit(solution)/shard_map/ppermute | solution.py:514
  17.7 13.8 %collective-permute-start.3 = (bf16[128,1024]{1,0:T(8,128)(2,1)S(1)}, bf16[128,1024]{1,0:T(8,128)(2,1)S(1)}, u32[]{:S(2)}, u32[]{:S(2)}) collective-permute-start(bf16[128,1024]{1,0:T(8,128)(2,1)S(1)} %shard_map.56.refs_1_), channel_id=1, source_target_pairs={{0,2},{1,3},{2,0},{3,1},{4,6},{5,7},{6,4},{7,5},{8,10},{9,11},{10,... | collective-permute-start | bytes 786440 | tf_op jit(solution)/shard_map/ppermute | solution.py:514
  19.4 9.7 %collective-permute-start.11 = (bf16[128,384]{1,0:T(8,128)(2,1)S(1)}, bf16[128,384]{1,0:T(8,128)(2,1)S(1)}, u32[]{:S(2)}, u32[]{:S(2)}) collective-permute-start(bf16[128,384]{1,0:T(8,128)(2,1)S(1)} %get-tuple-element.34), channel_id=1, source_target_pairs={{0,2},{1,3},{2,0},{3,1},{4,6},{5,7},{6,4},{7,5},{8,10},{9,11},{10,... | collective-permute-start | bytes 294920 | tf_op jit(solution)/shard_map/ppermute | solution.py:514
  19.9 11.5 %collective-permute-start.13 = (bf16[128,384]{1,0:T(8,128)(2,1)S(1)}, bf16[128,384]{1,0:T(8,128)(2,1)S(1)}, u32[]{:S(2)}, u32[]{:S(2)}) collective-permute-start(bf16[128,384]{1,0:T(8,128)(2,1)S(1)} %get-tuple-element.36), channel_id=1, source_target_pairs={{0,18},{1,19},{2,16},{3,17},{4,22},{5,23},{6,20},{7,21},{8,26},{9,... | collective-permute-start | bytes 294920 | tf_op jit(solution)/shard_map/ppermute | solution.py:514
  22.4 9.6 %collective-permute-start.12 = (bf16[128,896]{1,0:T(8,128)(2,1)S(1)}, bf16[128,896]{1,0:T(8,128)(2,1)S(1)}, u32[]{:S(2)}, u32[]{:S(2)}) collective-permute-start(bf16[128,896]{1,0:T(8,128)(2,1)S(1)} %get-tuple-element.35), channel_id=1, source_target_pairs={{0,16},{1,17},{2,18},{3,19},{4,20},{5,21},{6,22},{7,23},{8,24},{9,... | collective-permute-start | bytes 688136 | tf_op jit(solution)/shard_map/ppermute | solution.py:514
  22.9 14.2 %collective-permute-start.4 = (bf16[128,1024]{1,0:T(8,128)(2,1)S(1)}, bf16[128,1024]{1,0:T(8,128)(2,1)S(1)}, u32[]{:S(2)}, u32[]{:S(2)}) collective-permute-start(bf16[128,1024]{1,0:T(8,128)(2,1)S(1)} %shard_map.56.refs_1_), channel_id=1, source_target_pairs={{0,16},{1,17},{2,18},{3,19},{4,20},{5,21},{6,22},{7,23},{8,24},{9,... | collective-permute-start | bytes 786440 | tf_op jit(solution)/shard_map/ppermute | solution.py:514
  29.0 11.1 %collective-permute-start.5 = (bf16[128,1024]{1,0:T(8,128)(2,1)S(1)}, bf16[128,1024]{1,0:T(8,128)(2,1)S(1)}, u32[]{:S(2)}, u32[]{:S(2)}) collective-permute-start(bf16[128,1024]{1,0:T(8,128)(2,1)S(1)} %shard_map.56.refs_1_), channel_id=1, source_target_pairs={{0,18},{1,19},{2,16},{3,17},{4,22},{5,23},{6,20},{7,21},{8,26},{9,... | collective-permute-start | bytes 786440 | tf_op jit(solution)/shard_map/ppermute | solution.py:514
  31.5 8.6 %collective-permute-start.6 = (bf16[128,1024]{1,0:T(8,128)(2,1)S(1)}, bf16[128,1024]{1,0:T(8,128)(2,1)S(1)}, u32[]{:S(2)}, u32[]{:S(2)}) collective-permute-start(bf16[128,1024]{1,0:T(8,128)(2,1)S(1)} %shard_map.56.refs_1_), channel_id=1, source_target_pairs={{0,1},{1,0},{2,3},{3,2},{4,5},{5,4},{6,7},{7,6},{8,9},{9,8},{10,11... | collective-permute-start | bytes 786440 | tf_op jit(solution)/shard_map/ppermute | solution.py:514
  31.5 11.0 %collective-permute-start.7 = (bf16[128,1024]{1,0:T(8,128)(2,1)S(1)}, bf16[128,1024]{1,0:T(8,128)(2,1)S(1)}, u32[]{:S(2)}, u32[]{:S(2)}) collective-permute-start(bf16[128,1024]{1,0:T(8,128)(2,1)S(1)} %collective-permute-done.3.refs_2_), channel_id=1, source_target_pairs={{0,1},{1,0},{2,3},{3,2},{4,5},{5,4},{6,7},{7,6},{8,9},{9,8},{10,11... | collective-permute-start | bytes 786440 | tf_op jit(solution)/shard_map/ppermute | solution.py:514
  32.6 12.6 %collective-permute-start.15 = (bf16[256,384]{1,0:T(8,128)(2,1)S(1)}, bf16[256,384]{1,0:T(8,128)(2,1)S(1)}, u32[]{:S(2)}, u32[]{:S(2)}) collective-permute-start(bf16[256,384]{1,0:T(8,128)(2,1)S(1)} %get-tuple-element.37.refs_9_), channel_id=1, source_target_pairs={{0,8},{1,9},{2,10},{3,11},{4,12},{5,13},{6,14},{7,15},{8,0},{9,1},... | collective-permute-start | bytes 589832 | tf_op jit(solution)/shard_map/ppermute | solution.py:514
  37.1 8.2 %collective-permute-start.8 = (bf16[128,1024]{1,0:T(8,128)(2,1)S(1)}, bf16[128,1024]{1,0:T(8,128)(2,1)S(1)}, u32[]{:S(2)}, u32[]{:S(2)}) collective-permute-start(bf16[128,1024]{1,0:T(8,128)(2,1)S(1)} %collective-permute-done.4.refs_3_), channel_id=1, source_target_pairs={{0,1},{1,0},{2,3},{3,2},{4,5},{5,4},{6,7},{7,6},{8,9},{9,8},{10,11... | collective-permute-start | bytes 786440 | tf_op jit(solution)/shard_map/ppermute | solution.py:514
  40.1 7.2 %collective-permute-start.9 = (bf16[128,1024]{1,0:T(8,128)(2,1)S(1)}, bf16[128,1024]{1,0:T(8,128)(2,1)S(1)}, u32[]{:S(2)}, u32[]{:S(2)}) collective-permute-start(bf16[128,1024]{1,0:T(8,128)(2,1)S(1)} %collective-permute-done.5.refs_4_), channel_id=1, source_target_pairs={{0,1},{1,0},{2,3},{3,2},{4,5},{5,4},{6,7},{7,6},{8,9},{9,8},{10,11... | collective-permute-start | bytes 786440 | tf_op jit(solution)/shard_map/ppermute | solution.py:514
  40.1 16.5 %collective-permute-start.35 = (bf16[256,512]{1,0:T(8,128)(2,1)S(1)}, bf16[256,512]{1,0:T(8,128)(2,1)S(1)}, u32[]{:S(2)}, u32[]{:S(2)}) collective-permute-start(bf16[256,512]{1,0:T(8,128)(2,1)S(1)} %get-tuple-element.39.refs_25_.refs_0_), channel_id=1, source_target_pairs={{0,8},{1,9},{2,10},{3,11},{4,12},{5,13},{6,14},{7,15},{8,0},{9,1},... | collective-permute-start | bytes 786440 | tf_op jit(solution)/shard_map/ppermute | solution.py:514
  42.5 14.1 %collective-permute-start.14 = (bf16[256,384]{1,0:T(8,128)(2,1)S(1)}, bf16[256,384]{1,0:T(8,128)(2,1)S(1)}, u32[]{:S(2)}, u32[]{:S(2)}) collective-permute-start(bf16[256,384]{1,0:T(8,128)(2,1)S(1)} %get-tuple-element.37.refs_9_), channel_id=1, source_target_pairs={{0,4},{1,5},{2,6},{3,7},{4,0},{5,1},{6,2},{7,3},{8,12},{9,13},{10,... | collective-permute-start | bytes 589832 | tf_op jit(solution)/shard_map/ppermute | solution.py:514
  45.2 16.6 %collective-permute-start.16 = (bf16[256,384]{1,0:T(8,128)(2,1)S(1)}, bf16[256,384]{1,0:T(8,128)(2,1)S(1)}, u32[]{:S(2)}, u32[]{:S(2)}) collective-permute-start(bf16[256,384]{1,0:T(8,128)(2,1)S(1)} %collective-permute-done.15.refs_11_), channel_id=1, source_target_pairs={{0,4},{1,5},{2,6},{3,7},{4,0},{5,1},{6,2},{7,3},{8,12},{9,13},{10,... | collective-permute-start | bytes 589832 | tf_op jit(solution)/shard_map/ppermute | solution.py:514
  45.3 35.0 %collective-permute-start.34 = (bf16[256,512]{1,0:T(8,128)(2,1)S(1)}, bf16[256,512]{1,0:T(8,128)(2,1)S(1)}, u32[]{:S(2)}, u32[]{:S(2)}) collective-permute-start(bf16[256,512]{1,0:T(8,128)(2,1)S(1)} %get-tuple-element.39.refs_25_.refs_0_), channel_id=1, source_target_pairs={{0,4},{1,5},{2,6},{3,7},{4,0},{5,1},{6,2},{7,3},{8,12},{9,13},{10,... | collective-permute-start | bytes 786440 | tf_op jit(solution)/shard_map/ppermute | solution.py:514
  47.3 23.2 %collective-permute-start.25 = (bf16[64,1024]{1,0:T(8,128)(2,1)S(1)}, bf16[64,1024]{1,0:T(8,128)(2,1)S(1)}, u32[]{:S(2)}, u32[]{:S(2)}) collective-permute-start(bf16[64,1024]{1,0:T(8,128)(2,1)S(1)} %get-tuple-element.38.refs_0_), channel_id=1, source_target_pairs={{0,8},{1,9},{2,10},{3,11},{4,12},{5,13},{6,14},{7,15},{8,0},{9,1},... | collective-permute-start | bytes 393224 | tf_op jit(solution)/shard_map/ppermute | solution.py:514
  56.6 24.2 %collective-permute-start.36 = (bf16[256,512]{1,0:T(8,128)(2,1)S(1)}, bf16[256,512]{1,0:T(8,128)(2,1)S(1)}, u32[]{:S(2)}, u32[]{:S(2)}) collective-permute-start(bf16[256,512]{1,0:T(8,128)(2,1)S(1)} %collective-permute-done.35.refs_27_.refs_2_), channel_id=1, source_target_pairs={{0,4},{1,5},{2,6},{3,7},{4,0},{5,1},{6,2},{7,3},{8,12},{9,13},{10,... | collective-permute-start | bytes 786440 | tf_op jit(solution)/shard_map/ppermute | solution.py:514
  69.5 12.5 %collective-permute-start.17 = (bf16[1024,128]{1,0:T(8,128)(2,1)S(1)}, bf16[1024,128]{1,0:T(8,128)(2,1)S(1)}, u32[]{:S(2)}, u32[]{:S(2)}) collective-permute-start(bf16[1024,128]{1,0:T(8,128)(2,1)S(1)} %shard_map.59.refs_9_), channel_id=1, source_target_pairs={{0,2},{1,3},{2,0},{3,1},{4,6},{5,7},{6,4},{7,5},{8,10},{9,11},{10,... | collective-permute-start | bytes 786440 | tf_op jit(solution)/shard_map/ppermute | solution.py:514
  70.5 7.9 %collective-permute-start.26 = (bf16[64,1024]{1,0:T(8,128)(2,1)S(1)}, bf16[64,1024]{1,0:T(8,128)(2,1)S(1)}, u32[]{:S(2)}, u32[]{:S(2)}) collective-permute-start(bf16[64,1024]{1,0:T(8,128)(2,1)S(1)} %collective-permute-done.25.refs_2_), channel_id=1, source_target_pairs={{0,4},{1,5},{2,6},{3,7},{4,0},{5,1},{6,2},{7,3},{8,12},{9,13},{10,... | collective-permute-start | bytes 393224 | tf_op jit(solution)/shard_map/ppermute | solution.py:514
  76.9 9.2 %collective-permute-start.18 = (bf16[1024,128]{1,0:T(8,128)(2,1)S(1)}, bf16[1024,128]{1,0:T(8,128)(2,1)S(1)}, u32[]{:S(2)}, u32[]{:S(2)}) collective-permute-start(bf16[1024,128]{1,0:T(8,128)(2,1)S(1)} %shard_map.59.refs_9_), channel_id=1, source_target_pairs={{0,16},{1,17},{2,18},{3,19},{4,20},{5,21},{6,22},{7,23},{8,24},{9,... | collective-permute-start | bytes 786440 | tf_op jit(solution)/shard_map/ppermute | solution.py:514
  78.4 13.7 %collective-permute-start.19 = (bf16[1024,128]{1,0:T(8,128)(2,1)S(1)}, bf16[1024,128]{1,0:T(8,128)(2,1)S(1)}, u32[]{:S(2)}, u32[]{:S(2)}) collective-permute-start(bf16[1024,128]{1,0:T(8,128)(2,1)S(1)} %shard_map.59.refs_9_), channel_id=1, source_target_pairs={{0,18},{1,19},{2,16},{3,17},{4,22},{5,23},{6,20},{7,21},{8,26},{9,... | collective-permute-start | bytes 786440 | tf_op jit(solution)/shard_map/ppermute | solution.py:514
  80.2 18.4 %collective-permute-start.27 = (bf16[256,1024]{1,0:T(8,128)(2,1)S(1)}, bf16[256,1024]{1,0:T(8,128)(2,1)S(1)}, u32[]{:S(2)}, u32[]{:S(2)}) collective-permute-start(bf16[256,1024]{1,0:T(8,128)(2,1)S(1)} %shard_map.60.refs_17_), channel_id=1, source_target_pairs={{0,2},{1,3},{2,0},{3,1},{4,6},{5,7},{6,4},{7,5},{8,10},{9,11},{10,... | collective-permute-start | bytes 1572872 | tf_op jit(solution)/shard_map/ppermute | solution.py:514
  80.8 22.1 %collective-permute-start.28 = (bf16[256,1024]{1,0:T(8,128)(2,1)S(1)}, bf16[256,1024]{1,0:T(8,128)(2,1)S(1)}, u32[]{:S(2)}, u32[]{:S(2)}) collective-permute-start(bf16[256,1024]{1,0:T(8,128)(2,1)S(1)} %shard_map.60.refs_17_), channel_id=1, source_target_pairs={{0,16},{1,17},{2,18},{3,19},{4,20},{5,21},{6,22},{7,23},{8,24},{9,... | collective-permute-start | bytes 1572872 | tf_op jit(solution)/shard_map/ppermute | solution.py:514
  82.0 29.7 %collective-permute-start.29 = (bf16[256,1024]{1,0:T(8,128)(2,1)S(1)}, bf16[256,1024]{1,0:T(8,128)(2,1)S(1)}, u32[]{:S(2)}, u32[]{:S(2)}) collective-permute-start(bf16[256,1024]{1,0:T(8,128)(2,1)S(1)} %shard_map.60.refs_17_), channel_id=1, source_target_pairs={{0,18},{1,19},{2,16},{3,17},{4,22},{5,23},{6,20},{7,21},{8,26},{9,... | collective-permute-start | bytes 1572872 | tf_op jit(solution)/shard_map/ppermute | solution.py:514
  92.1 19.5 %collective-permute-start.30 = (bf16[256,1024]{1,0:T(8,128)(2,1)S(1)}, bf16[256,1024]{1,0:T(8,128)(2,1)S(1)}, u32[]{:S(2)}, u32[]{:S(2)}) collective-permute-start(bf16[256,1024]{1,0:T(8,128)(2,1)S(1)} %shard_map.60.refs_17_), channel_id=1, source_target_pairs={{0,1},{1,0},{2,3},{3,2},{4,5},{5,4},{6,7},{7,6},{8,9},{9,8},{10,11... | collective-permute-start | bytes 1572872 | tf_op jit(solution)/shard_map/ppermute | solution.py:514
  92.2 20.0 %collective-permute-start.21 = (bf16[1024,128]{1,0:T(8,128)(2,1)S(1)}, bf16[1024,128]{1,0:T(8,128)(2,1)S(1)}, u32[]{:S(2)}, u32[]{:S(2)}) collective-permute-start(bf16[1024,128]{1,0:T(8,128)(2,1)S(1)} %collective-permute-done.17.refs_10_), channel_id=1, source_target_pairs={{0,1},{1,0},{2,3},{3,2},{4,5},{5,4},{6,7},{7,6},{8,9},{9,8},{10,11... | collective-permute-start | bytes 786440 | tf_op jit(solution)/shard_map/ppermute | solution.py:514
  98.7 16.1 %collective-permute-start.31 = (bf16[256,1024]{1,0:T(8,128)(2,1)S(1)}, bf16[256,1024]{1,0:T(8,128)(2,1)S(1)}, u32[]{:S(2)}, u32[]{:S(2)}) collective-permute-start(bf16[256,1024]{1,0:T(8,128)(2,1)S(1)} %collective-permute-done.27.refs_18_), channel_id=1, source_target_pairs={{0,1},{1,0},{2,3},{3,2},{4,5},{5,4},{6,7},{7,6},{8,9},{9,8},{10,11... | collective-permute-start | bytes 1572872 | tf_op jit(solution)/shard_map/ppermute | solution.py:514
  102.9 11.9 %collective-permute-start.32 = (bf16[256,1024]{1,0:T(8,128)(2,1)S(1)}, bf16[256,1024]{1,0:T(8,128)(2,1)S(1)}, u32[]{:S(2)}, u32[]{:S(2)}) collective-permute-start(bf16[256,1024]{1,0:T(8,128)(2,1)S(1)} %collective-permute-done.28.refs_19_), channel_id=1, source_target_pairs={{0,1},{1,0},{2,3},{3,2},{4,5},{5,4},{6,7},{7,6},{8,9},{9,8},{10,11... | collective-permute-start | bytes 1572872 | tf_op jit(solution)/shard_map/ppermute | solution.py:514
  114.0 17.1 %collective-permute-start.41 = (bf16[256,512]{1,0:T(8,128)(2,1)S(1)}, bf16[256,512]{1,0:T(8,128)(2,1)S(1)}, u32[]{:S(2)}, u32[]{:S(2)}) collective-permute-start(bf16[256,512]{1,0:T(8,128)(2,1)S(1)} %shard_map.63.refs_7_), channel_id=1, source_target_pairs={{0,2},{1,3},{2,0},{3,1},{4,6},{5,7},{6,4},{7,5},{8,10},{9,11},{10,... | collective-permute-start | bytes 786440 | tf_op jit(solution)/shard_map/ppermute | solution.py:514
  141.3 8.1 %collective-permute-start.45 = (bf16[64,512]{1,0:T(8,128)(2,1)S(1)}, bf16[64,512]{1,0:T(8,128)(2,1)S(1)}, u32[]{:S(2)}, u32[]{:S(2)}) collective-permute-start(bf16[64,512]{1,0:T(8,128)(2,1)S(1)} %get-tuple-element.45), channel_id=1, source_target_pairs={{0,8},{1,9},{2,10},{3,11},{4,12},{5,13},{6,14},{7,15},{8,0},{9,1},... | collective-permute-start | bytes 196616 | tf_op jit(solution)/shard_map/ppermute | solution.py:514
  (22 other events, 105.2 us)

commit v3 on v2

--- a/solution.py
+++ b/solution.py
@@ -299,21 +299,34 @@
         copy.wait()
 
 
-def pair_kernel(plan, keep, given, cross, *outs):
+def pair_kernel(plan, keep, given, *outs):
     rows = plan.w_rows
-    for chip_no, (out, chip) in enumerate(zip(outs, plan.chips)):
-        out[0:rows, 0 : 3 * plan.cols] = keep[chip_no]
-        out[rows:, 0 : 3 * plan.cols] = given[chip_no]
-        if chip == (1, 0):
-            out[:, 3 * plan.cols :] = cross[...]
-
-
-def sort_kernel(plan, where, proj_weight, merge_weight, *refs):
+    for chip_no, out in enumerate(outs):
+        out[0:rows, :] = keep[chip_no]
+        out[rows:, :] = given[chip_no]
+
+
+def merge_kernel(plan, where, proj_weight, merge_weight, crossed, mats, last):
+    rows, width = (plan.w_rows, plan.half_cols)
+    for section in range(plan.sections):
+
+        @pl.when(where[0] == section)
+        def _():
+            lanes = slice(section * width, (section + 1) * width)
+            mine = proj_weight[0, :, lanes]
+            others = crossed[0:rows, :]
+            mats[:, 0:width] = mine if section == 0 else others
+            last[...] = others if section == 0 else mine
+            total = merge_weight[0, :, lanes].astype(jnp.float32)
+            total = total + crossed[rows:, :].astype(jnp.float32)
+            mats[:, width:] = total.astype(jnp.bfloat16)
+
+
+def sort_kernel(plan, where, last, *refs):
     count = len(plan.chips)
-    pieces, (rows_a, rows_b, mats) = (refs[:count], refs[count:])
-    rows, width, cols = (plan.w_rows, plan.half_cols, 3 * plan.cols)
-    lone = width // plan.inner
-    crossed = pieces[plan.chips.index((1, 0))]
+    pieces, (rows_a, rows_b) = (refs[:count], refs[count:])
+    rows, cols = (plan.w_rows, 3 * plan.cols)
+    lone = plan.half_cols // plan.inner
     for section in range(plan.sections):
 
         @pl.when(where[0] == section)
@@ -321,17 +334,10 @@
             outs = (rows_a, rows_b)
             for piece, (mx, mi) in zip(pieces, plan.chips):
                 part = slice(mi * rows, (mi + 2) * rows)
-                outs[section ^ mx][part, 0:cols] = piece[:, 0:cols]
-            lanes = slice(section * width, (section + 1) * width)
-            mine = proj_weight[0, :, lanes]
-            others = crossed[0:rows, cols:]
-            mats[:, 0:width] = mine if section == 0 else others
-            last = others if section == 0 else mine
-            for mi in range(plan.inner):
-                rows_b[mi * rows : (mi + 1) * rows, cols:] = last[:, mi * lone : (mi + 1) * lone]
-            total = merge_weight[0, :, lanes].astype(jnp.float32)
-            total = total + crossed[rows:, cols:].astype(jnp.float32)
-            mats[:, width:] = total.astype(jnp.bfloat16)
+                outs[section ^ mx][part, 0:cols] = piece[...]
+
+    for mi in range(plan.inner):
+        rows_b[mi * rows : (mi + 1) * rows, cols:] = last[:, mi * lone : (mi + 1) * lone]
 
 
 def last_kernel(plan, *refs):
@@ -549,6 +555,10 @@
     def core_gather(pieces):
         return pieces + [swap(piece, plan.mask(mi=1)) for piece in pieces]
 
+    latents, qkv_weight, proj_weight, merge_weight = (
+        pltpu.with_memory_space_constraint(value, pltpu.HBM)
+        for value in (latents, qkv_weight, proj_weight, merge_weight)
+    )
     prepared = call(
         lambda *refs: prepare_kernel(plan, *refs),
         [(plan.half, features)] * windows
@@ -564,14 +574,12 @@
     )
     shares, (keep, give, cross) = (prepared[:windows], prepared[windows:])
     given = swap(give, plan.mask(mi=1))
+    crossed = swap(cross, plan.mask(mx=1))
     shares = [shares[0]] + [swap(shares[mz], plan.mask(mz=mz)) for mz in range(1, windows)]
     outgoing = call(
         lambda *refs: pair_kernel(plan, *refs),
-        [
-            (2 * plan.w_rows, 3 * cols + (width if chip == (1, 0) else 0))
-            for chip in plan.chips
-        ],
-        [keep, given, cross],
+        [(2 * plan.w_rows, 3 * cols)] * len(plan.chips),
+        [keep, given],
         limit=8,
     )
     incoming = [outgoing[0]] + [
@@ -581,16 +589,23 @@
     ]
     hidden = chip_gather(stack(shares))
     hidden = core_gather(hidden)
-    rows_a, rows_b, mats = call(
+    mats, last = call(
+        lambda *refs: merge_kernel(plan, *refs),
+        [(plan.w_rows, 2 * width), (plan.w_rows, width)],
+        [where, proj_weight, merge_weight, crossed],
+        (),
+        [smem] + [vmem] * 3,
+        limit=8,
+    )
+    rows_a, rows_b = call(
         lambda *refs: sort_kernel(plan, *refs),
         [
             (plan.group, 3 * cols),
             (plan.group, 3 * cols + width // inner),
-            (plan.w_rows, 2 * width),
         ],
-        [where, proj_weight, merge_weight] + incoming,
+        [where, last] + incoming,
         (),
-        [smem] + [vmem] * (2 + len(incoming)),
+        [smem] + [vmem] * (1 + len(incoming)),
         limit=8,
     )
     mats = z_gather(mats)

time: 151 us -> 142 us (0.940)
  waiting for transfers between devices: 78.8 us -> 68.9 us
  local copies, waits for them, and re-layouts: 4.53 us -> 0.68 us
  starting transfers between devices: 42.4 us -> 46 us
    ppermute x47 -> x48, waiting for transfers between devices: 78.8 us -> 68.9 us  [swap(): return lax.ppermute(value, ('section', 'seq'), pairs)]
    unnamed x14 -> x2, local copies, waits for them, and re-layouts: 4.53 us -> 0.68 us
    ppermute x47 -> x48, starting transfers between devices: 42.4 us -> 46 us  [swap(): return lax.ppermute(value, ('section', 'seq'), pairs)]
    pallas_call x11 -> x12, Pallas kernels: 24.9 us -> 26.3 us  [call(): pl.pallas_call(kernel, out_shape=shapes, in_specs=specs or [vmem] * len(i...]
  transfers between devices with their start and end apart: 47 -> 48, of which waited for: 22 -> 15; matrix products, arithmetic and copies ran while one was open for 0% -> 0% of each run, Pallas kernels for 14% -> 16%
where the time goes in v3:
time: 142 us
  waiting for transfers between devices  68.9 us (49%)
  starting transfers between devices  46 us (32%)
  Pallas kernels  26.3 us (19%)
    ppermute x48, waiting for transfers between devices, swap(): return lax.ppermute(value, ('section', 'seq'), pairs)  68.9 us
    ppermute x48, starting transfers between devices, swap(): return lax.ppermute(value, ('section', 'seq'), pairs)  46 us
    pallas_call x12, Pallas kernels, call(): pl.pallas_call(kernel, out_shape=shapes, in_specs=specs or [vmem] * len(i...  26.3 us
  transfers between devices with their start and end apart: 48, of which 15 were waited for; matrix products, arithmetic and copies ran while one was open for 0% of the time, Pallas kernels for 16%

profile of v3, /device:TPU:0, one launch (start us, length us, event | category | flops | bytes accessed | tf_op | source)
XLA Modules:
  0.0 142.0 jit_solution(7244687474728069767)
XLA Ops:
  0.7 1.8 %shard_map.55 = (bf16[32,1024]{1,0:T(8,128)(2,1)S(1)}, bf16[32,1024]{1,0:T(8,128)(2,1)S(1)}, bf16[32,1024]{1,0:T(8,128)(2,1)S(1)}, bf16[32,1024]{1,0:T(8,128)(2,...) custom-call(s32[3]{0:T(128)S(1)} %compare_select_fusion.1.refs_0_, ...), custom_call_target="tpu_custom_call" | custom-call | bytes 1181702 | tf_op jit(solution)/shard_map/pallas_call | solution.py:525
  3.0 2.6 %collective-permute-start.10 = (bf16[128,512]{1,0:T(8,128)(2,1)S(1)}, bf16[128,512]{1,0:T(8,128)(2,1)S(1)}, u32[]{:S(2)}, u32[]{:S(2)}) collective-permute-start(bf16[128,512]{1,0:T(8,128)(2,1)S(1)} %get-tuple-element.31), channel_id=1, source_target_pairs={{0,16},{1,17},{2,18},{3,19},{4,20},{5,21},{6,22},{7,23},{8,24},{9,... | collective-permute-start | bytes 393224 | tf_op jit(solution)/shard_map/ppermute | solution.py:520
  5.6 1.6 %collective-permute-start = (bf16[32,1024]{1,0:T(8,128)(2,1)S(1)}, bf16[32,1024]{1,0:T(8,128)(2,1)S(1)}, u32[]{:S(2)}, u32[]{:S(2)}) collective-permute-start(bf16[32,1024]{1,0:T(8,128)(2,1)S(1)} %get-tuple-element.28), channel_id=1, source_target_pairs={{0,4},{1,5},{2,6},{3,7},{4,0},{5,1},{6,2},{7,3},{8,12},{9,13},{10,... | collective-permute-start | bytes 196616 | tf_op jit(solution)/shard_map/ppermute | solution.py:520
  7.2 2.6 %collective-permute-start.1 = (bf16[32,1024]{1,0:T(8,128)(2,1)S(1)}, bf16[32,1024]{1,0:T(8,128)(2,1)S(1)}, u32[]{:S(2)}, u32[]{:S(2)}) collective-permute-start(bf16[32,1024]{1,0:T(8,128)(2,1)S(1)} %get-tuple-element.29), channel_id=1, source_target_pairs={{0,8},{1,9},{2,10},{3,11},{4,12},{5,13},{6,14},{7,15},{8,0},{9,1},... | collective-permute-start | bytes 196616 | tf_op jit(solution)/shard_map/ppermute | solution.py:520
  10.8 1.8 %collective-permute-start.25 = (bf16[64,1024]{1,0:T(8,128)(2,1)S(1)}, bf16[64,1024]{1,0:T(8,128)(2,1)S(1)}, u32[]{:S(2)}, u32[]{:S(2)}) collective-permute-start(bf16[64,1024]{1,0:T(8,128)(2,1)S(1)} %get-tuple-element.40.refs_0_), channel_id=1, source_target_pairs={{0,4},{1,5},{2,6},{3,7},{4,0},{5,1},{6,2},{7,3},{8,12},{9,13},{10,... | collective-permute-start | bytes 393224 | tf_op jit(solution)/shard_map/ppermute | solution.py:520
  12.6 2.5 %collective-permute-start.2 = (bf16[32,1024]{1,0:T(8,128)(2,1)S(1)}, bf16[32,1024]{1,0:T(8,128)(2,1)S(1)}, u32[]{:S(2)}, u32[]{:S(2)}) collective-permute-start(bf16[32,1024]{1,0:T(8,128)(2,1)S(1)} %get-tuple-element.30), channel_id=1, source_target_pairs={{0,12},{1,13},{2,14},{3,15},{4,8},{5,9},{6,10},{7,11},{8,4},{9,5},... | collective-permute-start | bytes 196616 | tf_op jit(solution)/shard_map/ppermute | solution.py:520
  15.1 1.6 %collective-permute-start.12 = (bf16[128,384]{1,0:T(8,128)(2,1)S(1)}, bf16[128,384]{1,0:T(8,128)(2,1)S(1)}, u32[]{:S(2)}, u32[]{:S(2)}) collective-permute-start(bf16[128,384]{1,0:T(8,128)(2,1)S(1)} %get-tuple-element.36), channel_id=1, source_target_pairs={{0,2},{1,3},{2,0},{3,1},{4,6},{5,7},{6,4},{7,5},{8,10},{9,11},{10,... | collective-permute-start | bytes 294920 | tf_op jit(solution)/shard_map/ppermute | solution.py:520
  16.7 2.7 %collective-permute-done.2.refs_3_ = bf16[32,1024]{1,0:T(8,128)(2,1)S(1)} collective-permute-done((bf16[32,1024]{1,0:T(8,128)(2,1)S(1)}, bf16[32,1024]{1,0:T(8,128)(2,1)S(1)}, u32[]{:S(2)}, u32[]{:S(2)}) %collective-permute-start.2) | collective-permute-done | bytes 65568 | tf_op jit(solution)/shard_map/ppermute | solution.py:520
  19.4 1.6 %collective-permute-start.3 = (bf16[128,1024]{1,0:T(8,128)(2,1)S(1)}, bf16[128,1024]{1,0:T(8,128)(2,1)S(1)}, u32[]{:S(2)}, u32[]{:S(2)}) collective-permute-start(bf16[128,1024]{1,0:T(8,128)(2,1)S(1)} %shard_map.56.refs_1_), channel_id=1, source_target_pairs={{0,2},{1,3},{2,0},{3,1},{4,6},{5,7},{6,4},{7,5},{8,10},{9,11},{10,... | collective-permute-start | bytes 786440 | tf_op jit(solution)/shard_map/ppermute | solution.py:520
  21.0 1.5 %collective-permute-start.4 = (bf16[128,1024]{1,0:T(8,128)(2,1)S(1)}, bf16[128,1024]{1,0:T(8,128)(2,1)S(1)}, u32[]{:S(2)}, u32[]{:S(2)}) collective-permute-start(bf16[128,1024]{1,0:T(8,128)(2,1)S(1)} %shard_map.56.refs_1_), channel_id=1, source_target_pairs={{0,16},{1,17},{2,18},{3,19},{4,20},{5,21},{6,22},{7,23},{8,24},{9,... | collective-permute-start | bytes 786440 | tf_op jit(solution)/shard_map/ppermute | solution.py:520
  24.5 1.5 %collective-permute-start.14 = (bf16[128,384]{1,0:T(8,128)(2,1)S(1)}, bf16[128,384]{1,0:T(8,128)(2,1)S(1)}, u32[]{:S(2)}, u32[]{:S(2)}) collective-permute-start(bf16[128,384]{1,0:T(8,128)(2,1)S(1)} %get-tuple-element.38), channel_id=1, source_target_pairs={{0,18},{1,19},{2,16},{3,17},{4,22},{5,23},{6,20},{7,21},{8,26},{9,... | collective-permute-start | bytes 294920 | tf_op jit(solution)/shard_map/ppermute | solution.py:520
  26.0 6.3 %collective-permute-done.13.refs_4_ = bf16[128,384]{1,0:T(8,128)(2,1)S(1)} collective-permute-done((bf16[128,384]{1,0:T(8,128)(2,1)S(1)}, bf16[128,384]{1,0:T(8,128)(2,1)S(1)}, u32[]{:S(2)}, u32[]{:S(2)}) %collective-permute-start.13) | collective-permute-done | bytes 98336 | tf_op jit(solution)/shard_map/ppermute | solution.py:520
  33.3 3.9 %collective-permute-done.14.refs_5_ = bf16[128,384]{1,0:T(8,128)(2,1)S(1)} collective-permute-done((bf16[128,384]{1,0:T(8,128)(2,1)S(1)}, bf16[128,384]{1,0:T(8,128)(2,1)S(1)}, u32[]{:S(2)}, u32[]{:S(2)}) %collective-permute-start.14) | collective-permute-done | bytes 98336 | tf_op jit(solution)/shard_map/ppermute | solution.py:520
  38.5 3.4 %collective-permute-start.16 = (bf16[256,384]{1,0:T(8,128)(2,1)S(1)}, bf16[256,384]{1,0:T(8,128)(2,1)S(1)}, u32[]{:S(2)}, u32[]{:S(2)}) collective-permute-start(bf16[256,384]{1,0:T(8,128)(2,1)S(1)} %get-tuple-element.39.refs_9_), channel_id=1, source_target_pairs={{0,8},{1,9},{2,10},{3,11},{4,12},{5,13},{6,14},{7,15},{8,0},{9,1},... | collective-permute-start | bytes 589832 | tf_op jit(solution)/shard_map/ppermute | solution.py:520
  41.9 2.0 %collective-permute-start.27 = (bf16[64,1024]{1,0:T(8,128)(2,1)S(1)}, bf16[64,1024]{1,0:T(8,128)(2,1)S(1)}, u32[]{:S(2)}, u32[]{:S(2)}) collective-permute-start(bf16[64,1024]{1,0:T(8,128)(2,1)S(1)} %collective-permute-done.26.refs_2_), channel_id=1, source_target_pairs={{0,4},{1,5},{2,6},{3,7},{4,0},{5,1},{6,2},{7,3},{8,12},{9,13},{10,... | collective-permute-start | bytes 393224 | tf_op jit(solution)/shard_map/ppermute | solution.py:520
  44.0 19.4 %collective-permute-done.27.refs_3_ = bf16[64,1024]{1,0:T(8,128)(2,1)S(1)} collective-permute-done((bf16[64,1024]{1,0:T(8,128)(2,1)S(1)}, bf16[64,1024]{1,0:T(8,128)(2,1)S(1)}, u32[]{:S(2)}, u32[]{:S(2)}) %collective-permute-start.27) | collective-permute-done | bytes 131104 | tf_op jit(solution)/shard_map/ppermute | solution.py:520
  64.1 1.6 %collective-permute-start.28 = (bf16[256,1024]{1,0:T(8,128)(2,1)S(1)}, bf16[256,1024]{1,0:T(8,128)(2,1)S(1)}, u32[]{:S(2)}, u32[]{:S(2)}) collective-permute-start(bf16[256,1024]{1,0:T(8,128)(2,1)S(1)} %shard_map.61.refs_17_), channel_id=1, source_target_pairs={{0,2},{1,3},{2,0},{3,1},{4,6},{5,7},{6,4},{7,5},{8,10},{9,11},{10,... | collective-permute-start | bytes 1572872 | tf_op jit(solution)/shard_map/ppermute | solution.py:520
  65.7 1.5 %collective-permute-start.29 = (bf16[256,1024]{1,0:T(8,128)(2,1)S(1)}, bf16[256,1024]{1,0:T(8,128)(2,1)S(1)}, u32[]{:S(2)}, u32[]{:S(2)}) collective-permute-start(bf16[256,1024]{1,0:T(8,128)(2,1)S(1)} %shard_map.61.refs_17_), channel_id=1, source_target_pairs={{0,16},{1,17},{2,18},{3,19},{4,20},{5,21},{6,22},{7,23},{8,24},{9,... | collective-permute-start | bytes 1572872 | tf_op jit(solution)/shard_map/ppermute | solution.py:520
  67.9 3.3 %collective-permute-done.17.refs_12_ = bf16[256,384]{1,0:T(8,128)(2,1)S(1)} collective-permute-done((bf16[256,384]{1,0:T(8,128)(2,1)S(1)}, bf16[256,384]{1,0:T(8,128)(2,1)S(1)}, u32[]{:S(2)}, u32[]{:S(2)}) %collective-permute-start.17) | collective-permute-done | bytes 196640 | tf_op jit(solution)/shard_map/ppermute | solution.py:520
  71.5 7.6 %shard_map.60.refs_9_ = bf16[1024,128]{1,0:T(8,128)(2,1)S(1)} custom-call(s32[3]{0:T(128)S(1)} %compare_select_fusion.1.refs_0_, bf16[128,1024]{1,0:T(8,128)(2,1)S(1)} %shard_map.56.refs_1_, bf16[128,1024]{1,0:T(8,128)(2,1)S(1)} %collective-permute-done.3.refs_2_, bf16[128,1024]{1,0:T(8,128)(2,1)S(1)} %collective-permute-done.4.refs_3_, ...), custom_call_target="tpu_custom_call" | custom-call | flops 10000000000 | bytes 2883590 | tf_op jit(solution)/shard_map/pallas_call | solution.py:525
  79.2 1.6 %collective-permute-start.18 = (bf16[1024,128]{1,0:T(8,128)(2,1)S(1)}, bf16[1024,128]{1,0:T(8,128)(2,1)S(1)}, u32[]{:S(2)}, u32[]{:S(2)}) collective-permute-start(bf16[1024,128]{1,0:T(8,128)(2,1)S(1)} %shard_map.60.refs_9_), channel_id=1, source_target_pairs={{0,2},{1,3},{2,0},{3,1},{4,6},{5,7},{6,4},{7,5},{8,10},{9,11},{10,... | collective-permute-start | bytes 786440 | tf_op jit(solution)/shard_map/ppermute | solution.py:520
  80.8 1.5 %collective-permute-start.19 = (bf16[1024,128]{1,0:T(8,128)(2,1)S(1)}, bf16[1024,128]{1,0:T(8,128)(2,1)S(1)}, u32[]{:S(2)}, u32[]{:S(2)}) collective-permute-start(bf16[1024,128]{1,0:T(8,128)(2,1)S(1)} %shard_map.60.refs_9_), channel_id=1, source_target_pairs={{0,16},{1,17},{2,18},{3,19},{4,20},{5,21},{6,22},{7,23},{8,24},{9,... | collective-permute-start | bytes 786440 | tf_op jit(solution)/shard_map/ppermute | solution.py:520
  82.7 9.2 %collective-permute-done.30.refs_20_ = bf16[256,1024]{1,0:T(8,128)(2,1)S(1)} collective-permute-done((bf16[256,1024]{1,0:T(8,128)(2,1)S(1)}, bf16[256,1024]{1,0:T(8,128)(2,1)S(1)}, u32[]{:S(2)}, u32[]{:S(2)}) %collective-permute-start.30) | collective-permute-done | bytes 524320 | tf_op jit(solution)/shard_map/ppermute | solution.py:520
  92.5 5.0 %collective-permute-done.18.refs_10_ = bf16[1024,128]{1,0:T(8,128)(2,1)S(1)} collective-permute-done((bf16[1024,128]{1,0:T(8,128)(2,1)S(1)}, bf16[1024,128]{1,0:T(8,128)(2,1)S(1)}, u32[]{:S(2)}, u32[]{:S(2)}) %collective-permute-start.18) | collective-permute-done | bytes 262176 | tf_op jit(solution)/shard_map/ppermute | solution.py:520
  98.0 4.4 %collective-permute-done.20.refs_12_ = bf16[1024,128]{1,0:T(8,128)(2,1)S(1)} collective-permute-done((bf16[1024,128]{1,0:T(8,128)(2,1)S(1)}, bf16[1024,128]{1,0:T(8,128)(2,1)S(1)}, u32[]{:S(2)}, u32[]{:S(2)}) %collective-permute-start.20) | collective-permute-done | bytes 262176 | tf_op jit(solution)/shard_map/ppermute | solution.py:520
  103.0 1.6 %collective-permute-done.23.refs_15_ = bf16[1024,128]{1,0:T(8,128)(2,1)S(1)} collective-permute-done((bf16[1024,128]{1,0:T(8,128)(2,1)S(1)}, bf16[1024,128]{1,0:T(8,128)(2,1)S(1)}, u32[]{:S(2)}, u32[]{:S(2)}) %collective-permute-start.23) | collective-permute-done | bytes 262176 | tf_op jit(solution)/shard_map/ppermute | solution.py:520
  105.9 12.7 %shard_map.62 = (bf16[512,128]{1,0:T(8,128)(2,1)S(1)}, bf16[512,128]{1,0:T(8,128)(2,1)S(1)}, bf16[256,512]{1,0:T(8,128)(2,1)S(1)}) custom-call(s32[3]{0:T(128)S(1)} %compare_select_fusion.1.refs_0_, bf16[128,1024]{1,0:T(8,128)(2,1)S(1)} %shard_map.56.refs_1_, bf16[128,1024]{1,0:T(8,128)(2,1)S(1)} %collective-permute-done.3.refs_2_, ...), custom_call_target="tpu_custom_call" | custom-call | flops 17999998976 | bytes 9437190 | tf_op jit(solution)/shard_map/pallas_call | solution.py:525
  125.4 2.5 %collective-permute-done.40.refs_3_.refs_5_ = bf16[512,128]{1,0:T(8,128)(2,1)S(1)} collective-permute-done((bf16[512,128]{1,0:T(8,128)(2,1)S(1)}, bf16[512,128]{1,0:T(8,128)(2,1)S(1)}, u32[]{:S(2)}, u32[]{:S(2)}) %collective-permute-start.40) | collective-permute-done | bytes 131104 | tf_op jit(solution)/shard_map/ppermute | solution.py:520
  128.1 1.5 %collective-permute-done.41.refs_6_ = bf16[1024,128]{1,0:T(8,128)(2,1)S(1)} collective-permute-done((bf16[1024,128]{1,0:T(8,128)(2,1)S(1)}, bf16[1024,128]{1,0:T(8,128)(2,1)S(1)}, u32[]{:S(2)}, u32[]{:S(2)}) %collective-permute-start.41) | collective-permute-done | bytes 262176 | tf_op jit(solution)/shard_map/ppermute | solution.py:520
  130.8 1.8 %collective-permute-start.45 = (bf16[64,512]{1,0:T(8,128)(2,1)S(1)}, bf16[64,512]{1,0:T(8,128)(2,1)S(1)}, u32[]{:S(2)}, u32[]{:S(2)}) collective-permute-start(bf16[64,512]{1,0:T(8,128)(2,1)S(1)} %get-tuple-element.46), channel_id=1, source_target_pairs={{0,4},{1,5},{2,6},{3,7},{4,0},{5,1},{6,2},{7,3},{8,12},{9,13},{10,... | collective-permute-start | bytes 196616 | tf_op jit(solution)/shard_map/ppermute | solution.py:520
  133.5 1.7 %collective-permute-start.47 = (bf16[64,512]{1,0:T(8,128)(2,1)S(1)}, bf16[64,512]{1,0:T(8,128)(2,1)S(1)}, u32[]{:S(2)}, u32[]{:S(2)}) collective-permute-start(bf16[64,512]{1,0:T(8,128)(2,1)S(1)} %get-tuple-element.48), channel_id=1, source_target_pairs={{0,12},{1,13},{2,14},{3,15},{4,8},{5,9},{6,10},{7,11},{8,4},{9,5},... | collective-permute-start | bytes 196616 | tf_op jit(solution)/shard_map/ppermute | solution.py:520
  135.2 5.5 %collective-permute-done.46.refs_3_ = bf16[64,512]{1,0:T(8,128)(2,1)S(1)} collective-permute-done((bf16[64,512]{1,0:T(8,128)(2,1)S(1)}, bf16[64,512]{1,0:T(8,128)(2,1)S(1)}, u32[]{:S(2)}, u32[]{:S(2)}) %collective-permute-start.46) | collective-permute-done | bytes 65568 | tf_op jit(solution)/shard_map/ppermute | solution.py:520
  (79 shorter events, 22.1 us)
Async XLA Ops:
  2.5 12.6 %collective-permute-start.11 = (bf16[4,64,384]{2,1,0:T(8,128)(2,1)S(1)}, bf16[4,64,384]{2,1,0:T(8,128)(2,1)S(1)}, u32[]{:S(2)}, u32[]{:S(2)}) collective-permute-start(bf16[4,64,384]{2,1,0:T(8,128)(2,1)S(1)} %get-tuple-element.34), channel_id=1, source_target_pairs={{0,1},{1,0},{2,3},{3,2},{4,5},{5,4},{6,7},{7,6},{8,9},{9,8},{10,11... | collective-permute-start | bytes 589832 | tf_op jit(solution)/shard_map/ppermute | solution.py:520
  5.6 11.1 %collective-permute-start = (bf16[32,1024]{1,0:T(8,128)(2,1)S(1)}, bf16[32,1024]{1,0:T(8,128)(2,1)S(1)}, u32[]{:S(2)}, u32[]{:S(2)}) collective-permute-start(bf16[32,1024]{1,0:T(8,128)(2,1)S(1)} %get-tuple-element.28), channel_id=1, source_target_pairs={{0,4},{1,5},{2,6},{3,7},{4,0},{5,1},{6,2},{7,3},{8,12},{9,13},{10,... | collective-permute-start | bytes 196616 | tf_op jit(solution)/shard_map/ppermute | solution.py:520
  7.2 9.5 %collective-permute-start.1 = (bf16[32,1024]{1,0:T(8,128)(2,1)S(1)}, bf16[32,1024]{1,0:T(8,128)(2,1)S(1)}, u32[]{:S(2)}, u32[]{:S(2)}) collective-permute-start(bf16[32,1024]{1,0:T(8,128)(2,1)S(1)} %get-tuple-element.29), channel_id=1, source_target_pairs={{0,8},{1,9},{2,10},{3,11},{4,12},{5,13},{6,14},{7,15},{8,0},{9,1},... | collective-permute-start | bytes 196616 | tf_op jit(solution)/shard_map/ppermute | solution.py:520
  10.8 12.3 %collective-permute-start.25 = (bf16[64,1024]{1,0:T(8,128)(2,1)S(1)}, bf16[64,1024]{1,0:T(8,128)(2,1)S(1)}, u32[]{:S(2)}, u32[]{:S(2)}) collective-permute-start(bf16[64,1024]{1,0:T(8,128)(2,1)S(1)} %get-tuple-element.40.refs_0_), channel_id=1, source_target_pairs={{0,4},{1,5},{2,6},{3,7},{4,0},{5,1},{6,2},{7,3},{8,12},{9,13},{10,... | collective-permute-start | bytes 393224 | tf_op jit(solution)/shard_map/ppermute | solution.py:520
  12.6 6.8 %collective-permute-start.2 = (bf16[32,1024]{1,0:T(8,128)(2,1)S(1)}, bf16[32,1024]{1,0:T(8,128)(2,1)S(1)}, u32[]{:S(2)}, u32[]{:S(2)}) collective-permute-start(bf16[32,1024]{1,0:T(8,128)(2,1)S(1)} %get-tuple-element.30), channel_id=1, source_target_pairs={{0,12},{1,13},{2,14},{3,15},{4,8},{5,9},{6,10},{7,11},{8,4},{9,5},... | collective-permute-start | bytes 196616 | tf_op jit(solution)/shard_map/ppermute | solution.py:520
  15.1 9.4 %collective-permute-start.12 = (bf16[128,384]{1,0:T(8,128)(2,1)S(1)}, bf16[128,384]{1,0:T(8,128)(2,1)S(1)}, u32[]{:S(2)}, u32[]{:S(2)}) collective-permute-start(bf16[128,384]{1,0:T(8,128)(2,1)S(1)} %get-tuple-element.36), channel_id=1, source_target_pairs={{0,2},{1,3},{2,0},{3,1},{4,6},{5,7},{6,4},{7,5},{8,10},{9,11},{10,... | collective-permute-start | bytes 294920 | tf_op jit(solution)/shard_map/ppermute | solution.py:520
  19.4 19.0 %collective-permute-start.3 = (bf16[128,1024]{1,0:T(8,128)(2,1)S(1)}, bf16[128,1024]{1,0:T(8,128)(2,1)S(1)}, u32[]{:S(2)}, u32[]{:S(2)}) collective-permute-start(bf16[128,1024]{1,0:T(8,128)(2,1)S(1)} %shard_map.56.refs_1_), channel_id=1, source_target_pairs={{0,2},{1,3},{2,0},{3,1},{4,6},{5,7},{6,4},{7,5},{8,10},{9,11},{10,... | collective-permute-start | bytes 786440 | tf_op jit(solution)/shard_map/ppermute | solution.py:520
  21.0 20.8 %collective-permute-start.4 = (bf16[128,1024]{1,0:T(8,128)(2,1)S(1)}, bf16[128,1024]{1,0:T(8,128)(2,1)S(1)}, u32[]{:S(2)}, u32[]{:S(2)}) collective-permute-start(bf16[128,1024]{1,0:T(8,128)(2,1)S(1)} %shard_map.56.refs_1_), channel_id=1, source_target_pairs={{0,16},{1,17},{2,18},{3,19},{4,20},{5,21},{6,22},{7,23},{8,24},{9,... | collective-permute-start | bytes 786440 | tf_op jit(solution)/shard_map/ppermute | solution.py:520
  22.5 9.8 %collective-permute-start.13 = (bf16[128,384]{1,0:T(8,128)(2,1)S(1)}, bf16[128,384]{1,0:T(8,128)(2,1)S(1)}, u32[]{:S(2)}, u32[]{:S(2)}) collective-permute-start(bf16[128,384]{1,0:T(8,128)(2,1)S(1)} %get-tuple-element.37), channel_id=1, source_target_pairs={{0,16},{1,17},{2,18},{3,19},{4,20},{5,21},{6,22},{7,23},{8,24},{9,... | collective-permute-start | bytes 294920 | tf_op jit(solution)/shard_map/ppermute | solution.py:520
  23.1 18.8 %collective-permute-start.5 = (bf16[128,1024]{1,0:T(8,128)(2,1)S(1)}, bf16[128,1024]{1,0:T(8,128)(2,1)S(1)}, u32[]{:S(2)}, u32[]{:S(2)}) collective-permute-start(bf16[128,1024]{1,0:T(8,128)(2,1)S(1)} %shard_map.56.refs_1_), channel_id=1, source_target_pairs={{0,18},{1,19},{2,16},{3,17},{4,22},{5,23},{6,20},{7,21},{8,26},{9,... | collective-permute-start | bytes 786440 | tf_op jit(solution)/shard_map/ppermute | solution.py:520
  24.5 12.7 %collective-permute-start.14 = (bf16[128,384]{1,0:T(8,128)(2,1)S(1)}, bf16[128,384]{1,0:T(8,128)(2,1)S(1)}, u32[]{:S(2)}, u32[]{:S(2)}) collective-permute-start(bf16[128,384]{1,0:T(8,128)(2,1)S(1)} %get-tuple-element.38), channel_id=1, source_target_pairs={{0,18},{1,19},{2,16},{3,17},{4,22},{5,23},{6,20},{7,21},{8,26},{9,... | collective-permute-start | bytes 294920 | tf_op jit(solution)/shard_map/ppermute | solution.py:520
  38.4 25.0 %collective-permute-start.15 = (bf16[256,384]{1,0:T(8,128)(2,1)S(1)}, bf16[256,384]{1,0:T(8,128)(2,1)S(1)}, u32[]{:S(2)}, u32[]{:S(2)}) collective-permute-start(bf16[256,384]{1,0:T(8,128)(2,1)S(1)} %get-tuple-element.39.refs_9_), channel_id=1, source_target_pairs={{0,4},{1,5},{2,6},{3,7},{4,0},{5,1},{6,2},{7,3},{8,12},{9,13},{10,... | collective-permute-start | bytes 589832 | tf_op jit(solution)/shard_map/ppermute | solution.py:520
  38.5 25.4 %collective-permute-start.16 = (bf16[256,384]{1,0:T(8,128)(2,1)S(1)}, bf16[256,384]{1,0:T(8,128)(2,1)S(1)}, u32[]{:S(2)}, u32[]{:S(2)}) collective-permute-start(bf16[256,384]{1,0:T(8,128)(2,1)S(1)} %get-tuple-element.39.refs_9_), channel_id=1, source_target_pairs={{0,8},{1,9},{2,10},{3,11},{4,12},{5,13},{6,14},{7,15},{8,0},{9,1},... | collective-permute-start | bytes 589832 | tf_op jit(solution)/shard_map/ppermute | solution.py:520
  41.9 22.1 %collective-permute-start.35 = (bf16[256,512]{1,0:T(8,128)(2,1)S(1)}, bf16[256,512]{1,0:T(8,128)(2,1)S(1)}, u32[]{:S(2)}, u32[]{:S(2)}) collective-permute-start(bf16[256,512]{1,0:T(8,128)(2,1)S(1)} %get-tuple-element.41.refs_25_.refs_0_), channel_id=1, source_target_pairs={{0,4},{1,5},{2,6},{3,7},{4,0},{5,1},{6,2},{7,3},{8,12},{9,13},{10,... | collective-permute-start | bytes 786440 | tf_op jit(solution)/shard_map/ppermute | solution.py:520
  41.9 21.5 %collective-permute-start.27 = (bf16[64,1024]{1,0:T(8,128)(2,1)S(1)}, bf16[64,1024]{1,0:T(8,128)(2,1)S(1)}, u32[]{:S(2)}, u32[]{:S(2)}) collective-permute-start(bf16[64,1024]{1,0:T(8,128)(2,1)S(1)} %collective-permute-done.26.refs_2_), channel_id=1, source_target_pairs={{0,4},{1,5},{2,6},{3,7},{4,0},{5,1},{6,2},{7,3},{8,12},{9,13},{10,... | collective-permute-start | bytes 393224 | tf_op jit(solution)/shard_map/ppermute | solution.py:520
  43.9 20.2 %collective-permute-start.36 = (bf16[256,512]{1,0:T(8,128)(2,1)S(1)}, bf16[256,512]{1,0:T(8,128)(2,1)S(1)}, u32[]{:S(2)}, u32[]{:S(2)}) collective-permute-start(bf16[256,512]{1,0:T(8,128)(2,1)S(1)} %get-tuple-element.41.refs_25_.refs_0_), channel_id=1, source_target_pairs={{0,8},{1,9},{2,10},{3,11},{4,12},{5,13},{6,14},{7,15},{8,0},{9,1},... | collective-permute-start | bytes 786440 | tf_op jit(solution)/shard_map/ppermute | solution.py:520
  64.0 7.2 %collective-permute-start.17 = (bf16[256,384]{1,0:T(8,128)(2,1)S(1)}, bf16[256,384]{1,0:T(8,128)(2,1)S(1)}, u32[]{:S(2)}, u32[]{:S(2)}) collective-permute-start(bf16[256,384]{1,0:T(8,128)(2,1)S(1)} %collective-permute-done.16.refs_11_), channel_id=1, source_target_pairs={{0,4},{1,5},{2,6},{3,7},{4,0},{5,1},{6,2},{7,3},{8,12},{9,13},{10,... | collective-permute-start | bytes 589832 | tf_op jit(solution)/shard_map/ppermute | solution.py:520
  64.1 16.7 %collective-permute-start.28 = (bf16[256,1024]{1,0:T(8,128)(2,1)S(1)}, bf16[256,1024]{1,0:T(8,128)(2,1)S(1)}, u32[]{:S(2)}, u32[]{:S(2)}) collective-permute-start(bf16[256,1024]{1,0:T(8,128)(2,1)S(1)} %shard_map.61.refs_17_), channel_id=1, source_target_pairs={{0,2},{1,3},{2,0},{3,1},{4,6},{5,7},{6,4},{7,5},{8,10},{9,11},{10,... | collective-permute-start | bytes 1572872 | tf_op jit(solution)/shard_map/ppermute | solution.py:520
  65.7 16.6 %collective-permute-start.29 = (bf16[256,1024]{1,0:T(8,128)(2,1)S(1)}, bf16[256,1024]{1,0:T(8,128)(2,1)S(1)}, u32[]{:S(2)}, u32[]{:S(2)}) collective-permute-start(bf16[256,1024]{1,0:T(8,128)(2,1)S(1)} %shard_map.61.refs_17_), channel_id=1, source_target_pairs={{0,16},{1,17},{2,18},{3,19},{4,20},{5,21},{6,22},{7,23},{8,24},{9,... | collective-permute-start | bytes 1572872 | tf_op jit(solution)/shard_map/ppermute | solution.py:520
  67.1 24.8 %collective-permute-start.30 = (bf16[256,1024]{1,0:T(8,128)(2,1)S(1)}, bf16[256,1024]{1,0:T(8,128)(2,1)S(1)}, u32[]{:S(2)}, u32[]{:S(2)}) collective-permute-start(bf16[256,1024]{1,0:T(8,128)(2,1)S(1)} %shard_map.61.refs_17_), channel_id=1, source_target_pairs={{0,18},{1,19},{2,16},{3,17},{4,22},{5,23},{6,20},{7,21},{8,26},{9,... | collective-permute-start | bytes 1572872 | tf_op jit(solution)/shard_map/ppermute | solution.py:520
  67.9 24.0 %collective-permute-start.31 = (bf16[256,1024]{1,0:T(8,128)(2,1)S(1)}, bf16[256,1024]{1,0:T(8,128)(2,1)S(1)}, u32[]{:S(2)}, u32[]{:S(2)}) collective-permute-start(bf16[256,1024]{1,0:T(8,128)(2,1)S(1)} %shard_map.61.refs_17_), channel_id=1, source_target_pairs={{0,1},{1,0},{2,3},{3,2},{4,5},{5,4},{6,7},{7,6},{8,9},{9,8},{10,11... | collective-permute-start | bytes 1572872 | tf_op jit(solution)/shard_map/ppermute | solution.py:520
  71.2 7.9 %collective-permute-start.37 = (bf16[256,512]{1,0:T(8,128)(2,1)S(1)}, bf16[256,512]{1,0:T(8,128)(2,1)S(1)}, u32[]{:S(2)}, u32[]{:S(2)}) collective-permute-start(bf16[256,512]{1,0:T(8,128)(2,1)S(1)} %collective-permute-done.36.refs_27_.refs_2_), channel_id=1, source_target_pairs={{0,4},{1,5},{2,6},{3,7},{4,0},{5,1},{6,2},{7,3},{8,12},{9,13},{10,... | collective-permute-start | bytes 786440 | tf_op jit(solution)/shard_map/ppermute | solution.py:520
  79.2 18.3 %collective-permute-start.18 = (bf16[1024,128]{1,0:T(8,128)(2,1)S(1)}, bf16[1024,128]{1,0:T(8,128)(2,1)S(1)}, u32[]{:S(2)}, u32[]{:S(2)}) collective-permute-start(bf16[1024,128]{1,0:T(8,128)(2,1)S(1)} %shard_map.60.refs_9_), channel_id=1, source_target_pairs={{0,2},{1,3},{2,0},{3,1},{4,6},{5,7},{6,4},{7,5},{8,10},{9,11},{10,... | collective-permute-start | bytes 786440 | tf_op jit(solution)/shard_map/ppermute | solution.py:520
  80.8 16.8 %collective-permute-start.19 = (bf16[1024,128]{1,0:T(8,128)(2,1)S(1)}, bf16[1024,128]{1,0:T(8,128)(2,1)S(1)}, u32[]{:S(2)}, u32[]{:S(2)}) collective-permute-start(bf16[1024,128]{1,0:T(8,128)(2,1)S(1)} %shard_map.60.refs_9_), channel_id=1, source_target_pairs={{0,16},{1,17},{2,18},{3,19},{4,20},{5,21},{6,22},{7,23},{8,24},{9,... | collective-permute-start | bytes 786440 | tf_op jit(solution)/shard_map/ppermute | solution.py:520
  82.2 20.1 %collective-permute-start.20 = (bf16[1024,128]{1,0:T(8,128)(2,1)S(1)}, bf16[1024,128]{1,0:T(8,128)(2,1)S(1)}, u32[]{:S(2)}, u32[]{:S(2)}) collective-permute-start(bf16[1024,128]{1,0:T(8,128)(2,1)S(1)} %shard_map.60.refs_9_), channel_id=1, source_target_pairs={{0,18},{1,19},{2,16},{3,17},{4,22},{5,23},{6,20},{7,21},{8,26},{9,... | collective-permute-start | bytes 786440 | tf_op jit(solution)/shard_map/ppermute | solution.py:520
  92.0 10.4 %collective-permute-start.21 = (bf16[1024,128]{1,0:T(8,128)(2,1)S(1)}, bf16[1024,128]{1,0:T(8,128)(2,1)S(1)}, u32[]{:S(2)}, u32[]{:S(2)}) collective-permute-start(bf16[1024,128]{1,0:T(8,128)(2,1)S(1)} %shard_map.60.refs_9_), channel_id=1, source_target_pairs={{0,1},{1,0},{2,3},{3,2},{4,5},{5,4},{6,7},{7,6},{8,9},{9,8},{10,11... | collective-permute-start | bytes 786440 | tf_op jit(solution)/shard_map/ppermute | solution.py:520
  92.0 13.9 %collective-permute-start.32 = (bf16[256,1024]{1,0:T(8,128)(2,1)S(1)}, bf16[256,1024]{1,0:T(8,128)(2,1)S(1)}, u32[]{:S(2)}, u32[]{:S(2)}) collective-permute-start(bf16[256,1024]{1,0:T(8,128)(2,1)S(1)} %collective-permute-done.28.refs_18_), channel_id=1, source_target_pairs={{0,1},{1,0},{2,3},{3,2},{4,5},{5,4},{6,7},{7,6},{8,9},{9,8},{10,11... | collective-permute-start | bytes 1572872 | tf_op jit(solution)/shard_map/ppermute | solution.py:520
  97.5 8.4 %collective-permute-start.33 = (bf16[256,1024]{1,0:T(8,128)(2,1)S(1)}, bf16[256,1024]{1,0:T(8,128)(2,1)S(1)}, u32[]{:S(2)}, u32[]{:S(2)}) collective-permute-start(bf16[256,1024]{1,0:T(8,128)(2,1)S(1)} %collective-permute-done.29.refs_19_), channel_id=1, source_target_pairs={{0,1},{1,0},{2,3},{3,2},{4,5},{5,4},{6,7},{7,6},{8,9},{9,8},{10,11... | collective-permute-start | bytes 1572872 | tf_op jit(solution)/shard_map/ppermute | solution.py:520
  104.7 17.5 %collective-permute-start.42 = (bf16[256,512]{1,0:T(8,128)(2,1)S(1)}, bf16[256,512]{1,0:T(8,128)(2,1)S(1)}, u32[]{:S(2)}, u32[]{:S(2)}) collective-permute-start(bf16[256,512]{1,0:T(8,128)(2,1)S(1)} %shard_map.64.refs_7_), channel_id=1, source_target_pairs={{0,2},{1,3},{2,0},{3,1},{4,6},{5,7},{6,4},{7,5},{8,10},{9,11},{10,... | collective-permute-start | bytes 786440 | tf_op jit(solution)/shard_map/ppermute | solution.py:520
  121.0 7.0 %collective-permute-start.40 = (bf16[512,128]{1,0:T(8,128)(2,1)S(1)}, bf16[512,128]{1,0:T(8,128)(2,1)S(1)}, u32[]{:S(2)}, u32[]{:S(2)}) collective-permute-start(bf16[512,128]{1,0:T(8,128)(2,1)S(1)} %get-tuple-element.44), channel_id=1, source_target_pairs={{0,18},{1,19},{2,16},{3,17},{4,22},{5,23},{6,20},{7,21},{8,26},{9,... | collective-permute-start | bytes 393224 | tf_op jit(solution)/shard_map/ppermute | solution.py:520
  132.6 8.2 %collective-permute-start.46 = (bf16[64,512]{1,0:T(8,128)(2,1)S(1)}, bf16[64,512]{1,0:T(8,128)(2,1)S(1)}, u32[]{:S(2)}, u32[]{:S(2)}) collective-permute-start(bf16[64,512]{1,0:T(8,128)(2,1)S(1)} %get-tuple-element.47), channel_id=1, source_target_pairs={{0,8},{1,9},{2,10},{3,11},{4,12},{5,13},{6,14},{7,15},{8,0},{9,1},... | collective-permute-start | bytes 196616 | tf_op jit(solution)/shard_map/ppermute | solution.py:520
  133.5 7.2 %collective-permute-start.47 = (bf16[64,512]{1,0:T(8,128)(2,1)S(1)}, bf16[64,512]{1,0:T(8,128)(2,1)S(1)}, u32[]{:S(2)}, u32[]{:S(2)}) collective-permute-start(bf16[64,512]{1,0:T(8,128)(2,1)S(1)} %get-tuple-element.48), channel_id=1, source_target_pairs={{0,12},{1,13},{2,14},{3,15},{4,8},{5,9},{6,10},{7,11},{8,4},{9,5},... | collective-permute-start | bytes 196616 | tf_op jit(solution)/shard_map/ppermute | solution.py:520
  (17 other events, 73.6 us)

commit v4 on v3

--- a/solution.py
+++ b/solution.py
@@ -213,33 +213,28 @@
         return mx * self.seq_count + mz * self.inner + mi
 
 
-def attention(qkv, out, cols, rows_q):
-    tokens = qkv.shape[0]
+def attention(qkv, out, cols):
     lane_head = lax.broadcasted_iota(jnp.int32, (1, cols), 1) // HEAD_DIM
-
-    def one_block(block_no, carry):
-        rows = pl.ds(pl.multiple_of(block_no * rows_q, rows_q), rows_q)
-        query = qkv[rows, 0:cols]
-        keys_in = qkv[:, cols : 2 * cols]
-        values_in = qkv[:, 2 * cols : 3 * cols]
-        mixed = jnp.zeros((rows_q, cols), jnp.float32)
-        for head in range(cols // HEAD_DIM):
-            mine = lane_head == head
-            picked = jnp.where(mine, query, jnp.zeros_like(query))
-            scores = lax.dot_general(
-                picked, keys_in, (((1,), (1,)), ((), ())), preferred_element_type=jnp.float32
-            )
-            row_max = jnp.max(scores, axis=-1, keepdims=True)
-            weights = jnp.exp(scores - row_max)
-            totals = jnp.sum(weights, axis=-1, keepdims=True)
-            part = jnp.dot(
-                weights.astype(jnp.bfloat16), values_in, preferred_element_type=jnp.float32
-            )
-            mixed = jnp.where(mine, part / totals, mixed)
-        out[rows, :] = mixed.astype(jnp.bfloat16)
-        return carry
-
-    lax.fori_loop(0, tokens // rows_q, one_block, 0)
+    queries = qkv[:, 0:cols]
+    keys_in = qkv[:, cols : 2 * cols]
+    values_in = qkv[:, 2 * cols : 3 * cols]
+    mixed = jnp.zeros(queries.shape, jnp.float32)
+    for head in range(cols // HEAD_DIM):
+        mine = lane_head == head
+        picked = jnp.where(mine, queries, jnp.zeros_like(queries))
+        scores = lax.dot_general(
+            keys_in, picked, (((1,), (1,)), ((), ())), preferred_element_type=jnp.float32
+        )
+        weights = jnp.exp(scores - jnp.max(scores, axis=0, keepdims=True))
+        totals = jnp.sum(weights, axis=0, keepdims=True)
+        part = lax.dot_general(
+            values_in,
+            weights.astype(jnp.bfloat16),
+            (((0,), (0,)), ((), ())),
+            preferred_element_type=jnp.float32,
+        )
+        mixed = jnp.where(mine, (part / totals).T, mixed)
+    out[...] = mixed.astype(jnp.bfloat16)
 
 
 def project_rows(normed, w_qkv, cols):
@@ -259,7 +254,7 @@
 
 def prepare_kernel(plan, where, latents, gain, qkv_weight, proj_weight, merge_weight, *rest):
     shares = rest[: plan.windows]
-    keep, give, cross, held, sems = rest[plan.windows :]
+    keep, give, cross, held, factor, sems = rest[plan.windows :]
     copies = []
 
     def add(source, target):
@@ -270,6 +265,7 @@
             qkv_weight.at[0, :, part * plan.features : (part + 1) * plan.features],
             held.at[part],
         )
+    add(gain, factor)
     width, rows = (plan.half_cols, plan.w_rows)
     for part, matrix in enumerate((proj_weight, merge_weight)):
         add(
@@ -280,13 +276,13 @@
         add(latents.at[where[1] ^ mz, aligned(where[0], plan.half), :], shares[mz])
     for copy in copies:
         copy.start()
+    for copy in copies[:4]:
+        copy.wait()
     first_row = (where[1] * plan.inner + where[2]) * rows
     row = first_row + lax.broadcasted_iota(jnp.int32, (rows, plan.features), 0)
     lane = lax.broadcasted_iota(jnp.int32, (rows, plan.features), 1)
-    factors = jnp.where(row == lane, gain[...], jnp.zeros((1, plan.features), jnp.float32))
+    factors = jnp.where(row == lane, factor[...], jnp.zeros((1, plan.features), jnp.float32))
     factors = jnp.sum(factors, axis=1, keepdims=True)
-    for copy in copies[:3]:
-        copy.wait()
     for core, target in ((1, give), (0, keep)):
         for chip_no, (mx, mi) in enumerate(plan.chips):
             lanes = aligned(slot_of(plan, where, mx, mi ^ core), plan.cols)
@@ -295,7 +291,7 @@
                 target[chip_no, :, part * plan.cols : (part + 1) * plan.cols] = scaled.astype(
                     jnp.bfloat16
                 )
-    for copy in copies[3:]:
+    for copy in copies[4:]:
         copy.wait()
 
 
@@ -387,68 +383,74 @@
     lax.fori_loop(0, plan.tokens // size, step, 0)
 
 
-def first_kernel(plan, where, *rest):
-    hidden_in = rest[: plan.slots]
-    pieces = rest[plan.slots : plan.slots + plan.windows]
-    out, w_qkv, normed, qkv = rest[plan.slots + plan.windows :]
+def norm_kernel(plan, where, *refs):
+    hid, normed = refs[plan.slots :]
+    for piece, (mx, mi) in zip(refs, plane_order(plan)):
+        rows = aligned(slot_of(plan, where, mx, mi), plan.shard)
+        hid[rows, :] = piece[...]
+        normed[rows, :] = normalize(piece[...].astype(jnp.float32))
+
+
+def first_kernel(plan, where, normed, *rest):
+    pieces = rest[: plan.windows]
+    out, w_qkv, qkv = rest[plan.windows :]
     gather_weights(plan, where, pieces, w_qkv)
-    for piece, (mx, mi) in zip(hidden_in, plane_order(plan)):
-        rows = aligned(slot_of(plan, where, mx, mi), plan.shard)
-        normed[rows, :] = normalize(piece[...].astype(jnp.float32))
 
     def one_block(rows):
         qkv[rows, :] = project_rows(normed[rows, :], w_qkv[...], plan.cols)
 
     row_blocks(plan, one_block)
-    attention(qkv, out, plan.cols, min(256, plan.tokens))
-
-
-def second_kernel(plan, where, *rest):
+    attention(qkv, out, plan.cols)
+
+
+def fold_kernel(plan, where, hid, *rest):
+    mats_in, (merged, folded, mats) = (rest[: plan.slots], rest[plan.slots :])
+    rows, width = (plan.w_rows, plan.half_cols)
+    for piece, (mx, mi) in zip(mats_in, plane_order(plan)):
+        for mz in range(plan.windows):
+            shard = (where[1] ^ mz) * plan.inner + (where[2] ^ mi)
+            part = piece[mz * rows : (mz + 1) * rows, :]
+            for kind in range(2):
+                lanes = aligned(where[0] ^ mx, width)
+                mats[kind, aligned(shard, rows), lanes] = part[:, kind * width : (kind + 1) * width]
+
+    def one_block(part):
+        merged[part, :] = jnp.dot(hid[part, :], mats[1], preferred_element_type=jnp.float32)
+
+    row_blocks(plan, one_block)
+    size = min(512, plan.features)
+
+    def one_part(block_no, carry):
+        part = aligned(block_no, size)
+        folded[part, :] = jnp.dot(
+            mats[0, part, :], mats[1], preferred_element_type=jnp.float32
+        ).astype(jnp.bfloat16)
+        return carry
+
+    lax.fori_loop(0, plan.features // size, one_part, 0)
+
+
+def second_kernel(plan, where, merged, folded, *rest):
     slots, windows = (plan.slots, plan.windows)
-    hidden_in, rest = (rest[:slots], rest[slots:])
     attended_in, rest = (rest[:slots], rest[slots:])
-    mats_in, rest = (rest[:slots], rest[slots:])
     pieces, rest = (rest[:windows], rest[windows:])
     outs, rest = (rest[: plan.inner // 2], rest[plan.inner // 2 :])
-    kept, hid, att, mats, w_qkv, joined, qkv, mixed = rest
-    order = plane_order(plan)
-    for piece, (mx, mi) in zip(hidden_in, order):
-        hid[aligned(slot_of(plan, where, mx, mi), plan.shard), :] = piece[...]
-    for piece, (mx, mi) in zip(attended_in, order):
+    kept, att, w_qkv, joined, qkv, mixed = rest
+    for piece, (mx, mi) in zip(attended_in, plane_order(plan)):
         att[:, aligned(slot_of(plan, where, mx, mi), plan.cols)] = piece[...]
-    rows = plan.w_rows
-    for piece, (mx, mi) in zip(mats_in, order):
-        for mz in range(windows):
-            shard = (where[1] ^ mz) * plan.inner + (where[2] ^ mi)
-            mats[where[0] ^ mx, aligned(shard, rows), :] = piece[mz * rows : (mz + 1) * rows, :]
     gather_weights(plan, where, pieces, w_qkv)
     width = plan.half_cols
 
     def one_block(part):
-        attended = att[part, :]
-        hidden = jnp.concatenate(
-            [
-                jnp.dot(attended, mats[side, :, 0:width], preferred_element_type=jnp.float32)
-                for side in range(plan.sections)
-            ],
-            axis=1,
-        )
-        hidden = (hid[part, :].astype(jnp.float32) + hidden).astype(jnp.bfloat16)
-        merged = jnp.concatenate(
-            [
-                jnp.dot(hidden, mats[side, :, width:], preferred_element_type=jnp.float32)
-                for side in range(plan.sections)
-            ],
-            axis=1,
-        )
-        merged = merged.astype(jnp.bfloat16)
-        joined[part, :] = merged
+        total = jnp.dot(att[part, :], folded[...], preferred_element_type=jnp.float32)
+        total = (merged[part, :] + total).astype(jnp.bfloat16)
+        joined[part, :] = total
         qkv[part, :] = project_rows(
-            normalize(merged.astype(jnp.float32)), w_qkv[...], plan.cols
+            normalize(total.astype(jnp.float32)), w_qkv[...], plan.cols
         )
 
     row_blocks(plan, one_block)
-    attention(qkv, mixed, plan.cols, min(256, plan.tokens))
+    attention(qkv, mixed, plan.cols)
     lanes = aligned(where[0], width)
     for side in range(plan.sections):
         for mi in range(plan.inner):
@@ -520,7 +522,8 @@
         return lax.ppermute(value, ("section", "seq"), pairs)
 
     def call(kernel, outs, ins, scratch=(), specs=None, flops=0, limit=40):
-        shapes = tuple(jax.ShapeDtypeStruct(shape, bf16) for shape in outs)
+        typed = [shape if isinstance(shape[0], tuple) else (shape, bf16) for shape in outs]
+        shapes = tuple(jax.ShapeDtypeStruct(*entry) for entry in typed)
         moved = sum(2 * value.size for value in ins)
         return pl.pallas_call(
             kernel,
@@ -555,9 +558,9 @@
     def core_gather(pieces):
         return pieces + [swap(piece, plan.mask(mi=1)) for piece in pieces]
 
-    latents, qkv_weight, proj_weight, merge_weight = (
+    latents, norm_gain, qkv_weight, proj_weight, merge_weight = (
         pltpu.with_memory_space_constraint(value, pltpu.HBM)
-        for value in (latents, qkv_weight, proj_weight, merge_weight)
+        for value in (latents, norm_gain, qkv_weight, proj_weight, merge_weight)
     )
     prepared = call(
         lambda *refs: prepare_kernel(plan, *refs),
@@ -567,9 +570,10 @@
         [where, latents, norm_gain, qkv_weight, proj_weight, merge_weight],
         [
             pltpu.VMEM((3, plan.w_rows, features), bf16),
-            pltpu.SemaphoreType.DMA((5 + windows,)),
+            pltpu.VMEM((1, features), jnp.float32),
+            pltpu.SemaphoreType.DMA((6 + windows,)),
         ],
-        [smem, hbm, vmem, hbm, hbm, hbm],
+        [smem] + [hbm] * 5,
         limit=8,
     )
     shares, (keep, give, cross) = (prepared[:windows], prepared[windows:])
@@ -613,37 +617,49 @@
     pieces_b = z_gather(rows_b)
     mats = chip_gather(stack(mats))
 
+    hid, normed = call(
+        lambda *refs: norm_kernel(plan, *refs),
+        [(tokens, features)] * 2,
+        [where] + hidden,
+        (),
+        [smem] + [vmem] * len(hidden),
+        limit=16,
+    )
     (attended,) = call(
         lambda *refs: first_kernel(plan, *refs),
         [(tokens, cols)],
-        [where] + hidden + pieces_a,
-        [
-            pltpu.VMEM((features, 3 * cols), bf16),
-            pltpu.VMEM((tokens, features), bf16),
-            pltpu.VMEM((tokens, 3 * cols), bf16),
-        ],
-        [smem] + [vmem] * (len(hidden) + windows),
+        [where, normed] + pieces_a,
+        [pltpu.VMEM((features, 3 * cols), bf16), pltpu.VMEM((tokens, 3 * cols), bf16)],
+        [smem] + [vmem] * (1 + windows),
         flops=10_000_000_000,
+        limit=20,
     )
     attended = core_gather(chip_gather(attended))
     mats = core_gather(mats)
+    merged, folded = call(
+        lambda *refs: fold_kernel(plan, *refs),
+        [((tokens, features), jnp.float32), (features, features)],
+        [where, hid] + mats,
+        [pltpu.VMEM((2, features, features), bf16)],
+        [smem] + [vmem] * (1 + plan.slots),
+        flops=4_000_000_000,
+        limit=30,
+    )
     (last,) = call(lambda *refs: last_kernel(plan, *refs), [(plan.group, width)], pieces_b, limit=8)
     last = [last] + [swap(last, plan.mask(mi=mi)) for mi in range(2, inner, 2)]
     last = core_gather(last)
     *attended, kept = call(
         lambda *refs: second_kernel(plan, *refs),
         [(2 * plan.sections * shard, cols)] * (inner // 2) + [(plan.sections * shard, width)],
-        [where] + hidden + attended + mats + pieces_b,
+        [where, merged, folded] + attended + pieces_b,
         [
             pltpu.VMEM((tokens, features), bf16),
-            pltpu.VMEM((tokens, features), bf16),
-            pltpu.VMEM((plan.sections, features, 2 * width), bf16),
             pltpu.VMEM((features, 3 * cols), bf16),
             pltpu.VMEM((tokens, features), bf16),
             pltpu.VMEM((tokens, 3 * cols), bf16),
             pltpu.VMEM((tokens, cols), bf16),
         ],
-        [smem] + [vmem] * (3 * plan.slots + windows),
+        [smem] + [vmem] * (2 + plan.slots + windows),
         flops=18_000_000_000,
     )
     back = [attended[0]] + [

time: 142 us -> 142 us (level)
  starting transfers between devices: 46 us -> 37.8 us
  waiting for transfers between devices: 68.9 us -> 75.7 us
  Pallas kernels: 26.3 us -> 28.1 us
    ppermute x48, starting transfers between devices: 46 us -> 37.8 us  [swap(): return lax.ppermute(value, ('section', 'seq'), pairs)]
    ppermute x48, waiting for transfers between devices: 68.9 us -> 75.7 us  [swap(): return lax.ppermute(value, ('section', 'seq'), pairs)]
    pallas_call x12 -> x14, Pallas kernels: 26.3 us -> 28.1 us  [call(): pl.pallas_call(kernel, out_shape=shapes, in_specs=specs or [vmem] * len(i...]
  transfers between devices with their start and end apart: 48 -> 48, of which waited for: 15 -> 20; matrix products, arithmetic and copies ran while one was open for 0% -> 0% of each run, Pallas kernels for 16% -> 17%
where the time goes in v4:
time: 142 us
  waiting for transfers between devices  75.7 us (53%)
  starting transfers between devices  37.8 us (27%)
  Pallas kernels  28.1 us (20%)
    ppermute x48, waiting for transfers between devices, swap(): return lax.ppermute(value, ('section', 'seq'), pairs)  75.7 us
    ppermute x48, starting transfers between devices, swap(): return lax.ppermute(value, ('section', 'seq'), pairs)  37.8 us
    pallas_call x14, Pallas kernels, call(): pl.pallas_call(kernel, out_shape=shapes, in_specs=specs or [vmem] * len(i...  28.1 us
  transfers between devices with their start and end apart: 48, of which 20 were waited for; matrix products, arithmetic and copies ran while one was open for 0% of the time, Pallas kernels for 17%

profile of v4, /device:TPU:0, one launch (start us, length us, event | category | flops | bytes accessed | tf_op | source)
XLA Modules:
  0.0 141.8 jit_solution(514470322610231146)
XLA Ops:
  0.0 1.9 %shard_map.55 = (bf16[32,1024]{1,0:T(8,128)(2,1)S(1)}, bf16[32,1024]{1,0:T(8,128)(2,1)S(1)}, bf16[32,1024]{1,0:T(8,128)(2,1)S(1)}, bf16[32,1024]{1,0:T(8,128)(2,...) custom-call(s32[3]{0:T(128)S(1)} %compare_select_fusion.1.refs_0_, ...), custom_call_target="tpu_custom_call" | custom-call | bytes 1181702 | tf_op jit(solution)/shard_map/pallas_call | solution.py:528
  2.4 2.6 %collective-permute-start.10 = (bf16[128,512]{1,0:T(8,128)(2,1)S(1)}, bf16[128,512]{1,0:T(8,128)(2,1)S(1)}, u32[]{:S(2)}, u32[]{:S(2)}) collective-permute-start(bf16[128,512]{1,0:T(8,128)(2,1)S(1)} %get-tuple-element.36), channel_id=1, source_target_pairs={{0,16},{1,17},{2,18},{3,19},{4,20},{5,21},{6,22},{7,23},{8,24},{9,... | collective-permute-start | bytes 393224 | tf_op jit(solution)/shard_map/ppermute | solution.py:522
  5.0 1.6 %collective-permute-start = (bf16[32,1024]{1,0:T(8,128)(2,1)S(1)}, bf16[32,1024]{1,0:T(8,128)(2,1)S(1)}, u32[]{:S(2)}, u32[]{:S(2)}) collective-permute-start(bf16[32,1024]{1,0:T(8,128)(2,1)S(1)} %get-tuple-element.32), channel_id=1, source_target_pairs={{0,4},{1,5},{2,6},{3,7},{4,0},{5,1},{6,2},{7,3},{8,12},{9,13},{10,... | collective-permute-start | bytes 196616 | tf_op jit(solution)/shard_map/ppermute | solution.py:522
  6.6 2.6 %collective-permute-start.1 = (bf16[32,1024]{1,0:T(8,128)(2,1)S(1)}, bf16[32,1024]{1,0:T(8,128)(2,1)S(1)}, u32[]{:S(2)}, u32[]{:S(2)}) collective-permute-start(bf16[32,1024]{1,0:T(8,128)(2,1)S(1)} %get-tuple-element.33), channel_id=1, source_target_pairs={{0,8},{1,9},{2,10},{3,11},{4,12},{5,13},{6,14},{7,15},{8,0},{9,1},... | collective-permute-start | bytes 196616 | tf_op jit(solution)/shard_map/ppermute | solution.py:522
  10.4 2.6 %collective-permute-start.12 = (bf16[64,1024]{1,0:T(8,128)(2,1)S(1)}, bf16[64,1024]{1,0:T(8,128)(2,1)S(1)}, u32[]{:S(2)}, u32[]{:S(2)}) collective-permute-start(bf16[64,1024]{1,0:T(8,128)(2,1)S(1)} %get-tuple-element.37.refs_0_), channel_id=1, source_target_pairs={{0,8},{1,9},{2,10},{3,11},{4,12},{5,13},{6,14},{7,15},{8,0},{9,1},... | collective-permute-start | bytes 393224 | tf_op jit(solution)/shard_map/ppermute | solution.py:522
  13.0 1.6 %collective-permute-start.22 = (bf16[128,384]{1,0:T(8,128)(2,1)S(1)}, bf16[128,384]{1,0:T(8,128)(2,1)S(1)}, u32[]{:S(2)}, u32[]{:S(2)}) collective-permute-start(bf16[128,384]{1,0:T(8,128)(2,1)S(1)} %get-tuple-element.45), channel_id=1, source_target_pairs={{0,2},{1,3},{2,0},{3,1},{4,6},{5,7},{6,4},{7,5},{8,10},{9,11},{10,... | collective-permute-start | bytes 294920 | tf_op jit(solution)/shard_map/ppermute | solution.py:522
  16.9 2.2 %collective-permute-start.4 = (bf16[128,1024]{1,0:T(8,128)(2,1)S(1)}, bf16[128,1024]{1,0:T(8,128)(2,1)S(1)}, u32[]{:S(2)}, u32[]{:S(2)}) collective-permute-start(bf16[128,1024]{1,0:T(8,128)(2,1)S(1)} %shard_map.56.refs_1_), channel_id=1, source_target_pairs={{0,16},{1,17},{2,18},{3,19},{4,20},{5,21},{6,22},{7,23},{8,24},{9,... | collective-permute-start | bytes 786440 | tf_op jit(solution)/shard_map/ppermute | solution.py:522
  19.1 2.1 %collective-permute-done.12.refs_2_ = bf16[64,1024]{1,0:T(8,128)(2,1)S(1)} collective-permute-done((bf16[64,1024]{1,0:T(8,128)(2,1)S(1)}, bf16[64,1024]{1,0:T(8,128)(2,1)S(1)}, u32[]{:S(2)}, u32[]{:S(2)}) %collective-permute-start.12) | collective-permute-done | bytes 131104 | tf_op jit(solution)/shard_map/ppermute | solution.py:522
  21.2 2.8 %collective-permute-start.24 = (bf16[128,384]{1,0:T(8,128)(2,1)S(1)}, bf16[128,384]{1,0:T(8,128)(2,1)S(1)}, u32[]{:S(2)}, u32[]{:S(2)}) collective-permute-start(bf16[128,384]{1,0:T(8,128)(2,1)S(1)} %get-tuple-element.47), channel_id=1, source_target_pairs={{0,18},{1,19},{2,16},{3,17},{4,22},{5,23},{6,20},{7,21},{8,26},{9,... | collective-permute-start | bytes 294920 | tf_op jit(solution)/shard_map/ppermute | solution.py:522
  24.0 7.8 %collective-permute-done.23.refs_4_ = bf16[128,384]{1,0:T(8,128)(2,1)S(1)} collective-permute-done((bf16[128,384]{1,0:T(8,128)(2,1)S(1)}, bf16[128,384]{1,0:T(8,128)(2,1)S(1)}, u32[]{:S(2)}, u32[]{:S(2)}) %collective-permute-start.23) | collective-permute-done | bytes 98336 | tf_op jit(solution)/shard_map/ppermute | solution.py:522
  35.0 1.8 %collective-permute-done.11.refs_1_ = bf16[64,1024]{1,0:T(8,128)(2,1)S(1)} collective-permute-done((bf16[64,1024]{1,0:T(8,128)(2,1)S(1)}, bf16[64,1024]{1,0:T(8,128)(2,1)S(1)}, u32[]{:S(2)}, u32[]{:S(2)}) %collective-permute-start.11) | collective-permute-done | bytes 131104 | tf_op jit(solution)/shard_map/ppermute | solution.py:522
  36.8 2.0 %collective-permute-start.26 = (bf16[256,384]{1,0:T(8,128)(2,1)S(1)}, bf16[256,384]{1,0:T(8,128)(2,1)S(1)}, u32[]{:S(2)}, u32[]{:S(2)}) collective-permute-start(bf16[256,384]{1,0:T(8,128)(2,1)S(1)} %get-tuple-element.48.refs_2_), channel_id=1, source_target_pairs={{0,8},{1,9},{2,10},{3,11},{4,12},{5,13},{6,14},{7,15},{8,0},{9,1},... | collective-permute-start | bytes 589832 | tf_op jit(solution)/shard_map/ppermute | solution.py:522
  39.4 8.8 %collective-permute-done.13.refs_3_ = bf16[64,1024]{1,0:T(8,128)(2,1)S(1)} collective-permute-done((bf16[64,1024]{1,0:T(8,128)(2,1)S(1)}, bf16[64,1024]{1,0:T(8,128)(2,1)S(1)}, u32[]{:S(2)}, u32[]{:S(2)}) %collective-permute-start.13) | collective-permute-done | bytes 131104 | tf_op jit(solution)/shard_map/ppermute | solution.py:522
  48.2 2.0 %collective-permute-start.25 = (bf16[256,384]{1,0:T(8,128)(2,1)S(1)}, bf16[256,384]{1,0:T(8,128)(2,1)S(1)}, u32[]{:S(2)}, u32[]{:S(2)}) collective-permute-start(bf16[256,384]{1,0:T(8,128)(2,1)S(1)} %get-tuple-element.48.refs_2_), channel_id=1, source_target_pairs={{0,4},{1,5},{2,6},{3,7},{4,0},{5,1},{6,2},{7,3},{8,12},{9,13},{10,... | collective-permute-start | bytes 589832 | tf_op jit(solution)/shard_map/ppermute | solution.py:522
  50.5 2.0 %shard_map.57 = (bf16[1024,1024]{1,0:T(8,128)(2,1)S(1)}, bf16[1024,1024]{1,0:T(8,128)(2,1)S(1)}) custom-call(s32[3]{0:T(128)S(1)} %compare_select_fusion.1.refs_0_, bf16[128,1024]{1,0:T(8,128)(2,1)S(1)} %shard_map.56.refs_1_, bf16[128,1024]{1,0:T(8,128)(2,1)S(1)} %collective-permute-done.3.refs_2_, bf16[128,1024]{1,0:T(8,128)(2,1)S(1)} %collective-permute-done.4.refs_3_, ...), custom_call_target="tpu_custom_call" | custom-call | bytes 2097158 | tf_op jit(solution)/shard_map/pallas_call | solution.py:528
  52.5 14.4 %collective-permute-done.25.refs_3_ = bf16[256,384]{1,0:T(8,128)(2,1)S(1)} collective-permute-done((bf16[256,384]{1,0:T(8,128)(2,1)S(1)}, bf16[256,384]{1,0:T(8,128)(2,1)S(1)}, u32[]{:S(2)}, u32[]{:S(2)}) %collective-permute-start.25) | collective-permute-done | bytes 196640 | tf_op jit(solution)/shard_map/ppermute | solution.py:522
  66.9 1.9 %collective-permute-start.15 = (bf16[256,1024]{1,0:T(8,128)(2,1)S(1)}, bf16[256,1024]{1,0:T(8,128)(2,1)S(1)}, u32[]{:S(2)}, u32[]{:S(2)}) collective-permute-start(bf16[256,1024]{1,0:T(8,128)(2,1)S(1)} %shard_map.59.refs_2_), channel_id=1, source_target_pairs={{0,16},{1,17},{2,18},{3,19},{4,20},{5,21},{6,22},{7,23},{8,24},{9,... | collective-permute-start | bytes 1572872 | tf_op jit(solution)/shard_map/ppermute | solution.py:522
  70.7 5.1 %shard_map.63.refs_3_ = bf16[1024,128]{1,0:T(8,128)(2,1)S(1)} custom-call(s32[3]{0:T(128)S(1)} %compare_select_fusion.1.refs_0_, bf16[1024,1024]{1,0:T(8,128)(2,1)S(1)} %get-tuple-element.40.refs_1_, bf16[256,384]{1,0:T(8,128)(2,1)S(1)} %get-tuple-element.48.refs_2_, bf16[256,384]{1,0:T(8,128)(2,1)S(1)} %collective-permute-done.25.refs_3_, ...), custom_call_target="tpu_custom_call" | custom-call | flops 10000000000 | bytes 2883590 | tf_op jit(solution)/shard_map/pallas_call | solution.py:528
  75.8 1.6 %collective-permute-done.37.refs_14_.refs_3_ = bf16[256,512]{1,0:T(8,128)(2,1)S(1)} collective-permute-done((bf16[256,512]{1,0:T(8,128)(2,1)S(1)}, bf16[256,512]{1,0:T(8,128)(2,1)S(1)}, u32[]{:S(2)}, u32[]{:S(2)}) %collective-permute-start.37) | collective-permute-done | bytes 262176 | tf_op jit(solution)/shard_map/ppermute | solution.py:522
  77.4 5.1 %collective-permute-done.16.refs_5_ = bf16[256,1024]{1,0:T(8,128)(2,1)S(1)} collective-permute-done((bf16[256,1024]{1,0:T(8,128)(2,1)S(1)}, bf16[256,1024]{1,0:T(8,128)(2,1)S(1)}, u32[]{:S(2)}, u32[]{:S(2)}) %collective-permute-start.16) | collective-permute-done | bytes 524320 | tf_op jit(solution)/shard_map/ppermute | solution.py:522
  82.6 8.4 %collective-permute-done.15.refs_4_ = bf16[256,1024]{1,0:T(8,128)(2,1)S(1)} collective-permute-done((bf16[256,1024]{1,0:T(8,128)(2,1)S(1)}, bf16[256,1024]{1,0:T(8,128)(2,1)S(1)}, u32[]{:S(2)}, u32[]{:S(2)}) %collective-permute-start.15) | collective-permute-done | bytes 524320 | tf_op jit(solution)/shard_map/ppermute | solution.py:522
  91.0 2.7 %collective-permute-done.14.refs_3_ = bf16[256,1024]{1,0:T(8,128)(2,1)S(1)} collective-permute-done((bf16[256,1024]{1,0:T(8,128)(2,1)S(1)}, bf16[256,1024]{1,0:T(8,128)(2,1)S(1)}, u32[]{:S(2)}, u32[]{:S(2)}) %collective-permute-start.14) | collective-permute-done | bytes 524320 | tf_op jit(solution)/shard_map/ppermute | solution.py:522
  93.7 2.9 %collective-permute-done.30.refs_6_ = bf16[1024,128]{1,0:T(8,128)(2,1)S(1)} collective-permute-done((bf16[1024,128]{1,0:T(8,128)(2,1)S(1)}, bf16[1024,128]{1,0:T(8,128)(2,1)S(1)}, u32[]{:S(2)}, u32[]{:S(2)}) %collective-permute-start.30) | collective-permute-done | bytes 262176 | tf_op jit(solution)/shard_map/ppermute | solution.py:522
  96.7 5.8 %collective-permute-done.29.refs_5_ = bf16[1024,128]{1,0:T(8,128)(2,1)S(1)} collective-permute-done((bf16[1024,128]{1,0:T(8,128)(2,1)S(1)}, bf16[1024,128]{1,0:T(8,128)(2,1)S(1)}, u32[]{:S(2)}, u32[]{:S(2)}) %collective-permute-start.29) | collective-permute-done | bytes 262176 | tf_op jit(solution)/shard_map/ppermute | solution.py:522
  103.9 5.8 %shard_map.60 = (f32[1024,1024]{1,0:T(8,128)S(1)}, bf16[1024,1024]{1,0:T(8,128)(2,1)S(1)}) custom-call(s32[3]{0:T(128)S(1)} %compare_select_fusion.1.refs_0_, bf16[1024,1024]{1,0:T(8,128)(2,1)S(1)} %get-tuple-element.35.refs_1_, bf16[256,1024]{1,0:T(8,128)(2,1)S(1)} %shard_map.59.refs_2_, bf16[256,1024]{1,0:T(8,128)(2,1)S(1)} %collective-permute-done.14.refs_3_, ...), custom_call_target="tpu_custom_call" | custom-call | flops 4000000000 | bytes 6291462 | tf_op jit(solution)/shard_map/pallas_call | solution.py:528
  109.8 9.1 %shard_map.64 = (bf16[512,128]{1,0:T(8,128)(2,1)S(1)}, bf16[512,128]{1,0:T(8,128)(2,1)S(1)}, bf16[256,512]{1,0:T(8,128)(2,1)S(1)}) custom-call(s32[3]{0:T(128)S(1)} %compare_select_fusion.1.refs_0_, f32[1024,1024]{1,0:T(8,128)S(1)} %get-tuple-element.38.refs_1_, bf16[1024,1024]{1,0:T(8,128)(2,1)S(1)} %get-tuple-element.39.refs_2_, ...), custom_call_target="tpu_custom_call" | custom-call | flops 17999998976 | bytes 7340038 | tf_op jit(solution)/shard_map/pallas_call | solution.py:528
  118.9 2.4 %collective-permute-start.40 = (bf16[512,128]{1,0:T(8,128)(2,1)S(1)}, bf16[512,128]{1,0:T(8,128)(2,1)S(1)}, u32[]{:S(2)}, u32[]{:S(2)}) collective-permute-start(bf16[512,128]{1,0:T(8,128)(2,1)S(1)} %get-tuple-element.52), channel_id=1, source_target_pairs={{0,18},{1,19},{2,16},{3,17},{4,22},{5,23},{6,20},{7,21},{8,26},{9,... | collective-permute-start | bytes 393224 | tf_op jit(solution)/shard_map/ppermute | solution.py:522
  123.0 3.1 %collective-permute-done.40.refs_3_.refs_5_ = bf16[512,128]{1,0:T(8,128)(2,1)S(1)} collective-permute-done((bf16[512,128]{1,0:T(8,128)(2,1)S(1)}, bf16[512,128]{1,0:T(8,128)(2,1)S(1)}, u32[]{:S(2)}, u32[]{:S(2)}) %collective-permute-start.40) | collective-permute-done | bytes 131104 | tf_op jit(solution)/shard_map/ppermute | solution.py:522
  126.0 2.4 %collective-permute-done.38.refs_1_.refs_3_ = bf16[512,128]{1,0:T(8,128)(2,1)S(1)} collective-permute-done((bf16[512,128]{1,0:T(8,128)(2,1)S(1)}, bf16[512,128]{1,0:T(8,128)(2,1)S(1)}, u32[]{:S(2)}, u32[]{:S(2)}) %collective-permute-start.38) | collective-permute-done | bytes 131104 | tf_op jit(solution)/shard_map/ppermute | solution.py:522
  132.1 2.1 %collective-permute-start.46 = (bf16[64,512]{1,0:T(8,128)(2,1)S(1)}, bf16[64,512]{1,0:T(8,128)(2,1)S(1)}, u32[]{:S(2)}, u32[]{:S(2)}) collective-permute-start(bf16[64,512]{1,0:T(8,128)(2,1)S(1)} %get-tuple-element.55), channel_id=1, source_target_pairs={{0,8},{1,9},{2,10},{3,11},{4,12},{5,13},{6,14},{7,15},{8,0},{9,1},... | collective-permute-start | bytes 196616 | tf_op jit(solution)/shard_map/ppermute | solution.py:522
  134.1 1.9 %collective-permute-start.47 = (bf16[64,512]{1,0:T(8,128)(2,1)S(1)}, bf16[64,512]{1,0:T(8,128)(2,1)S(1)}, u32[]{:S(2)}, u32[]{:S(2)}) collective-permute-start(bf16[64,512]{1,0:T(8,128)(2,1)S(1)} %get-tuple-element.56), channel_id=1, source_target_pairs={{0,12},{1,13},{2,14},{3,15},{4,8},{5,9},{6,10},{7,11},{8,4},{9,5},... | collective-permute-start | bytes 196616 | tf_op jit(solution)/shard_map/ppermute | solution.py:522
  136.7 3.9 %collective-permute-done.46.refs_3_ = bf16[64,512]{1,0:T(8,128)(2,1)S(1)} collective-permute-done((bf16[64,512]{1,0:T(8,128)(2,1)S(1)}, bf16[64,512]{1,0:T(8,128)(2,1)S(1)}, u32[]{:S(2)}, u32[]{:S(2)}) %collective-permute-start.46) | collective-permute-done | bytes 65568 | tf_op jit(solution)/shard_map/ppermute | solution.py:522
  (79 shorter events, 18.7 us)
Async XLA Ops:
  1.9 11.1 %collective-permute-start.21 = (bf16[4,64,384]{2,1,0:T(8,128)(2,1)S(1)}, bf16[4,64,384]{2,1,0:T(8,128)(2,1)S(1)}, u32[]{:S(2)}, u32[]{:S(2)}) collective-permute-start(bf16[4,64,384]{2,1,0:T(8,128)(2,1)S(1)} %get-tuple-element.43), channel_id=1, source_target_pairs={{0,1},{1,0},{2,3},{3,2},{4,5},{5,4},{6,7},{7,6},{8,9},{9,8},{10,11... | collective-permute-start | bytes 589832 | tf_op jit(solution)/shard_map/ppermute | solution.py:522
  5.0 9.6 %collective-permute-start = (bf16[32,1024]{1,0:T(8,128)(2,1)S(1)}, bf16[32,1024]{1,0:T(8,128)(2,1)S(1)}, u32[]{:S(2)}, u32[]{:S(2)}) collective-permute-start(bf16[32,1024]{1,0:T(8,128)(2,1)S(1)} %get-tuple-element.32), channel_id=1, source_target_pairs={{0,4},{1,5},{2,6},{3,7},{4,0},{5,1},{6,2},{7,3},{8,12},{9,13},{10,... | collective-permute-start | bytes 196616 | tf_op jit(solution)/shard_map/ppermute | solution.py:522
  6.6 8.1 %collective-permute-start.1 = (bf16[32,1024]{1,0:T(8,128)(2,1)S(1)}, bf16[32,1024]{1,0:T(8,128)(2,1)S(1)}, u32[]{:S(2)}, u32[]{:S(2)}) collective-permute-start(bf16[32,1024]{1,0:T(8,128)(2,1)S(1)} %get-tuple-element.33), channel_id=1, source_target_pairs={{0,8},{1,9},{2,10},{3,11},{4,12},{5,13},{6,14},{7,15},{8,0},{9,1},... | collective-permute-start | bytes 196616 | tf_op jit(solution)/shard_map/ppermute | solution.py:522
  10.4 10.8 %collective-permute-start.12 = (bf16[64,1024]{1,0:T(8,128)(2,1)S(1)}, bf16[64,1024]{1,0:T(8,128)(2,1)S(1)}, u32[]{:S(2)}, u32[]{:S(2)}) collective-permute-start(bf16[64,1024]{1,0:T(8,128)(2,1)S(1)} %get-tuple-element.37.refs_0_), channel_id=1, source_target_pairs={{0,8},{1,9},{2,10},{3,11},{4,12},{5,13},{6,14},{7,15},{8,0},{9,1},... | collective-permute-start | bytes 393224 | tf_op jit(solution)/shard_map/ppermute | solution.py:522
  13.0 8.2 %collective-permute-start.22 = (bf16[128,384]{1,0:T(8,128)(2,1)S(1)}, bf16[128,384]{1,0:T(8,128)(2,1)S(1)}, u32[]{:S(2)}, u32[]{:S(2)}) collective-permute-start(bf16[128,384]{1,0:T(8,128)(2,1)S(1)} %get-tuple-element.45), channel_id=1, source_target_pairs={{0,2},{1,3},{2,0},{3,1},{4,6},{5,7},{6,4},{7,5},{8,10},{9,11},{10,... | collective-permute-start | bytes 294920 | tf_op jit(solution)/shard_map/ppermute | solution.py:522
  16.0 18.4 %collective-permute-start.5 = (bf16[128,1024]{1,0:T(8,128)(2,1)S(1)}, bf16[128,1024]{1,0:T(8,128)(2,1)S(1)}, u32[]{:S(2)}, u32[]{:S(2)}) collective-permute-start(bf16[128,1024]{1,0:T(8,128)(2,1)S(1)} %shard_map.56.refs_1_), channel_id=1, source_target_pairs={{0,18},{1,19},{2,16},{3,17},{4,22},{5,23},{6,20},{7,21},{8,26},{9,... | collective-permute-start | bytes 786440 | tf_op jit(solution)/shard_map/ppermute | solution.py:522
  16.9 22.0 %collective-permute-start.4 = (bf16[128,1024]{1,0:T(8,128)(2,1)S(1)}, bf16[128,1024]{1,0:T(8,128)(2,1)S(1)}, u32[]{:S(2)}, u32[]{:S(2)}) collective-permute-start(bf16[128,1024]{1,0:T(8,128)(2,1)S(1)} %shard_map.56.refs_1_), channel_id=1, source_target_pairs={{0,16},{1,17},{2,18},{3,19},{4,20},{5,21},{6,22},{7,23},{8,24},{9,... | collective-permute-start | bytes 786440 | tf_op jit(solution)/shard_map/ppermute | solution.py:522
  19.1 12.7 %collective-permute-start.23 = (bf16[128,384]{1,0:T(8,128)(2,1)S(1)}, bf16[128,384]{1,0:T(8,128)(2,1)S(1)}, u32[]{:S(2)}, u32[]{:S(2)}) collective-permute-start(bf16[128,384]{1,0:T(8,128)(2,1)S(1)} %get-tuple-element.46), channel_id=1, source_target_pairs={{0,16},{1,17},{2,18},{3,19},{4,20},{5,21},{6,22},{7,23},{8,24},{9,... | collective-permute-start | bytes 294920 | tf_op jit(solution)/shard_map/ppermute | solution.py:522
  21.2 17.6 %collective-permute-start.6 = (bf16[128,1024]{1,0:T(8,128)(2,1)S(1)}, bf16[128,1024]{1,0:T(8,128)(2,1)S(1)}, u32[]{:S(2)}, u32[]{:S(2)}) collective-permute-start(bf16[128,1024]{1,0:T(8,128)(2,1)S(1)} %shard_map.56.refs_1_), channel_id=1, source_target_pairs={{0,1},{1,0},{2,3},{3,2},{4,5},{5,4},{6,7},{7,6},{8,9},{9,8},{10,11... | collective-permute-start | bytes 786440 | tf_op jit(solution)/shard_map/ppermute | solution.py:522
  21.2 11.8 %collective-permute-start.24 = (bf16[128,384]{1,0:T(8,128)(2,1)S(1)}, bf16[128,384]{1,0:T(8,128)(2,1)S(1)}, u32[]{:S(2)}, u32[]{:S(2)}) collective-permute-start(bf16[128,384]{1,0:T(8,128)(2,1)S(1)} %get-tuple-element.47), channel_id=1, source_target_pairs={{0,18},{1,19},{2,16},{3,17},{4,22},{5,23},{6,20},{7,21},{8,26},{9,... | collective-permute-start | bytes 294920 | tf_op jit(solution)/shard_map/ppermute | solution.py:522
  34.4 13.8 %collective-permute-start.9 = (bf16[128,1024]{1,0:T(8,128)(2,1)S(1)}, bf16[128,1024]{1,0:T(8,128)(2,1)S(1)}, u32[]{:S(2)}, u32[]{:S(2)}) collective-permute-start(bf16[128,1024]{1,0:T(8,128)(2,1)S(1)} %collective-permute-done.5.refs_4_), channel_id=1, source_target_pairs={{0,1},{1,0},{2,3},{3,2},{4,5},{5,4},{6,7},{7,6},{8,9},{9,8},{10,11... | collective-permute-start | bytes 786440 | tf_op jit(solution)/shard_map/ppermute | solution.py:522
  36.8 11.4 %collective-permute-start.26 = (bf16[256,384]{1,0:T(8,128)(2,1)S(1)}, bf16[256,384]{1,0:T(8,128)(2,1)S(1)}, u32[]{:S(2)}, u32[]{:S(2)}) collective-permute-start(bf16[256,384]{1,0:T(8,128)(2,1)S(1)} %get-tuple-element.48.refs_2_), channel_id=1, source_target_pairs={{0,8},{1,9},{2,10},{3,11},{4,12},{5,13},{6,14},{7,15},{8,0},{9,1},... | collective-permute-start | bytes 589832 | tf_op jit(solution)/shard_map/ppermute | solution.py:522
  38.8 11.4 %collective-permute-start.8 = (bf16[128,1024]{1,0:T(8,128)(2,1)S(1)}, bf16[128,1024]{1,0:T(8,128)(2,1)S(1)}, u32[]{:S(2)}, u32[]{:S(2)}) collective-permute-start(bf16[128,1024]{1,0:T(8,128)(2,1)S(1)} %collective-permute-done.4.refs_3_), channel_id=1, source_target_pairs={{0,1},{1,0},{2,3},{3,2},{4,5},{5,4},{6,7},{7,6},{8,9},{9,8},{10,11... | collective-permute-start | bytes 786440 | tf_op jit(solution)/shard_map/ppermute | solution.py:522
  38.9 9.4 %collective-permute-start.13 = (bf16[64,1024]{1,0:T(8,128)(2,1)S(1)}, bf16[64,1024]{1,0:T(8,128)(2,1)S(1)}, u32[]{:S(2)}, u32[]{:S(2)}) collective-permute-start(bf16[64,1024]{1,0:T(8,128)(2,1)S(1)} %collective-permute-done.12.refs_2_), channel_id=1, source_target_pairs={{0,4},{1,5},{2,6},{3,7},{4,0},{5,1},{6,2},{7,3},{8,12},{9,13},{10,... | collective-permute-start | bytes 393224 | tf_op jit(solution)/shard_map/ppermute | solution.py:522
  39.4 11.0 %collective-permute-start.7 = (bf16[128,1024]{1,0:T(8,128)(2,1)S(1)}, bf16[128,1024]{1,0:T(8,128)(2,1)S(1)}, u32[]{:S(2)}, u32[]{:S(2)}) collective-permute-start(bf16[128,1024]{1,0:T(8,128)(2,1)S(1)} %collective-permute-done.3.refs_2_), channel_id=1, source_target_pairs={{0,1},{1,0},{2,3},{3,2},{4,5},{5,4},{6,7},{7,6},{8,9},{9,8},{10,11... | collective-permute-start | bytes 786440 | tf_op jit(solution)/shard_map/ppermute | solution.py:522
  48.2 18.7 %collective-permute-start.36 = (bf16[256,512]{1,0:T(8,128)(2,1)S(1)}, bf16[256,512]{1,0:T(8,128)(2,1)S(1)}, u32[]{:S(2)}, u32[]{:S(2)}) collective-permute-start(bf16[256,512]{1,0:T(8,128)(2,1)S(1)} %get-tuple-element.49.refs_11_.refs_0_), channel_id=1, source_target_pairs={{0,8},{1,9},{2,10},{3,11},{4,12},{5,13},{6,14},{7,15},{8,0},{9,1},... | collective-permute-start | bytes 786440 | tf_op jit(solution)/shard_map/ppermute | solution.py:522
  48.2 20.6 %collective-permute-start.35 = (bf16[256,512]{1,0:T(8,128)(2,1)S(1)}, bf16[256,512]{1,0:T(8,128)(2,1)S(1)}, u32[]{:S(2)}, u32[]{:S(2)}) collective-permute-start(bf16[256,512]{1,0:T(8,128)(2,1)S(1)} %get-tuple-element.49.refs_11_.refs_0_), channel_id=1, source_target_pairs={{0,4},{1,5},{2,6},{3,7},{4,0},{5,1},{6,2},{7,3},{8,12},{9,13},{10,... | collective-permute-start | bytes 786440 | tf_op jit(solution)/shard_map/ppermute | solution.py:522
  48.2 18.6 %collective-permute-start.25 = (bf16[256,384]{1,0:T(8,128)(2,1)S(1)}, bf16[256,384]{1,0:T(8,128)(2,1)S(1)}, u32[]{:S(2)}, u32[]{:S(2)}) collective-permute-start(bf16[256,384]{1,0:T(8,128)(2,1)S(1)} %get-tuple-element.48.refs_2_), channel_id=1, source_target_pairs={{0,4},{1,5},{2,6},{3,7},{4,0},{5,1},{6,2},{7,3},{8,12},{9,13},{10,... | collective-permute-start | bytes 589832 | tf_op jit(solution)/shard_map/ppermute | solution.py:522
  50.3 20.1 %collective-permute-start.27 = (bf16[256,384]{1,0:T(8,128)(2,1)S(1)}, bf16[256,384]{1,0:T(8,128)(2,1)S(1)}, u32[]{:S(2)}, u32[]{:S(2)}) collective-permute-start(bf16[256,384]{1,0:T(8,128)(2,1)S(1)} %collective-permute-done.26.refs_4_), channel_id=1, source_target_pairs={{0,4},{1,5},{2,6},{3,7},{4,0},{5,1},{6,2},{7,3},{8,12},{9,13},{10,... | collective-permute-start | bytes 589832 | tf_op jit(solution)/shard_map/ppermute | solution.py:522
  50.4 43.3 %collective-permute-start.17 = (bf16[256,1024]{1,0:T(8,128)(2,1)S(1)}, bf16[256,1024]{1,0:T(8,128)(2,1)S(1)}, u32[]{:S(2)}, u32[]{:S(2)}) collective-permute-start(bf16[256,1024]{1,0:T(8,128)(2,1)S(1)} %shard_map.59.refs_2_), channel_id=1, source_target_pairs={{0,1},{1,0},{2,3},{3,2},{4,5},{5,4},{6,7},{7,6},{8,9},{9,8},{10,11... | collective-permute-start | bytes 1572872 | tf_op jit(solution)/shard_map/ppermute | solution.py:522
  66.9 15.7 %collective-permute-start.16 = (bf16[256,1024]{1,0:T(8,128)(2,1)S(1)}, bf16[256,1024]{1,0:T(8,128)(2,1)S(1)}, u32[]{:S(2)}, u32[]{:S(2)}) collective-permute-start(bf16[256,1024]{1,0:T(8,128)(2,1)S(1)} %shard_map.59.refs_2_), channel_id=1, source_target_pairs={{0,18},{1,19},{2,16},{3,17},{4,22},{5,23},{6,20},{7,21},{8,26},{9,... | collective-permute-start | bytes 1572872 | tf_op jit(solution)/shard_map/ppermute | solution.py:522
  66.9 24.1 %collective-permute-start.15 = (bf16[256,1024]{1,0:T(8,128)(2,1)S(1)}, bf16[256,1024]{1,0:T(8,128)(2,1)S(1)}, u32[]{:S(2)}, u32[]{:S(2)}) collective-permute-start(bf16[256,1024]{1,0:T(8,128)(2,1)S(1)} %shard_map.59.refs_2_), channel_id=1, source_target_pairs={{0,16},{1,17},{2,18},{3,19},{4,20},{5,21},{6,22},{7,23},{8,24},{9,... | collective-permute-start | bytes 1572872 | tf_op jit(solution)/shard_map/ppermute | solution.py:522
  68.9 24.9 %collective-permute-start.14 = (bf16[256,1024]{1,0:T(8,128)(2,1)S(1)}, bf16[256,1024]{1,0:T(8,128)(2,1)S(1)}, u32[]{:S(2)}, u32[]{:S(2)}) collective-permute-start(bf16[256,1024]{1,0:T(8,128)(2,1)S(1)} %shard_map.59.refs_2_), channel_id=1, source_target_pairs={{0,2},{1,3},{2,0},{3,1},{4,6},{5,7},{6,4},{7,5},{8,10},{9,11},{10,... | collective-permute-start | bytes 1572872 | tf_op jit(solution)/shard_map/ppermute | solution.py:522
  77.4 19.2 %collective-permute-start.30 = (bf16[1024,128]{1,0:T(8,128)(2,1)S(1)}, bf16[1024,128]{1,0:T(8,128)(2,1)S(1)}, u32[]{:S(2)}, u32[]{:S(2)}) collective-permute-start(bf16[1024,128]{1,0:T(8,128)(2,1)S(1)} %shard_map.63.refs_3_), channel_id=1, source_target_pairs={{0,18},{1,19},{2,16},{3,17},{4,22},{5,23},{6,20},{7,21},{8,26},{9,... | collective-permute-start | bytes 786440 | tf_op jit(solution)/shard_map/ppermute | solution.py:522
  82.6 20.7 %collective-permute-start.20 = (bf16[256,1024]{1,0:T(8,128)(2,1)S(1)}, bf16[256,1024]{1,0:T(8,128)(2,1)S(1)}, u32[]{:S(2)}, u32[]{:S(2)}) collective-permute-start(bf16[256,1024]{1,0:T(8,128)(2,1)S(1)} %collective-permute-done.16.refs_5_), channel_id=1, source_target_pairs={{0,1},{1,0},{2,3},{3,2},{4,5},{5,4},{6,7},{7,6},{8,9},{9,8},{10,11... | collective-permute-start | bytes 1572872 | tf_op jit(solution)/shard_map/ppermute | solution.py:522
  91.0 12.4 %collective-permute-start.19 = (bf16[256,1024]{1,0:T(8,128)(2,1)S(1)}, bf16[256,1024]{1,0:T(8,128)(2,1)S(1)}, u32[]{:S(2)}, u32[]{:S(2)}) collective-permute-start(bf16[256,1024]{1,0:T(8,128)(2,1)S(1)} %collective-permute-done.15.refs_4_), channel_id=1, source_target_pairs={{0,1},{1,0},{2,3},{3,2},{4,5},{5,4},{6,7},{7,6},{8,9},{9,8},{10,11... | collective-permute-start | bytes 1572872 | tf_op jit(solution)/shard_map/ppermute | solution.py:522
  93.7 10.1 %collective-permute-start.18 = (bf16[256,1024]{1,0:T(8,128)(2,1)S(1)}, bf16[256,1024]{1,0:T(8,128)(2,1)S(1)}, u32[]{:S(2)}, u32[]{:S(2)}) collective-permute-start(bf16[256,1024]{1,0:T(8,128)(2,1)S(1)} %collective-permute-done.14.refs_3_), channel_id=1, source_target_pairs={{0,1},{1,0},{2,3},{3,2},{4,5},{5,4},{6,7},{7,6},{8,9},{9,8},{10,11... | collective-permute-start | bytes 1572872 | tf_op jit(solution)/shard_map/ppermute | solution.py:522
  93.7 8.7 %collective-permute-start.29 = (bf16[1024,128]{1,0:T(8,128)(2,1)S(1)}, bf16[1024,128]{1,0:T(8,128)(2,1)S(1)}, u32[]{:S(2)}, u32[]{:S(2)}) collective-permute-start(bf16[1024,128]{1,0:T(8,128)(2,1)S(1)} %shard_map.63.refs_3_), channel_id=1, source_target_pairs={{0,16},{1,17},{2,18},{3,19},{4,20},{5,21},{6,22},{7,23},{8,24},{9,... | collective-permute-start | bytes 786440 | tf_op jit(solution)/shard_map/ppermute | solution.py:522
  102.4 7.3 %collective-permute-start.31 = (bf16[1024,128]{1,0:T(8,128)(2,1)S(1)}, bf16[1024,128]{1,0:T(8,128)(2,1)S(1)}, u32[]{:S(2)}, u32[]{:S(2)}) collective-permute-start(bf16[1024,128]{1,0:T(8,128)(2,1)S(1)} %shard_map.63.refs_3_), channel_id=1, source_target_pairs={{0,1},{1,0},{2,3},{3,2},{4,5},{5,4},{6,7},{7,6},{8,9},{9,8},{10,11... | collective-permute-start | bytes 786440 | tf_op jit(solution)/shard_map/ppermute | solution.py:522
  103.0 19.5 %collective-permute-start.42 = (bf16[256,512]{1,0:T(8,128)(2,1)S(1)}, bf16[256,512]{1,0:T(8,128)(2,1)S(1)}, u32[]{:S(2)}, u32[]{:S(2)}) collective-permute-start(bf16[256,512]{1,0:T(8,128)(2,1)S(1)} %shard_map.66.refs_7_), channel_id=1, source_target_pairs={{0,2},{1,3},{2,0},{3,1},{4,6},{5,7},{6,4},{7,5},{8,10},{9,11},{10,... | collective-permute-start | bytes 786440 | tf_op jit(solution)/shard_map/ppermute | solution.py:522
  121.3 7.2 %collective-permute-start.38 = (bf16[512,128]{1,0:T(8,128)(2,1)S(1)}, bf16[512,128]{1,0:T(8,128)(2,1)S(1)}, u32[]{:S(2)}, u32[]{:S(2)}) collective-permute-start(bf16[512,128]{1,0:T(8,128)(2,1)S(1)} %get-tuple-element.52), channel_id=1, source_target_pairs={{0,2},{1,3},{2,0},{3,1},{4,6},{5,7},{6,4},{7,5},{8,10},{9,11},{10,... | collective-permute-start | bytes 393224 | tf_op jit(solution)/shard_map/ppermute | solution.py:522
  132.1 8.5 %collective-permute-start.46 = (bf16[64,512]{1,0:T(8,128)(2,1)S(1)}, bf16[64,512]{1,0:T(8,128)(2,1)S(1)}, u32[]{:S(2)}, u32[]{:S(2)}) collective-permute-start(bf16[64,512]{1,0:T(8,128)(2,1)S(1)} %get-tuple-element.55), channel_id=1, source_target_pairs={{0,8},{1,9},{2,10},{3,11},{4,12},{5,13},{6,14},{7,15},{8,0},{9,1},... | collective-permute-start | bytes 196616 | tf_op jit(solution)/shard_map/ppermute | solution.py:522
  (16 other events, 97.4 us)

commit v5 on v4

--- a/solution.py
+++ b/solution.py
@@ -205,7 +205,7 @@
         if sections != 2 or windows & (windows - 1) or seq_count % (2 * windows):
             return False
         inner = seq_count // windows
-        if inner & (inner - 1) or features % (sections * inner * 2 * HEAD_DIM):
+        if inner != 4 or features % (sections * inner * 2 * HEAD_DIM):
             return False
         return features == HEADS * HEAD_DIM and tok_rows % 32 == 0
 
@@ -213,9 +213,8 @@
         return mx * self.seq_count + mz * self.inner + mi
 
 
-def attention(qkv, out, cols):
+def attention(queries, qkv, out, cols):
     lane_head = lax.broadcasted_iota(jnp.int32, (1, cols), 1) // HEAD_DIM
-    queries = qkv[:, 0:cols]
     keys_in = qkv[:, cols : 2 * cols]
     values_in = qkv[:, 2 * cols : 3 * cols]
     mixed = jnp.zeros(queries.shape, jnp.float32)
@@ -400,7 +399,7 @@
         qkv[rows, :] = project_rows(normed[rows, :], w_qkv[...], plan.cols)
 
     row_blocks(plan, one_block)
-    attention(qkv, out, plan.cols)
+    attention(qkv[:, 0 : plan.cols], qkv, out, plan.cols)
 
 
 def fold_kernel(plan, where, hid, *rest):
@@ -434,8 +433,7 @@
     slots, windows = (plan.slots, plan.windows)
     attended_in, rest = (rest[:slots], rest[slots:])
     pieces, rest = (rest[:windows], rest[windows:])
-    outs, rest = (rest[: plan.inner // 2], rest[plan.inner // 2 :])
-    kept, att, w_qkv, joined, qkv, mixed = rest
+    out, kept, qkv, att, w_qkv, joined = rest
     for piece, (mx, mi) in zip(attended_in, plane_order(plan)):
         att[:, aligned(slot_of(plan, where, mx, mi), plan.cols)] = piece[...]
     gather_weights(plan, where, pieces, w_qkv)
@@ -450,15 +448,26 @@
         )
 
     row_blocks(plan, one_block)
-    attention(qkv, mixed, plan.cols)
     lanes = aligned(where[0], width)
     for side in range(plan.sections):
-        for mi in range(plan.inner):
-            part = aligned(side * plan.inner + (where[2] ^ mi), plan.shard)
-            start = ((mi % 2) * plan.sections + side) * plan.shard
-            outs[mi // 2][start : start + plan.shard, :] = mixed[part, :]
-            if mi == 0:
-                kept[side * plan.shard : (side + 1) * plan.shard, :] = joined[part, lanes]
+        part = aligned(side * plan.inner + where[2], plan.shard)
+        kept[side * plan.shard : (side + 1) * plan.shard, :] = joined[part, lanes]
+    attention(chip_queries(plan, where, qkv, 2), qkv, out, plan.cols)
+
+
+def chip_queries(plan, where, qkv, mi):
+    return jnp.concatenate(
+        [
+            qkv[aligned(side * plan.inner + (where[2] ^ mi ^ core), plan.shard), 0 : plan.cols]
+            for core in range(2)
+            for side in range(plan.sections)
+        ],
+        axis=0,
+    )
+
+
+def rest_kernel(plan, where, qkv, out):
+    attention(chip_queries(plan, where, qkv, 0), qkv, out, plan.cols)
 
 
 def third_kernel(plan, where, kept, *rest):
@@ -648,20 +657,32 @@
     (last,) = call(lambda *refs: last_kernel(plan, *refs), [(plan.group, width)], pieces_b, limit=8)
     last = [last] + [swap(last, plan.mask(mi=mi)) for mi in range(2, inner, 2)]
     last = core_gather(last)
-    *attended, kept = call(
+    far_rows, kept, qkv = call(
         lambda *refs: second_kernel(plan, *refs),
-        [(2 * plan.sections * shard, cols)] * (inner // 2) + [(plan.sections * shard, width)],
+        [
+            (2 * plan.sections * shard, cols),
+            (plan.sections * shard, width),
+            (tokens, 3 * cols),
+        ],
         [where, merged, folded] + attended + pieces_b,
         [
             pltpu.VMEM((tokens, features), bf16),
             pltpu.VMEM((features, 3 * cols), bf16),
             pltpu.VMEM((tokens, features), bf16),
-            pltpu.VMEM((tokens, 3 * cols), bf16),
-            pltpu.VMEM((tokens, cols), bf16),
         ],
         [smem] + [vmem] * (2 + plan.slots + windows),
-        flops=18_000_000_000,
-    )
+        flops=12_000_000_000,
+    )
+    (near_rows,) = call(
+        lambda *refs: rest_kernel(plan, *refs),
+        [far_rows.shape],
+        [where, qkv],
+        (),
+        [smem, vmem],
+        flops=6_000_000_000,
+        limit=20,
+    )
+    attended = [near_rows, far_rows]
     back = [attended[0]] + [
         swap(attended[mi // 2], plan.mask(mx=mx, mi=mi))
         for chip_no, (mx, mi) in enumerate(plan.chips)

time: 142 us -> 144 us (1.014)
    pallas_call x14 -> x15, Pallas kernels: 28.1 us -> 29.2 us  [call(): pl.pallas_call(kernel, out_shape=shapes, in_specs=specs or [vmem] * len(i...]
where the time goes in v5:
time: 144 us
  waiting for transfers between devices  76.8 us (53%)
  starting transfers between devices  37.8 us (26%)
  Pallas kernels  29.2 us (20%)
    ppermute x48, waiting for transfers between devices, swap(): return lax.ppermute(value, ('section', 'seq'), pairs)  76.8 us
    ppermute x48, starting transfers between devices, swap(): return lax.ppermute(value, ('section', 'seq'), pairs)  37.8 us
    pallas_call x15, Pallas kernels, call(): pl.pallas_call(kernel, out_shape=shapes, in_specs=specs or [vmem] * len(i...  29.2 us
  transfers between devices with their start and end apart: 48, of which 20 were waited for; matrix products, arithmetic and copies ran while one was open for 0% of the time, Pallas kernels for 17%

profile of v5, /device:TPU:0, one launch (start us, length us, event | category | flops | bytes accessed | tf_op | source)
XLA Modules:
  0.0 144.1 jit_solution(15248236496900438043)
XLA Ops:
  0.0 1.9 %shard_map.55 = (bf16[32,1024]{1,0:T(8,128)(2,1)S(1)}, bf16[32,1024]{1,0:T(8,128)(2,1)S(1)}, bf16[32,1024]{1,0:T(8,128)(2,1)S(1)}, bf16[32,1024]{1,0:T(8,128)(2,...) custom-call(s32[3]{0:T(128)S(1)} %compare_select_fusion.1.refs_0_, ...), custom_call_target="tpu_custom_call" | custom-call | bytes 1181702 | tf_op jit(solution)/shard_map/pallas_call | solution.py:537
  2.4 2.6 %collective-permute-start.10 = (bf16[128,512]{1,0:T(8,128)(2,1)S(1)}, bf16[128,512]{1,0:T(8,128)(2,1)S(1)}, u32[]{:S(2)}, u32[]{:S(2)}) collective-permute-start(bf16[128,512]{1,0:T(8,128)(2,1)S(1)} %get-tuple-element.36), channel_id=1, source_target_pairs={{0,16},{1,17},{2,18},{3,19},{4,20},{5,21},{6,22},{7,23},{8,24},{9,... | collective-permute-start | bytes 393224 | tf_op jit(solution)/shard_map/ppermute | solution.py:531
  6.6 2.6 %collective-permute-start.1 = (bf16[32,1024]{1,0:T(8,128)(2,1)S(1)}, bf16[32,1024]{1,0:T(8,128)(2,1)S(1)}, u32[]{:S(2)}, u32[]{:S(2)}) collective-permute-start(bf16[32,1024]{1,0:T(8,128)(2,1)S(1)} %get-tuple-element.33), channel_id=1, source_target_pairs={{0,8},{1,9},{2,10},{3,11},{4,12},{5,13},{6,14},{7,15},{8,0},{9,1},... | collective-permute-start | bytes 196616 | tf_op jit(solution)/shard_map/ppermute | solution.py:531
  10.4 2.6 %collective-permute-start.12 = (bf16[64,1024]{1,0:T(8,128)(2,1)S(1)}, bf16[64,1024]{1,0:T(8,128)(2,1)S(1)}, u32[]{:S(2)}, u32[]{:S(2)}) collective-permute-start(bf16[64,1024]{1,0:T(8,128)(2,1)S(1)} %get-tuple-element.37.refs_0_), channel_id=1, source_target_pairs={{0,8},{1,9},{2,10},{3,11},{4,12},{5,13},{6,14},{7,15},{8,0},{9,1},... | collective-permute-start | bytes 393224 | tf_op jit(solution)/shard_map/ppermute | solution.py:531
  13.0 1.6 %collective-permute-start.22 = (bf16[128,384]{1,0:T(8,128)(2,1)S(1)}, bf16[128,384]{1,0:T(8,128)(2,1)S(1)}, u32[]{:S(2)}, u32[]{:S(2)}) collective-permute-start(bf16[128,384]{1,0:T(8,128)(2,1)S(1)} %get-tuple-element.45), channel_id=1, source_target_pairs={{0,2},{1,3},{2,0},{3,1},{4,6},{5,7},{6,4},{7,5},{8,10},{9,11},{10,... | collective-permute-start | bytes 294920 | tf_op jit(solution)/shard_map/ppermute | solution.py:531
  16.9 2.2 %collective-permute-start.4 = (bf16[128,1024]{1,0:T(8,128)(2,1)S(1)}, bf16[128,1024]{1,0:T(8,128)(2,1)S(1)}, u32[]{:S(2)}, u32[]{:S(2)}) collective-permute-start(bf16[128,1024]{1,0:T(8,128)(2,1)S(1)} %shard_map.56.refs_1_), channel_id=1, source_target_pairs={{0,16},{1,17},{2,18},{3,19},{4,20},{5,21},{6,22},{7,23},{8,24},{9,... | collective-permute-start | bytes 786440 | tf_op jit(solution)/shard_map/ppermute | solution.py:531
  19.1 2.1 %collective-permute-done.12.refs_2_ = bf16[64,1024]{1,0:T(8,128)(2,1)S(1)} collective-permute-done((bf16[64,1024]{1,0:T(8,128)(2,1)S(1)}, bf16[64,1024]{1,0:T(8,128)(2,1)S(1)}, u32[]{:S(2)}, u32[]{:S(2)}) %collective-permute-start.12) | collective-permute-done | bytes 131104 | tf_op jit(solution)/shard_map/ppermute | solution.py:531
  21.2 2.8 %collective-permute-start.24 = (bf16[128,384]{1,0:T(8,128)(2,1)S(1)}, bf16[128,384]{1,0:T(8,128)(2,1)S(1)}, u32[]{:S(2)}, u32[]{:S(2)}) collective-permute-start(bf16[128,384]{1,0:T(8,128)(2,1)S(1)} %get-tuple-element.47), channel_id=1, source_target_pairs={{0,18},{1,19},{2,16},{3,17},{4,22},{5,23},{6,20},{7,21},{8,26},{9,... | collective-permute-start | bytes 294920 | tf_op jit(solution)/shard_map/ppermute | solution.py:531
  24.0 7.8 %collective-permute-done.23.refs_4_ = bf16[128,384]{1,0:T(8,128)(2,1)S(1)} collective-permute-done((bf16[128,384]{1,0:T(8,128)(2,1)S(1)}, bf16[128,384]{1,0:T(8,128)(2,1)S(1)}, u32[]{:S(2)}, u32[]{:S(2)}) %collective-permute-start.23) | collective-permute-done | bytes 98336 | tf_op jit(solution)/shard_map/ppermute | solution.py:531
  35.0 1.8 %collective-permute-done.11.refs_1_ = bf16[64,1024]{1,0:T(8,128)(2,1)S(1)} collective-permute-done((bf16[64,1024]{1,0:T(8,128)(2,1)S(1)}, bf16[64,1024]{1,0:T(8,128)(2,1)S(1)}, u32[]{:S(2)}, u32[]{:S(2)}) %collective-permute-start.11) | collective-permute-done | bytes 131104 | tf_op jit(solution)/shard_map/ppermute | solution.py:531
  36.8 2.0 %collective-permute-start.26 = (bf16[256,384]{1,0:T(8,128)(2,1)S(1)}, bf16[256,384]{1,0:T(8,128)(2,1)S(1)}, u32[]{:S(2)}, u32[]{:S(2)}) collective-permute-start(bf16[256,384]{1,0:T(8,128)(2,1)S(1)} %get-tuple-element.48.refs_2_), channel_id=1, source_target_pairs={{0,8},{1,9},{2,10},{3,11},{4,12},{5,13},{6,14},{7,15},{8,0},{9,1},... | collective-permute-start | bytes 589832 | tf_op jit(solution)/shard_map/ppermute | solution.py:531
  39.4 8.8 %collective-permute-done.13.refs_3_ = bf16[64,1024]{1,0:T(8,128)(2,1)S(1)} collective-permute-done((bf16[64,1024]{1,0:T(8,128)(2,1)S(1)}, bf16[64,1024]{1,0:T(8,128)(2,1)S(1)}, u32[]{:S(2)}, u32[]{:S(2)}) %collective-permute-start.13) | collective-permute-done | bytes 131104 | tf_op jit(solution)/shard_map/ppermute | solution.py:531
  48.2 2.0 %collective-permute-start.25 = (bf16[256,384]{1,0:T(8,128)(2,1)S(1)}, bf16[256,384]{1,0:T(8,128)(2,1)S(1)}, u32[]{:S(2)}, u32[]{:S(2)}) collective-permute-start(bf16[256,384]{1,0:T(8,128)(2,1)S(1)} %get-tuple-element.48.refs_2_), channel_id=1, source_target_pairs={{0,4},{1,5},{2,6},{3,7},{4,0},{5,1},{6,2},{7,3},{8,12},{9,13},{10,... | collective-permute-start | bytes 589832 | tf_op jit(solution)/shard_map/ppermute | solution.py:531
  50.5 2.0 %shard_map.57 = (bf16[1024,1024]{1,0:T(8,128)(2,1)S(1)}, bf16[1024,1024]{1,0:T(8,128)(2,1)S(1)}) custom-call(s32[3]{0:T(128)S(1)} %compare_select_fusion.1.refs_0_, bf16[128,1024]{1,0:T(8,128)(2,1)S(1)} %shard_map.56.refs_1_, bf16[128,1024]{1,0:T(8,128)(2,1)S(1)} %collective-permute-done.3.refs_2_, bf16[128,1024]{1,0:T(8,128)(2,1)S(1)} %collective-permute-done.4.refs_3_, ...), custom_call_target="tpu_custom_call" | custom-call | bytes 2097158 | tf_op jit(solution)/shard_map/pallas_call | solution.py:537
  52.5 14.4 %collective-permute-done.25.refs_3_ = bf16[256,384]{1,0:T(8,128)(2,1)S(1)} collective-permute-done((bf16[256,384]{1,0:T(8,128)(2,1)S(1)}, bf16[256,384]{1,0:T(8,128)(2,1)S(1)}, u32[]{:S(2)}, u32[]{:S(2)}) %collective-permute-start.25) | collective-permute-done | bytes 196640 | tf_op jit(solution)/shard_map/ppermute | solution.py:531
  66.9 1.9 %collective-permute-start.15 = (bf16[256,1024]{1,0:T(8,128)(2,1)S(1)}, bf16[256,1024]{1,0:T(8,128)(2,1)S(1)}, u32[]{:S(2)}, u32[]{:S(2)}) collective-permute-start(bf16[256,1024]{1,0:T(8,128)(2,1)S(1)} %shard_map.59.refs_2_), channel_id=1, source_target_pairs={{0,16},{1,17},{2,18},{3,19},{4,20},{5,21},{6,22},{7,23},{8,24},{9,... | collective-permute-start | bytes 1572872 | tf_op jit(solution)/shard_map/ppermute | solution.py:531
  70.7 5.1 %shard_map.63.refs_3_ = bf16[1024,128]{1,0:T(8,128)(2,1)S(1)} custom-call(s32[3]{0:T(128)S(1)} %compare_select_fusion.1.refs_0_, bf16[1024,1024]{1,0:T(8,128)(2,1)S(1)} %get-tuple-element.40.refs_1_, bf16[256,384]{1,0:T(8,128)(2,1)S(1)} %get-tuple-element.48.refs_2_, bf16[256,384]{1,0:T(8,128)(2,1)S(1)} %collective-permute-done.25.refs_3_, ...), custom_call_target="tpu_custom_call" | custom-call | flops 10000000000 | bytes 2883590 | tf_op jit(solution)/shard_map/pallas_call | solution.py:537
  75.8 1.6 %collective-permute-done.37.refs_14_.refs_3_ = bf16[256,512]{1,0:T(8,128)(2,1)S(1)} collective-permute-done((bf16[256,512]{1,0:T(8,128)(2,1)S(1)}, bf16[256,512]{1,0:T(8,128)(2,1)S(1)}, u32[]{:S(2)}, u32[]{:S(2)}) %collective-permute-start.37) | collective-permute-done | bytes 262176 | tf_op jit(solution)/shard_map/ppermute | solution.py:531
  77.4 5.1 %collective-permute-done.16.refs_5_ = bf16[256,1024]{1,0:T(8,128)(2,1)S(1)} collective-permute-done((bf16[256,1024]{1,0:T(8,128)(2,1)S(1)}, bf16[256,1024]{1,0:T(8,128)(2,1)S(1)}, u32[]{:S(2)}, u32[]{:S(2)}) %collective-permute-start.16) | collective-permute-done | bytes 524320 | tf_op jit(solution)/shard_map/ppermute | solution.py:531
  82.6 8.4 %collective-permute-done.15.refs_4_ = bf16[256,1024]{1,0:T(8,128)(2,1)S(1)} collective-permute-done((bf16[256,1024]{1,0:T(8,128)(2,1)S(1)}, bf16[256,1024]{1,0:T(8,128)(2,1)S(1)}, u32[]{:S(2)}, u32[]{:S(2)}) %collective-permute-start.15) | collective-permute-done | bytes 524320 | tf_op jit(solution)/shard_map/ppermute | solution.py:531
  91.0 2.7 %collective-permute-done.14.refs_3_ = bf16[256,1024]{1,0:T(8,128)(2,1)S(1)} collective-permute-done((bf16[256,1024]{1,0:T(8,128)(2,1)S(1)}, bf16[256,1024]{1,0:T(8,128)(2,1)S(1)}, u32[]{:S(2)}, u32[]{:S(2)}) %collective-permute-start.14) | collective-permute-done | bytes 524320 | tf_op jit(solution)/shard_map/ppermute | solution.py:531
  93.7 2.9 %collective-permute-done.30.refs_6_ = bf16[1024,128]{1,0:T(8,128)(2,1)S(1)} collective-permute-done((bf16[1024,128]{1,0:T(8,128)(2,1)S(1)}, bf16[1024,128]{1,0:T(8,128)(2,1)S(1)}, u32[]{:S(2)}, u32[]{:S(2)}) %collective-permute-start.30) | collective-permute-done | bytes 262176 | tf_op jit(solution)/shard_map/ppermute | solution.py:531
  96.7 5.8 %collective-permute-done.29.refs_5_ = bf16[1024,128]{1,0:T(8,128)(2,1)S(1)} collective-permute-done((bf16[1024,128]{1,0:T(8,128)(2,1)S(1)}, bf16[1024,128]{1,0:T(8,128)(2,1)S(1)}, u32[]{:S(2)}, u32[]{:S(2)}) %collective-permute-start.29) | collective-permute-done | bytes 262176 | tf_op jit(solution)/shard_map/ppermute | solution.py:531
  103.9 5.8 %shard_map.60 = (f32[1024,1024]{1,0:T(8,128)S(1)}, bf16[1024,1024]{1,0:T(8,128)(2,1)S(1)}) custom-call(s32[3]{0:T(128)S(1)} %compare_select_fusion.1.refs_0_, bf16[1024,1024]{1,0:T(8,128)(2,1)S(1)} %get-tuple-element.35.refs_1_, bf16[256,1024]{1,0:T(8,128)(2,1)S(1)} %shard_map.59.refs_2_, bf16[256,1024]{1,0:T(8,128)(2,1)S(1)} %collective-permute-done.14.refs_3_, ...), custom_call_target="tpu_custom_call" | custom-call | flops 4000000000 | bytes 6291462 | tf_op jit(solution)/shard_map/pallas_call | solution.py:537
  109.8 7.8 %shard_map.64 = (bf16[512,128]{1,0:T(8,128)(2,1)S(1)}, bf16[256,512]{1,0:T(8,128)(2,1)S(1)}, bf16[1024,384]{1,0:T(8,128)(2,1)S(1)}) custom-call(s32[3]{0:T(128)S(1)} %compare_select_fusion.1.refs_0_, f32[1024,1024]{1,0:T(8,128)S(1)} %get-tuple-element.38.refs_1_, bf16[1024,1024]{1,0:T(8,128)(2,1)S(1)} %get-tuple-element.39.refs_2_, ...), custom_call_target="tpu_custom_call" | custom-call | flops 12000000000 | bytes 7340038 | tf_op jit(solution)/shard_map/pallas_call | solution.py:537
  117.6 2.4 %shard_map.65.refs_0_.refs_2_ = bf16[512,128]{1,0:T(8,128)(2,1)S(1)} custom-call(s32[3]{0:T(128)S(1)} %compare_select_fusion.1.refs_0_, bf16[1024,384]{1,0:T(8,128)(2,1)S(1)} %get-tuple-element.51.refs_1_), custom_call_target="tpu_custom_call" | custom-call | flops 6000000000 | bytes 786438 | tf_op jit(solution)/shard_map/pallas_call | solution.py:537
  120.0 1.6 %collective-permute-start.39 = (bf16[512,128]{1,0:T(8,128)(2,1)S(1)}, bf16[512,128]{1,0:T(8,128)(2,1)S(1)}, u32[]{:S(2)}, u32[]{:S(2)}) collective-permute-start(bf16[512,128]{1,0:T(8,128)(2,1)S(1)} %shard_map.65.refs_0_.refs_2_), channel_id=1, source_target_pairs={{0,16},{1,17},{2,18},{3,19},{4,20},{5,21},{6,22},{7,23},{8,24},{9,... | collective-permute-start | bytes 393224 | tf_op jit(solution)/shard_map/ppermute | solution.py:531
  124.1 2.4 %collective-permute-done.39.refs_2_.refs_4_ = bf16[512,128]{1,0:T(8,128)(2,1)S(1)} collective-permute-done((bf16[512,128]{1,0:T(8,128)(2,1)S(1)}, bf16[512,128]{1,0:T(8,128)(2,1)S(1)}, u32[]{:S(2)}, u32[]{:S(2)}) %collective-permute-start.39) | collective-permute-done | bytes 131104 | tf_op jit(solution)/shard_map/ppermute | solution.py:531
  126.4 3.5 %collective-permute-done.40.refs_3_.refs_5_ = bf16[512,128]{1,0:T(8,128)(2,1)S(1)} collective-permute-done((bf16[512,128]{1,0:T(8,128)(2,1)S(1)}, bf16[512,128]{1,0:T(8,128)(2,1)S(1)}, u32[]{:S(2)}, u32[]{:S(2)}) %collective-permute-start.40) | collective-permute-done | bytes 131104 | tf_op jit(solution)/shard_map/ppermute | solution.py:531
  134.5 2.1 %collective-permute-start.46 = (bf16[64,512]{1,0:T(8,128)(2,1)S(1)}, bf16[64,512]{1,0:T(8,128)(2,1)S(1)}, u32[]{:S(2)}, u32[]{:S(2)}) collective-permute-start(bf16[64,512]{1,0:T(8,128)(2,1)S(1)} %get-tuple-element.55), channel_id=1, source_target_pairs={{0,8},{1,9},{2,10},{3,11},{4,12},{5,13},{6,14},{7,15},{8,0},{9,1},... | collective-permute-start | bytes 196616 | tf_op jit(solution)/shard_map/ppermute | solution.py:531
  136.6 2.0 %collective-permute-start.47 = (bf16[64,512]{1,0:T(8,128)(2,1)S(1)}, bf16[64,512]{1,0:T(8,128)(2,1)S(1)}, u32[]{:S(2)}, u32[]{:S(2)}) collective-permute-start(bf16[64,512]{1,0:T(8,128)(2,1)S(1)} %get-tuple-element.56), channel_id=1, source_target_pairs={{0,12},{1,13},{2,14},{3,15},{4,8},{5,9},{6,10},{7,11},{8,4},{9,5},... | collective-permute-start | bytes 196616 | tf_op jit(solution)/shard_map/ppermute | solution.py:531
  139.2 3.6 %collective-permute-done.46.refs_3_ = bf16[64,512]{1,0:T(8,128)(2,1)S(1)} collective-permute-done((bf16[64,512]{1,0:T(8,128)(2,1)S(1)}, bf16[64,512]{1,0:T(8,128)(2,1)S(1)}, u32[]{:S(2)}, u32[]{:S(2)}) %collective-permute-start.46) | collective-permute-done | bytes 65568 | tf_op jit(solution)/shard_map/ppermute | solution.py:531
  (80 shorter events, 22.0 us)
Async XLA Ops:
  1.9 11.1 %collective-permute-start.21 = (bf16[4,64,384]{2,1,0:T(8,128)(2,1)S(1)}, bf16[4,64,384]{2,1,0:T(8,128)(2,1)S(1)}, u32[]{:S(2)}, u32[]{:S(2)}) collective-permute-start(bf16[4,64,384]{2,1,0:T(8,128)(2,1)S(1)} %get-tuple-element.43), channel_id=1, source_target_pairs={{0,1},{1,0},{2,3},{3,2},{4,5},{5,4},{6,7},{7,6},{8,9},{9,8},{10,11... | collective-permute-start | bytes 589832 | tf_op jit(solution)/shard_map/ppermute | solution.py:531
  5.0 9.6 %collective-permute-start = (bf16[32,1024]{1,0:T(8,128)(2,1)S(1)}, bf16[32,1024]{1,0:T(8,128)(2,1)S(1)}, u32[]{:S(2)}, u32[]{:S(2)}) collective-permute-start(bf16[32,1024]{1,0:T(8,128)(2,1)S(1)} %get-tuple-element.32), channel_id=1, source_target_pairs={{0,4},{1,5},{2,6},{3,7},{4,0},{5,1},{6,2},{7,3},{8,12},{9,13},{10,... | collective-permute-start | bytes 196616 | tf_op jit(solution)/shard_map/ppermute | solution.py:531
  6.6 8.1 %collective-permute-start.1 = (bf16[32,1024]{1,0:T(8,128)(2,1)S(1)}, bf16[32,1024]{1,0:T(8,128)(2,1)S(1)}, u32[]{:S(2)}, u32[]{:S(2)}) collective-permute-start(bf16[32,1024]{1,0:T(8,128)(2,1)S(1)} %get-tuple-element.33), channel_id=1, source_target_pairs={{0,8},{1,9},{2,10},{3,11},{4,12},{5,13},{6,14},{7,15},{8,0},{9,1},... | collective-permute-start | bytes 196616 | tf_op jit(solution)/shard_map/ppermute | solution.py:531
  10.4 10.8 %collective-permute-start.12 = (bf16[64,1024]{1,0:T(8,128)(2,1)S(1)}, bf16[64,1024]{1,0:T(8,128)(2,1)S(1)}, u32[]{:S(2)}, u32[]{:S(2)}) collective-permute-start(bf16[64,1024]{1,0:T(8,128)(2,1)S(1)} %get-tuple-element.37.refs_0_), channel_id=1, source_target_pairs={{0,8},{1,9},{2,10},{3,11},{4,12},{5,13},{6,14},{7,15},{8,0},{9,1},... | collective-permute-start | bytes 393224 | tf_op jit(solution)/shard_map/ppermute | solution.py:531
  13.0 8.2 %collective-permute-start.22 = (bf16[128,384]{1,0:T(8,128)(2,1)S(1)}, bf16[128,384]{1,0:T(8,128)(2,1)S(1)}, u32[]{:S(2)}, u32[]{:S(2)}) collective-permute-start(bf16[128,384]{1,0:T(8,128)(2,1)S(1)} %get-tuple-element.45), channel_id=1, source_target_pairs={{0,2},{1,3},{2,0},{3,1},{4,6},{5,7},{6,4},{7,5},{8,10},{9,11},{10,... | collective-permute-start | bytes 294920 | tf_op jit(solution)/shard_map/ppermute | solution.py:531
  16.0 18.4 %collective-permute-start.5 = (bf16[128,1024]{1,0:T(8,128)(2,1)S(1)}, bf16[128,1024]{1,0:T(8,128)(2,1)S(1)}, u32[]{:S(2)}, u32[]{:S(2)}) collective-permute-start(bf16[128,1024]{1,0:T(8,128)(2,1)S(1)} %shard_map.56.refs_1_), channel_id=1, source_target_pairs={{0,18},{1,19},{2,16},{3,17},{4,22},{5,23},{6,20},{7,21},{8,26},{9,... | collective-permute-start | bytes 786440 | tf_op jit(solution)/shard_map/ppermute | solution.py:531
  16.9 22.0 %collective-permute-start.4 = (bf16[128,1024]{1,0:T(8,128)(2,1)S(1)}, bf16[128,1024]{1,0:T(8,128)(2,1)S(1)}, u32[]{:S(2)}, u32[]{:S(2)}) collective-permute-start(bf16[128,1024]{1,0:T(8,128)(2,1)S(1)} %shard_map.56.refs_1_), channel_id=1, source_target_pairs={{0,16},{1,17},{2,18},{3,19},{4,20},{5,21},{6,22},{7,23},{8,24},{9,... | collective-permute-start | bytes 786440 | tf_op jit(solution)/shard_map/ppermute | solution.py:531
  19.1 12.7 %collective-permute-start.23 = (bf16[128,384]{1,0:T(8,128)(2,1)S(1)}, bf16[128,384]{1,0:T(8,128)(2,1)S(1)}, u32[]{:S(2)}, u32[]{:S(2)}) collective-permute-start(bf16[128,384]{1,0:T(8,128)(2,1)S(1)} %get-tuple-element.46), channel_id=1, source_target_pairs={{0,16},{1,17},{2,18},{3,19},{4,20},{5,21},{6,22},{7,23},{8,24},{9,... | collective-permute-start | bytes 294920 | tf_op jit(solution)/shard_map/ppermute | solution.py:531
  21.2 17.6 %collective-permute-start.6 = (bf16[128,1024]{1,0:T(8,128)(2,1)S(1)}, bf16[128,1024]{1,0:T(8,128)(2,1)S(1)}, u32[]{:S(2)}, u32[]{:S(2)}) collective-permute-start(bf16[128,1024]{1,0:T(8,128)(2,1)S(1)} %shard_map.56.refs_1_), channel_id=1, source_target_pairs={{0,1},{1,0},{2,3},{3,2},{4,5},{5,4},{6,7},{7,6},{8,9},{9,8},{10,11... | collective-permute-start | bytes 786440 | tf_op jit(solution)/shard_map/ppermute | solution.py:531
  21.2 11.8 %collective-permute-start.24 = (bf16[128,384]{1,0:T(8,128)(2,1)S(1)}, bf16[128,384]{1,0:T(8,128)(2,1)S(1)}, u32[]{:S(2)}, u32[]{:S(2)}) collective-permute-start(bf16[128,384]{1,0:T(8,128)(2,1)S(1)} %get-tuple-element.47), channel_id=1, source_target_pairs={{0,18},{1,19},{2,16},{3,17},{4,22},{5,23},{6,20},{7,21},{8,26},{9,... | collective-permute-start | bytes 294920 | tf_op jit(solution)/shard_map/ppermute | solution.py:531
  34.4 13.8 %collective-permute-start.9 = (bf16[128,1024]{1,0:T(8,128)(2,1)S(1)}, bf16[128,1024]{1,0:T(8,128)(2,1)S(1)}, u32[]{:S(2)}, u32[]{:S(2)}) collective-permute-start(bf16[128,1024]{1,0:T(8,128)(2,1)S(1)} %collective-permute-done.5.refs_4_), channel_id=1, source_target_pairs={{0,1},{1,0},{2,3},{3,2},{4,5},{5,4},{6,7},{7,6},{8,9},{9,8},{10,11... | collective-permute-start | bytes 786440 | tf_op jit(solution)/shard_map/ppermute | solution.py:531
  36.8 11.4 %collective-permute-start.26 = (bf16[256,384]{1,0:T(8,128)(2,1)S(1)}, bf16[256,384]{1,0:T(8,128)(2,1)S(1)}, u32[]{:S(2)}, u32[]{:S(2)}) collective-permute-start(bf16[256,384]{1,0:T(8,128)(2,1)S(1)} %get-tuple-element.48.refs_2_), channel_id=1, source_target_pairs={{0,8},{1,9},{2,10},{3,11},{4,12},{5,13},{6,14},{7,15},{8,0},{9,1},... | collective-permute-start | bytes 589832 | tf_op jit(solution)/shard_map/ppermute | solution.py:531
  38.8 11.4 %collective-permute-start.8 = (bf16[128,1024]{1,0:T(8,128)(2,1)S(1)}, bf16[128,1024]{1,0:T(8,128)(2,1)S(1)}, u32[]{:S(2)}, u32[]{:S(2)}) collective-permute-start(bf16[128,1024]{1,0:T(8,128)(2,1)S(1)} %collective-permute-done.4.refs_3_), channel_id=1, source_target_pairs={{0,1},{1,0},{2,3},{3,2},{4,5},{5,4},{6,7},{7,6},{8,9},{9,8},{10,11... | collective-permute-start | bytes 786440 | tf_op jit(solution)/shard_map/ppermute | solution.py:531
  38.9 9.4 %collective-permute-start.13 = (bf16[64,1024]{1,0:T(8,128)(2,1)S(1)}, bf16[64,1024]{1,0:T(8,128)(2,1)S(1)}, u32[]{:S(2)}, u32[]{:S(2)}) collective-permute-start(bf16[64,1024]{1,0:T(8,128)(2,1)S(1)} %collective-permute-done.12.refs_2_), channel_id=1, source_target_pairs={{0,4},{1,5},{2,6},{3,7},{4,0},{5,1},{6,2},{7,3},{8,12},{9,13},{10,... | collective-permute-start | bytes 393224 | tf_op jit(solution)/shard_map/ppermute | solution.py:531
  39.4 11.0 %collective-permute-start.7 = (bf16[128,1024]{1,0:T(8,128)(2,1)S(1)}, bf16[128,1024]{1,0:T(8,128)(2,1)S(1)}, u32[]{:S(2)}, u32[]{:S(2)}) collective-permute-start(bf16[128,1024]{1,0:T(8,128)(2,1)S(1)} %collective-permute-done.3.refs_2_), channel_id=1, source_target_pairs={{0,1},{1,0},{2,3},{3,2},{4,5},{5,4},{6,7},{7,6},{8,9},{9,8},{10,11... | collective-permute-start | bytes 786440 | tf_op jit(solution)/shard_map/ppermute | solution.py:531
  48.2 18.7 %collective-permute-start.36 = (bf16[256,512]{1,0:T(8,128)(2,1)S(1)}, bf16[256,512]{1,0:T(8,128)(2,1)S(1)}, u32[]{:S(2)}, u32[]{:S(2)}) collective-permute-start(bf16[256,512]{1,0:T(8,128)(2,1)S(1)} %get-tuple-element.49.refs_11_.refs_0_), channel_id=1, source_target_pairs={{0,8},{1,9},{2,10},{3,11},{4,12},{5,13},{6,14},{7,15},{8,0},{9,1},... | collective-permute-start | bytes 786440 | tf_op jit(solution)/shard_map/ppermute | solution.py:531
  48.2 20.6 %collective-permute-start.35 = (bf16[256,512]{1,0:T(8,128)(2,1)S(1)}, bf16[256,512]{1,0:T(8,128)(2,1)S(1)}, u32[]{:S(2)}, u32[]{:S(2)}) collective-permute-start(bf16[256,512]{1,0:T(8,128)(2,1)S(1)} %get-tuple-element.49.refs_11_.refs_0_), channel_id=1, source_target_pairs={{0,4},{1,5},{2,6},{3,7},{4,0},{5,1},{6,2},{7,3},{8,12},{9,13},{10,... | collective-permute-start | bytes 786440 | tf_op jit(solution)/shard_map/ppermute | solution.py:531
  48.2 18.6 %collective-permute-start.25 = (bf16[256,384]{1,0:T(8,128)(2,1)S(1)}, bf16[256,384]{1,0:T(8,128)(2,1)S(1)}, u32[]{:S(2)}, u32[]{:S(2)}) collective-permute-start(bf16[256,384]{1,0:T(8,128)(2,1)S(1)} %get-tuple-element.48.refs_2_), channel_id=1, source_target_pairs={{0,4},{1,5},{2,6},{3,7},{4,0},{5,1},{6,2},{7,3},{8,12},{9,13},{10,... | collective-permute-start | bytes 589832 | tf_op jit(solution)/shard_map/ppermute | solution.py:531
  50.3 20.1 %collective-permute-start.27 = (bf16[256,384]{1,0:T(8,128)(2,1)S(1)}, bf16[256,384]{1,0:T(8,128)(2,1)S(1)}, u32[]{:S(2)}, u32[]{:S(2)}) collective-permute-start(bf16[256,384]{1,0:T(8,128)(2,1)S(1)} %collective-permute-done.26.refs_4_), channel_id=1, source_target_pairs={{0,4},{1,5},{2,6},{3,7},{4,0},{5,1},{6,2},{7,3},{8,12},{9,13},{10,... | collective-permute-start | bytes 589832 | tf_op jit(solution)/shard_map/ppermute | solution.py:531
  50.4 43.3 %collective-permute-start.17 = (bf16[256,1024]{1,0:T(8,128)(2,1)S(1)}, bf16[256,1024]{1,0:T(8,128)(2,1)S(1)}, u32[]{:S(2)}, u32[]{:S(2)}) collective-permute-start(bf16[256,1024]{1,0:T(8,128)(2,1)S(1)} %shard_map.59.refs_2_), channel_id=1, source_target_pairs={{0,1},{1,0},{2,3},{3,2},{4,5},{5,4},{6,7},{7,6},{8,9},{9,8},{10,11... | collective-permute-start | bytes 1572872 | tf_op jit(solution)/shard_map/ppermute | solution.py:531
  66.9 15.7 %collective-permute-start.16 = (bf16[256,1024]{1,0:T(8,128)(2,1)S(1)}, bf16[256,1024]{1,0:T(8,128)(2,1)S(1)}, u32[]{:S(2)}, u32[]{:S(2)}) collective-permute-start(bf16[256,1024]{1,0:T(8,128)(2,1)S(1)} %shard_map.59.refs_2_), channel_id=1, source_target_pairs={{0,18},{1,19},{2,16},{3,17},{4,22},{5,23},{6,20},{7,21},{8,26},{9,... | collective-permute-start | bytes 1572872 | tf_op jit(solution)/shard_map/ppermute | solution.py:531
  66.9 24.1 %collective-permute-start.15 = (bf16[256,1024]{1,0:T(8,128)(2,1)S(1)}, bf16[256,1024]{1,0:T(8,128)(2,1)S(1)}, u32[]{:S(2)}, u32[]{:S(2)}) collective-permute-start(bf16[256,1024]{1,0:T(8,128)(2,1)S(1)} %shard_map.59.refs_2_), channel_id=1, source_target_pairs={{0,16},{1,17},{2,18},{3,19},{4,20},{5,21},{6,22},{7,23},{8,24},{9,... | collective-permute-start | bytes 1572872 | tf_op jit(solution)/shard_map/ppermute | solution.py:531
  68.9 24.9 %collective-permute-start.14 = (bf16[256,1024]{1,0:T(8,128)(2,1)S(1)}, bf16[256,1024]{1,0:T(8,128)(2,1)S(1)}, u32[]{:S(2)}, u32[]{:S(2)}) collective-permute-start(bf16[256,1024]{1,0:T(8,128)(2,1)S(1)} %shard_map.59.refs_2_), channel_id=1, source_target_pairs={{0,2},{1,3},{2,0},{3,1},{4,6},{5,7},{6,4},{7,5},{8,10},{9,11},{10,... | collective-permute-start | bytes 1572872 | tf_op jit(solution)/shard_map/ppermute | solution.py:531
  77.4 19.2 %collective-permute-start.30 = (bf16[1024,128]{1,0:T(8,128)(2,1)S(1)}, bf16[1024,128]{1,0:T(8,128)(2,1)S(1)}, u32[]{:S(2)}, u32[]{:S(2)}) collective-permute-start(bf16[1024,128]{1,0:T(8,128)(2,1)S(1)} %shard_map.63.refs_3_), channel_id=1, source_target_pairs={{0,18},{1,19},{2,16},{3,17},{4,22},{5,23},{6,20},{7,21},{8,26},{9,... | collective-permute-start | bytes 786440 | tf_op jit(solution)/shard_map/ppermute | solution.py:531
  82.6 20.7 %collective-permute-start.20 = (bf16[256,1024]{1,0:T(8,128)(2,1)S(1)}, bf16[256,1024]{1,0:T(8,128)(2,1)S(1)}, u32[]{:S(2)}, u32[]{:S(2)}) collective-permute-start(bf16[256,1024]{1,0:T(8,128)(2,1)S(1)} %collective-permute-done.16.refs_5_), channel_id=1, source_target_pairs={{0,1},{1,0},{2,3},{3,2},{4,5},{5,4},{6,7},{7,6},{8,9},{9,8},{10,11... | collective-permute-start | bytes 1572872 | tf_op jit(solution)/shard_map/ppermute | solution.py:531
  91.0 12.4 %collective-permute-start.19 = (bf16[256,1024]{1,0:T(8,128)(2,1)S(1)}, bf16[256,1024]{1,0:T(8,128)(2,1)S(1)}, u32[]{:S(2)}, u32[]{:S(2)}) collective-permute-start(bf16[256,1024]{1,0:T(8,128)(2,1)S(1)} %collective-permute-done.15.refs_4_), channel_id=1, source_target_pairs={{0,1},{1,0},{2,3},{3,2},{4,5},{5,4},{6,7},{7,6},{8,9},{9,8},{10,11... | collective-permute-start | bytes 1572872 | tf_op jit(solution)/shard_map/ppermute | solution.py:531
  93.7 10.1 %collective-permute-start.18 = (bf16[256,1024]{1,0:T(8,128)(2,1)S(1)}, bf16[256,1024]{1,0:T(8,128)(2,1)S(1)}, u32[]{:S(2)}, u32[]{:S(2)}) collective-permute-start(bf16[256,1024]{1,0:T(8,128)(2,1)S(1)} %collective-permute-done.14.refs_3_), channel_id=1, source_target_pairs={{0,1},{1,0},{2,3},{3,2},{4,5},{5,4},{6,7},{7,6},{8,9},{9,8},{10,11... | collective-permute-start | bytes 1572872 | tf_op jit(solution)/shard_map/ppermute | solution.py:531
  93.7 8.7 %collective-permute-start.29 = (bf16[1024,128]{1,0:T(8,128)(2,1)S(1)}, bf16[1024,128]{1,0:T(8,128)(2,1)S(1)}, u32[]{:S(2)}, u32[]{:S(2)}) collective-permute-start(bf16[1024,128]{1,0:T(8,128)(2,1)S(1)} %shard_map.63.refs_3_), channel_id=1, source_target_pairs={{0,16},{1,17},{2,18},{3,19},{4,20},{5,21},{6,22},{7,23},{8,24},{9,... | collective-permute-start | bytes 786440 | tf_op jit(solution)/shard_map/ppermute | solution.py:531
  103.0 20.5 %collective-permute-start.42 = (bf16[256,512]{1,0:T(8,128)(2,1)S(1)}, bf16[256,512]{1,0:T(8,128)(2,1)S(1)}, u32[]{:S(2)}, u32[]{:S(2)}) collective-permute-start(bf16[256,512]{1,0:T(8,128)(2,1)S(1)} %shard_map.67.refs_7_), channel_id=1, source_target_pairs={{0,2},{1,3},{2,0},{3,1},{4,6},{5,7},{6,4},{7,5},{8,10},{9,11},{10,... | collective-permute-start | bytes 786440 | tf_op jit(solution)/shard_map/ppermute | solution.py:531
  121.6 8.3 %collective-permute-start.40 = (bf16[512,128]{1,0:T(8,128)(2,1)S(1)}, bf16[512,128]{1,0:T(8,128)(2,1)S(1)}, u32[]{:S(2)}, u32[]{:S(2)}) collective-permute-start(bf16[512,128]{1,0:T(8,128)(2,1)S(1)} %get-tuple-element.52), channel_id=1, source_target_pairs={{0,18},{1,19},{2,16},{3,17},{4,22},{5,23},{6,20},{7,21},{8,26},{9,... | collective-permute-start | bytes 393224 | tf_op jit(solution)/shard_map/ppermute | solution.py:531
  123.2 8.1 %collective-permute-start.38 = (bf16[512,128]{1,0:T(8,128)(2,1)S(1)}, bf16[512,128]{1,0:T(8,128)(2,1)S(1)}, u32[]{:S(2)}, u32[]{:S(2)}) collective-permute-start(bf16[512,128]{1,0:T(8,128)(2,1)S(1)} %get-tuple-element.52), channel_id=1, source_target_pairs={{0,2},{1,3},{2,0},{3,1},{4,6},{5,7},{6,4},{7,5},{8,10},{9,11},{10,... | collective-permute-start | bytes 393224 | tf_op jit(solution)/shard_map/ppermute | solution.py:531
  134.5 8.3 %collective-permute-start.46 = (bf16[64,512]{1,0:T(8,128)(2,1)S(1)}, bf16[64,512]{1,0:T(8,128)(2,1)S(1)}, u32[]{:S(2)}, u32[]{:S(2)}) collective-permute-start(bf16[64,512]{1,0:T(8,128)(2,1)S(1)} %get-tuple-element.55), channel_id=1, source_target_pairs={{0,8},{1,9},{2,10},{3,11},{4,12},{5,13},{6,14},{7,15},{8,0},{9,1},... | collective-permute-start | bytes 196616 | tf_op jit(solution)/shard_map/ppermute | solution.py:531
  (16 other events, 100.0 us)

commit v6 on v5

--- a/solution.py
+++ b/solution.py
@@ -373,7 +373,7 @@
 
 
 def row_blocks(plan, one_block):
-    size = min(512, plan.tokens)
+    size = min(1024, plan.tokens)
 
     def step(block_no, carry):
         one_block(aligned(block_no, size))
@@ -385,9 +385,12 @@
 def norm_kernel(plan, where, *refs):
     hid, normed = refs[plan.slots :]
     for piece, (mx, mi) in zip(refs, plane_order(plan)):
-        rows = aligned(slot_of(plan, where, mx, mi), plan.shard)
-        hid[rows, :] = piece[...]
-        normed[rows, :] = normalize(piece[...].astype(jnp.float32))
+        hid[aligned(slot_of(plan, where, mx, mi), plan.shard), :] = piece[...]
+
+    def one_block(rows):
+        normed[rows, :] = normalize(hid[rows, :].astype(jnp.float32))
+
+    row_blocks(plan, one_block)
 
 
 def first_kernel(plan, where, normed, *rest):

time: 144 us -> 144 us (level)
  no operation moved by 1% of the time
where the time goes in v6:
time: 144 us
  waiting for transfers between devices  77.1 us (54%)
  starting transfers between devices  37.8 us (26%)
  Pallas kernels  28.7 us (20%)
    ppermute x48, waiting for transfers between devices, swap(): return lax.ppermute(value, ('section', 'seq'), pairs)  77.1 us
    ppermute x48, starting transfers between devices, swap(): return lax.ppermute(value, ('section', 'seq'), pairs)  37.8 us
    pallas_call x15, Pallas kernels, call(): pl.pallas_call(kernel, out_shape=shapes, in_specs=specs or [vmem] * len(i...  28.7 us
  transfers between devices with their start and end apart: 48, of which 20 were waited for; matrix products, arithmetic and copies ran while one was open for 0% of the time, Pallas kernels for 17%

profile of v6, /device:TPU:0, one launch (start us, length us, event | category | flops | bytes accessed | tf_op | source)
XLA Modules:
  0.0 143.8 jit_solution(3783532540838587112)
XLA Ops:
  0.0 1.9 %shard_map.55 = (bf16[32,1024]{1,0:T(8,128)(2,1)S(1)}, bf16[32,1024]{1,0:T(8,128)(2,1)S(1)}, bf16[32,1024]{1,0:T(8,128)(2,1)S(1)}, bf16[32,1024]{1,0:T(8,128)(2,...) custom-call(s32[3]{0:T(128)S(1)} %compare_select_fusion.1.refs_0_, ...), custom_call_target="tpu_custom_call" | custom-call | bytes 1181702 | tf_op jit(solution)/shard_map/pallas_call | solution.py:540
  2.4 2.6 %collective-permute-start.10 = (bf16[128,512]{1,0:T(8,128)(2,1)S(1)}, bf16[128,512]{1,0:T(8,128)(2,1)S(1)}, u32[]{:S(2)}, u32[]{:S(2)}) collective-permute-start(bf16[128,512]{1,0:T(8,128)(2,1)S(1)} %get-tuple-element.36), channel_id=1, source_target_pairs={{0,16},{1,17},{2,18},{3,19},{4,20},{5,21},{6,22},{7,23},{8,24},{9,... | collective-permute-start | bytes 393224 | tf_op jit(solution)/shard_map/ppermute | solution.py:534
  6.6 2.6 %collective-permute-start.1 = (bf16[32,1024]{1,0:T(8,128)(2,1)S(1)}, bf16[32,1024]{1,0:T(8,128)(2,1)S(1)}, u32[]{:S(2)}, u32[]{:S(2)}) collective-permute-start(bf16[32,1024]{1,0:T(8,128)(2,1)S(1)} %get-tuple-element.33), channel_id=1, source_target_pairs={{0,8},{1,9},{2,10},{3,11},{4,12},{5,13},{6,14},{7,15},{8,0},{9,1},... | collective-permute-start | bytes 196616 | tf_op jit(solution)/shard_map/ppermute | solution.py:534
  10.4 2.6 %collective-permute-start.12 = (bf16[64,1024]{1,0:T(8,128)(2,1)S(1)}, bf16[64,1024]{1,0:T(8,128)(2,1)S(1)}, u32[]{:S(2)}, u32[]{:S(2)}) collective-permute-start(bf16[64,1024]{1,0:T(8,128)(2,1)S(1)} %get-tuple-element.37.refs_0_), channel_id=1, source_target_pairs={{0,8},{1,9},{2,10},{3,11},{4,12},{5,13},{6,14},{7,15},{8,0},{9,1},... | collective-permute-start | bytes 393224 | tf_op jit(solution)/shard_map/ppermute | solution.py:534
  13.0 1.6 %collective-permute-start.22 = (bf16[128,384]{1,0:T(8,128)(2,1)S(1)}, bf16[128,384]{1,0:T(8,128)(2,1)S(1)}, u32[]{:S(2)}, u32[]{:S(2)}) collective-permute-start(bf16[128,384]{1,0:T(8,128)(2,1)S(1)} %get-tuple-element.45), channel_id=1, source_target_pairs={{0,2},{1,3},{2,0},{3,1},{4,6},{5,7},{6,4},{7,5},{8,10},{9,11},{10,... | collective-permute-start | bytes 294920 | tf_op jit(solution)/shard_map/ppermute | solution.py:534
  16.9 2.2 %collective-permute-start.4 = (bf16[128,1024]{1,0:T(8,128)(2,1)S(1)}, bf16[128,1024]{1,0:T(8,128)(2,1)S(1)}, u32[]{:S(2)}, u32[]{:S(2)}) collective-permute-start(bf16[128,1024]{1,0:T(8,128)(2,1)S(1)} %shard_map.56.refs_1_), channel_id=1, source_target_pairs={{0,16},{1,17},{2,18},{3,19},{4,20},{5,21},{6,22},{7,23},{8,24},{9,... | collective-permute-start | bytes 786440 | tf_op jit(solution)/shard_map/ppermute | solution.py:534
  19.1 2.1 %collective-permute-done.12.refs_2_ = bf16[64,1024]{1,0:T(8,128)(2,1)S(1)} collective-permute-done((bf16[64,1024]{1,0:T(8,128)(2,1)S(1)}, bf16[64,1024]{1,0:T(8,128)(2,1)S(1)}, u32[]{:S(2)}, u32[]{:S(2)}) %collective-permute-start.12) | collective-permute-done | bytes 131104 | tf_op jit(solution)/shard_map/ppermute | solution.py:534
  21.2 2.8 %collective-permute-start.24 = (bf16[128,384]{1,0:T(8,128)(2,1)S(1)}, bf16[128,384]{1,0:T(8,128)(2,1)S(1)}, u32[]{:S(2)}, u32[]{:S(2)}) collective-permute-start(bf16[128,384]{1,0:T(8,128)(2,1)S(1)} %get-tuple-element.47), channel_id=1, source_target_pairs={{0,18},{1,19},{2,16},{3,17},{4,22},{5,23},{6,20},{7,21},{8,26},{9,... | collective-permute-start | bytes 294920 | tf_op jit(solution)/shard_map/ppermute | solution.py:534
  24.0 7.8 %collective-permute-done.23.refs_4_ = bf16[128,384]{1,0:T(8,128)(2,1)S(1)} collective-permute-done((bf16[128,384]{1,0:T(8,128)(2,1)S(1)}, bf16[128,384]{1,0:T(8,128)(2,1)S(1)}, u32[]{:S(2)}, u32[]{:S(2)}) %collective-permute-start.23) | collective-permute-done | bytes 98336 | tf_op jit(solution)/shard_map/ppermute | solution.py:534
  35.0 1.8 %collective-permute-done.11.refs_1_ = bf16[64,1024]{1,0:T(8,128)(2,1)S(1)} collective-permute-done((bf16[64,1024]{1,0:T(8,128)(2,1)S(1)}, bf16[64,1024]{1,0:T(8,128)(2,1)S(1)}, u32[]{:S(2)}, u32[]{:S(2)}) %collective-permute-start.11) | collective-permute-done | bytes 131104 | tf_op jit(solution)/shard_map/ppermute | solution.py:534
  36.8 2.0 %collective-permute-start.26 = (bf16[256,384]{1,0:T(8,128)(2,1)S(1)}, bf16[256,384]{1,0:T(8,128)(2,1)S(1)}, u32[]{:S(2)}, u32[]{:S(2)}) collective-permute-start(bf16[256,384]{1,0:T(8,128)(2,1)S(1)} %get-tuple-element.48.refs_2_), channel_id=1, source_target_pairs={{0,8},{1,9},{2,10},{3,11},{4,12},{5,13},{6,14},{7,15},{8,0},{9,1},... | collective-permute-start | bytes 589832 | tf_op jit(solution)/shard_map/ppermute | solution.py:534
  39.4 8.8 %collective-permute-done.13.refs_3_ = bf16[64,1024]{1,0:T(8,128)(2,1)S(1)} collective-permute-done((bf16[64,1024]{1,0:T(8,128)(2,1)S(1)}, bf16[64,1024]{1,0:T(8,128)(2,1)S(1)}, u32[]{:S(2)}, u32[]{:S(2)}) %collective-permute-start.13) | collective-permute-done | bytes 131104 | tf_op jit(solution)/shard_map/ppermute | solution.py:534
  48.2 2.0 %collective-permute-start.25 = (bf16[256,384]{1,0:T(8,128)(2,1)S(1)}, bf16[256,384]{1,0:T(8,128)(2,1)S(1)}, u32[]{:S(2)}, u32[]{:S(2)}) collective-permute-start(bf16[256,384]{1,0:T(8,128)(2,1)S(1)} %get-tuple-element.48.refs_2_), channel_id=1, source_target_pairs={{0,4},{1,5},{2,6},{3,7},{4,0},{5,1},{6,2},{7,3},{8,12},{9,13},{10,... | collective-permute-start | bytes 589832 | tf_op jit(solution)/shard_map/ppermute | solution.py:534
  50.5 1.9 %shard_map.57 = (bf16[1024,1024]{1,0:T(8,128)(2,1)S(1)}, bf16[1024,1024]{1,0:T(8,128)(2,1)S(1)}) custom-call(s32[3]{0:T(128)S(1)} %compare_select_fusion.1.refs_0_, bf16[128,1024]{1,0:T(8,128)(2,1)S(1)} %shard_map.56.refs_1_, bf16[128,1024]{1,0:T(8,128)(2,1)S(1)} %collective-permute-done.3.refs_2_, bf16[128,1024]{1,0:T(8,128)(2,1)S(1)} %collective-permute-done.4.refs_3_, ...), custom_call_target="tpu_custom_call" | custom-call | bytes 2097158 | tf_op jit(solution)/shard_map/pallas_call | solution.py:540
  52.4 14.5 %collective-permute-done.25.refs_3_ = bf16[256,384]{1,0:T(8,128)(2,1)S(1)} collective-permute-done((bf16[256,384]{1,0:T(8,128)(2,1)S(1)}, bf16[256,384]{1,0:T(8,128)(2,1)S(1)}, u32[]{:S(2)}, u32[]{:S(2)}) %collective-permute-start.25) | collective-permute-done | bytes 196640 | tf_op jit(solution)/shard_map/ppermute | solution.py:534
  66.9 1.9 %collective-permute-start.15 = (bf16[256,1024]{1,0:T(8,128)(2,1)S(1)}, bf16[256,1024]{1,0:T(8,128)(2,1)S(1)}, u32[]{:S(2)}, u32[]{:S(2)}) collective-permute-start(bf16[256,1024]{1,0:T(8,128)(2,1)S(1)} %shard_map.59.refs_2_), channel_id=1, source_target_pairs={{0,16},{1,17},{2,18},{3,19},{4,20},{5,21},{6,22},{7,23},{8,24},{9,... | collective-permute-start | bytes 1572872 | tf_op jit(solution)/shard_map/ppermute | solution.py:534
  70.7 5.0 %shard_map.63.refs_3_ = bf16[1024,128]{1,0:T(8,128)(2,1)S(1)} custom-call(s32[3]{0:T(128)S(1)} %compare_select_fusion.1.refs_0_, bf16[1024,1024]{1,0:T(8,128)(2,1)S(1)} %get-tuple-element.40.refs_1_, bf16[256,384]{1,0:T(8,128)(2,1)S(1)} %get-tuple-element.48.refs_2_, bf16[256,384]{1,0:T(8,128)(2,1)S(1)} %collective-permute-done.25.refs_3_, ...), custom_call_target="tpu_custom_call" | custom-call | flops 10000000000 | bytes 2883590 | tf_op jit(solution)/shard_map/pallas_call | solution.py:540
  75.7 1.7 %collective-permute-done.37.refs_14_.refs_3_ = bf16[256,512]{1,0:T(8,128)(2,1)S(1)} collective-permute-done((bf16[256,512]{1,0:T(8,128)(2,1)S(1)}, bf16[256,512]{1,0:T(8,128)(2,1)S(1)}, u32[]{:S(2)}, u32[]{:S(2)}) %collective-permute-start.37) | collective-permute-done | bytes 262176 | tf_op jit(solution)/shard_map/ppermute | solution.py:534
  77.4 5.1 %collective-permute-done.16.refs_5_ = bf16[256,1024]{1,0:T(8,128)(2,1)S(1)} collective-permute-done((bf16[256,1024]{1,0:T(8,128)(2,1)S(1)}, bf16[256,1024]{1,0:T(8,128)(2,1)S(1)}, u32[]{:S(2)}, u32[]{:S(2)}) %collective-permute-start.16) | collective-permute-done | bytes 524320 | tf_op jit(solution)/shard_map/ppermute | solution.py:534
  82.6 8.4 %collective-permute-done.15.refs_4_ = bf16[256,1024]{1,0:T(8,128)(2,1)S(1)} collective-permute-done((bf16[256,1024]{1,0:T(8,128)(2,1)S(1)}, bf16[256,1024]{1,0:T(8,128)(2,1)S(1)}, u32[]{:S(2)}, u32[]{:S(2)}) %collective-permute-start.15) | collective-permute-done | bytes 524320 | tf_op jit(solution)/shard_map/ppermute | solution.py:534
  91.0 2.7 %collective-permute-done.14.refs_3_ = bf16[256,1024]{1,0:T(8,128)(2,1)S(1)} collective-permute-done((bf16[256,1024]{1,0:T(8,128)(2,1)S(1)}, bf16[256,1024]{1,0:T(8,128)(2,1)S(1)}, u32[]{:S(2)}, u32[]{:S(2)}) %collective-permute-start.14) | collective-permute-done | bytes 524320 | tf_op jit(solution)/shard_map/ppermute | solution.py:534
  93.7 2.9 %collective-permute-done.30.refs_6_ = bf16[1024,128]{1,0:T(8,128)(2,1)S(1)} collective-permute-done((bf16[1024,128]{1,0:T(8,128)(2,1)S(1)}, bf16[1024,128]{1,0:T(8,128)(2,1)S(1)}, u32[]{:S(2)}, u32[]{:S(2)}) %collective-permute-start.30) | collective-permute-done | bytes 262176 | tf_op jit(solution)/shard_map/ppermute | solution.py:534
  96.7 5.8 %collective-permute-done.29.refs_5_ = bf16[1024,128]{1,0:T(8,128)(2,1)S(1)} collective-permute-done((bf16[1024,128]{1,0:T(8,128)(2,1)S(1)}, bf16[1024,128]{1,0:T(8,128)(2,1)S(1)}, u32[]{:S(2)}, u32[]{:S(2)}) %collective-permute-start.29) | collective-permute-done | bytes 262176 | tf_op jit(solution)/shard_map/ppermute | solution.py:534
  103.9 5.9 %shard_map.60 = (f32[1024,1024]{1,0:T(8,128)S(1)}, bf16[1024,1024]{1,0:T(8,128)(2,1)S(1)}) custom-call(s32[3]{0:T(128)S(1)} %compare_select_fusion.1.refs_0_, bf16[1024,1024]{1,0:T(8,128)(2,1)S(1)} %get-tuple-element.35.refs_1_, bf16[256,1024]{1,0:T(8,128)(2,1)S(1)} %shard_map.59.refs_2_, bf16[256,1024]{1,0:T(8,128)(2,1)S(1)} %collective-permute-done.14.refs_3_, ...), custom_call_target="tpu_custom_call" | custom-call | flops 4000000000 | bytes 6291462 | tf_op jit(solution)/shard_map/pallas_call | solution.py:540
  109.8 7.5 %shard_map.64 = (bf16[512,128]{1,0:T(8,128)(2,1)S(1)}, bf16[256,512]{1,0:T(8,128)(2,1)S(1)}, bf16[1024,384]{1,0:T(8,128)(2,1)S(1)}) custom-call(s32[3]{0:T(128)S(1)} %compare_select_fusion.1.refs_0_, f32[1024,1024]{1,0:T(8,128)S(1)} %get-tuple-element.38.refs_1_, bf16[1024,1024]{1,0:T(8,128)(2,1)S(1)} %get-tuple-element.39.refs_2_, ...), custom_call_target="tpu_custom_call" | custom-call | flops 12000000000 | bytes 7340038 | tf_op jit(solution)/shard_map/pallas_call | solution.py:540
  117.3 2.4 %shard_map.65.refs_0_.refs_2_ = bf16[512,128]{1,0:T(8,128)(2,1)S(1)} custom-call(s32[3]{0:T(128)S(1)} %compare_select_fusion.1.refs_0_, bf16[1024,384]{1,0:T(8,128)(2,1)S(1)} %get-tuple-element.51.refs_1_), custom_call_target="tpu_custom_call" | custom-call | flops 6000000000 | bytes 786438 | tf_op jit(solution)/shard_map/pallas_call | solution.py:540
  119.7 1.6 %collective-permute-start.39 = (bf16[512,128]{1,0:T(8,128)(2,1)S(1)}, bf16[512,128]{1,0:T(8,128)(2,1)S(1)}, u32[]{:S(2)}, u32[]{:S(2)}) collective-permute-start(bf16[512,128]{1,0:T(8,128)(2,1)S(1)} %shard_map.65.refs_0_.refs_2_), channel_id=1, source_target_pairs={{0,16},{1,17},{2,18},{3,19},{4,20},{5,21},{6,22},{7,23},{8,24},{9,... | collective-permute-start | bytes 393224 | tf_op jit(solution)/shard_map/ppermute | solution.py:534
  123.8 2.4 %collective-permute-done.39.refs_2_.refs_4_ = bf16[512,128]{1,0:T(8,128)(2,1)S(1)} collective-permute-done((bf16[512,128]{1,0:T(8,128)(2,1)S(1)}, bf16[512,128]{1,0:T(8,128)(2,1)S(1)}, u32[]{:S(2)}, u32[]{:S(2)}) %collective-permute-start.39) | collective-permute-done | bytes 131104 | tf_op jit(solution)/shard_map/ppermute | solution.py:534
  126.1 3.5 %collective-permute-done.40.refs_3_.refs_5_ = bf16[512,128]{1,0:T(8,128)(2,1)S(1)} collective-permute-done((bf16[512,128]{1,0:T(8,128)(2,1)S(1)}, bf16[512,128]{1,0:T(8,128)(2,1)S(1)}, u32[]{:S(2)}, u32[]{:S(2)}) %collective-permute-start.40) | collective-permute-done | bytes 131104 | tf_op jit(solution)/shard_map/ppermute | solution.py:534
  134.2 2.1 %collective-permute-start.46 = (bf16[64,512]{1,0:T(8,128)(2,1)S(1)}, bf16[64,512]{1,0:T(8,128)(2,1)S(1)}, u32[]{:S(2)}, u32[]{:S(2)}) collective-permute-start(bf16[64,512]{1,0:T(8,128)(2,1)S(1)} %get-tuple-element.55), channel_id=1, source_target_pairs={{0,8},{1,9},{2,10},{3,11},{4,12},{5,13},{6,14},{7,15},{8,0},{9,1},... | collective-permute-start | bytes 196616 | tf_op jit(solution)/shard_map/ppermute | solution.py:534
  136.3 2.0 %collective-permute-start.47 = (bf16[64,512]{1,0:T(8,128)(2,1)S(1)}, bf16[64,512]{1,0:T(8,128)(2,1)S(1)}, u32[]{:S(2)}, u32[]{:S(2)}) collective-permute-start(bf16[64,512]{1,0:T(8,128)(2,1)S(1)} %get-tuple-element.56), channel_id=1, source_target_pairs={{0,12},{1,13},{2,14},{3,15},{4,8},{5,9},{6,10},{7,11},{8,4},{9,5},... | collective-permute-start | bytes 196616 | tf_op jit(solution)/shard_map/ppermute | solution.py:534
  138.9 3.6 %collective-permute-done.46.refs_3_ = bf16[64,512]{1,0:T(8,128)(2,1)S(1)} collective-permute-done((bf16[64,512]{1,0:T(8,128)(2,1)S(1)}, bf16[64,512]{1,0:T(8,128)(2,1)S(1)}, u32[]{:S(2)}, u32[]{:S(2)}) %collective-permute-start.46) | collective-permute-done | bytes 65568 | tf_op jit(solution)/shard_map/ppermute | solution.py:534
  (80 shorter events, 22.0 us)
Async XLA Ops:
  1.9 11.1 %collective-permute-start.21 = (bf16[4,64,384]{2,1,0:T(8,128)(2,1)S(1)}, bf16[4,64,384]{2,1,0:T(8,128)(2,1)S(1)}, u32[]{:S(2)}, u32[]{:S(2)}) collective-permute-start(bf16[4,64,384]{2,1,0:T(8,128)(2,1)S(1)} %get-tuple-element.43), channel_id=1, source_target_pairs={{0,1},{1,0},{2,3},{3,2},{4,5},{5,4},{6,7},{7,6},{8,9},{9,8},{10,11... | collective-permute-start | bytes 589832 | tf_op jit(solution)/shard_map/ppermute | solution.py:534
  5.0 9.6 %collective-permute-start = (bf16[32,1024]{1,0:T(8,128)(2,1)S(1)}, bf16[32,1024]{1,0:T(8,128)(2,1)S(1)}, u32[]{:S(2)}, u32[]{:S(2)}) collective-permute-start(bf16[32,1024]{1,0:T(8,128)(2,1)S(1)} %get-tuple-element.32), channel_id=1, source_target_pairs={{0,4},{1,5},{2,6},{3,7},{4,0},{5,1},{6,2},{7,3},{8,12},{9,13},{10,... | collective-permute-start | bytes 196616 | tf_op jit(solution)/shard_map/ppermute | solution.py:534
  6.6 8.1 %collective-permute-start.1 = (bf16[32,1024]{1,0:T(8,128)(2,1)S(1)}, bf16[32,1024]{1,0:T(8,128)(2,1)S(1)}, u32[]{:S(2)}, u32[]{:S(2)}) collective-permute-start(bf16[32,1024]{1,0:T(8,128)(2,1)S(1)} %get-tuple-element.33), channel_id=1, source_target_pairs={{0,8},{1,9},{2,10},{3,11},{4,12},{5,13},{6,14},{7,15},{8,0},{9,1},... | collective-permute-start | bytes 196616 | tf_op jit(solution)/shard_map/ppermute | solution.py:534
  10.4 10.8 %collective-permute-start.12 = (bf16[64,1024]{1,0:T(8,128)(2,1)S(1)}, bf16[64,1024]{1,0:T(8,128)(2,1)S(1)}, u32[]{:S(2)}, u32[]{:S(2)}) collective-permute-start(bf16[64,1024]{1,0:T(8,128)(2,1)S(1)} %get-tuple-element.37.refs_0_), channel_id=1, source_target_pairs={{0,8},{1,9},{2,10},{3,11},{4,12},{5,13},{6,14},{7,15},{8,0},{9,1},... | collective-permute-start | bytes 393224 | tf_op jit(solution)/shard_map/ppermute | solution.py:534
  13.0 8.2 %collective-permute-start.22 = (bf16[128,384]{1,0:T(8,128)(2,1)S(1)}, bf16[128,384]{1,0:T(8,128)(2,1)S(1)}, u32[]{:S(2)}, u32[]{:S(2)}) collective-permute-start(bf16[128,384]{1,0:T(8,128)(2,1)S(1)} %get-tuple-element.45), channel_id=1, source_target_pairs={{0,2},{1,3},{2,0},{3,1},{4,6},{5,7},{6,4},{7,5},{8,10},{9,11},{10,... | collective-permute-start | bytes 294920 | tf_op jit(solution)/shard_map/ppermute | solution.py:534
  16.0 18.4 %collective-permute-start.5 = (bf16[128,1024]{1,0:T(8,128)(2,1)S(1)}, bf16[128,1024]{1,0:T(8,128)(2,1)S(1)}, u32[]{:S(2)}, u32[]{:S(2)}) collective-permute-start(bf16[128,1024]{1,0:T(8,128)(2,1)S(1)} %shard_map.56.refs_1_), channel_id=1, source_target_pairs={{0,18},{1,19},{2,16},{3,17},{4,22},{5,23},{6,20},{7,21},{8,26},{9,... | collective-permute-start | bytes 786440 | tf_op jit(solution)/shard_map/ppermute | solution.py:534
  16.9 22.0 %collective-permute-start.4 = (bf16[128,1024]{1,0:T(8,128)(2,1)S(1)}, bf16[128,1024]{1,0:T(8,128)(2,1)S(1)}, u32[]{:S(2)}, u32[]{:S(2)}) collective-permute-start(bf16[128,1024]{1,0:T(8,128)(2,1)S(1)} %shard_map.56.refs_1_), channel_id=1, source_target_pairs={{0,16},{1,17},{2,18},{3,19},{4,20},{5,21},{6,22},{7,23},{8,24},{9,... | collective-permute-start | bytes 786440 | tf_op jit(solution)/shard_map/ppermute | solution.py:534
  19.1 12.7 %collective-permute-start.23 = (bf16[128,384]{1,0:T(8,128)(2,1)S(1)}, bf16[128,384]{1,0:T(8,128)(2,1)S(1)}, u32[]{:S(2)}, u32[]{:S(2)}) collective-permute-start(bf16[128,384]{1,0:T(8,128)(2,1)S(1)} %get-tuple-element.46), channel_id=1, source_target_pairs={{0,16},{1,17},{2,18},{3,19},{4,20},{5,21},{6,22},{7,23},{8,24},{9,... | collective-permute-start | bytes 294920 | tf_op jit(solution)/shard_map/ppermute | solution.py:534
  21.2 17.6 %collective-permute-start.6 = (bf16[128,1024]{1,0:T(8,128)(2,1)S(1)}, bf16[128,1024]{1,0:T(8,128)(2,1)S(1)}, u32[]{:S(2)}, u32[]{:S(2)}) collective-permute-start(bf16[128,1024]{1,0:T(8,128)(2,1)S(1)} %shard_map.56.refs_1_), channel_id=1, source_target_pairs={{0,1},{1,0},{2,3},{3,2},{4,5},{5,4},{6,7},{7,6},{8,9},{9,8},{10,11... | collective-permute-start | bytes 786440 | tf_op jit(solution)/shard_map/ppermute | solution.py:534
  21.2 11.8 %collective-permute-start.24 = (bf16[128,384]{1,0:T(8,128)(2,1)S(1)}, bf16[128,384]{1,0:T(8,128)(2,1)S(1)}, u32[]{:S(2)}, u32[]{:S(2)}) collective-permute-start(bf16[128,384]{1,0:T(8,128)(2,1)S(1)} %get-tuple-element.47), channel_id=1, source_target_pairs={{0,18},{1,19},{2,16},{3,17},{4,22},{5,23},{6,20},{7,21},{8,26},{9,... | collective-permute-start | bytes 294920 | tf_op jit(solution)/shard_map/ppermute | solution.py:534
  34.4 13.8 %collective-permute-start.9 = (bf16[128,1024]{1,0:T(8,128)(2,1)S(1)}, bf16[128,1024]{1,0:T(8,128)(2,1)S(1)}, u32[]{:S(2)}, u32[]{:S(2)}) collective-permute-start(bf16[128,1024]{1,0:T(8,128)(2,1)S(1)} %collective-permute-done.5.refs_4_), channel_id=1, source_target_pairs={{0,1},{1,0},{2,3},{3,2},{4,5},{5,4},{6,7},{7,6},{8,9},{9,8},{10,11... | collective-permute-start | bytes 786440 | tf_op jit(solution)/shard_map/ppermute | solution.py:534
  36.8 11.4 %collective-permute-start.26 = (bf16[256,384]{1,0:T(8,128)(2,1)S(1)}, bf16[256,384]{1,0:T(8,128)(2,1)S(1)}, u32[]{:S(2)}, u32[]{:S(2)}) collective-permute-start(bf16[256,384]{1,0:T(8,128)(2,1)S(1)} %get-tuple-element.48.refs_2_), channel_id=1, source_target_pairs={{0,8},{1,9},{2,10},{3,11},{4,12},{5,13},{6,14},{7,15},{8,0},{9,1},... | collective-permute-start | bytes 589832 | tf_op jit(solution)/shard_map/ppermute | solution.py:534
  38.8 11.4 %collective-permute-start.8 = (bf16[128,1024]{1,0:T(8,128)(2,1)S(1)}, bf16[128,1024]{1,0:T(8,128)(2,1)S(1)}, u32[]{:S(2)}, u32[]{:S(2)}) collective-permute-start(bf16[128,1024]{1,0:T(8,128)(2,1)S(1)} %collective-permute-done.4.refs_3_), channel_id=1, source_target_pairs={{0,1},{1,0},{2,3},{3,2},{4,5},{5,4},{6,7},{7,6},{8,9},{9,8},{10,11... | collective-permute-start | bytes 786440 | tf_op jit(solution)/shard_map/ppermute | solution.py:534
  38.9 9.4 %collective-permute-start.13 = (bf16[64,1024]{1,0:T(8,128)(2,1)S(1)}, bf16[64,1024]{1,0:T(8,128)(2,1)S(1)}, u32[]{:S(2)}, u32[]{:S(2)}) collective-permute-start(bf16[64,1024]{1,0:T(8,128)(2,1)S(1)} %collective-permute-done.12.refs_2_), channel_id=1, source_target_pairs={{0,4},{1,5},{2,6},{3,7},{4,0},{5,1},{6,2},{7,3},{8,12},{9,13},{10,... | collective-permute-start | bytes 393224 | tf_op jit(solution)/shard_map/ppermute | solution.py:534
  39.4 11.0 %collective-permute-start.7 = (bf16[128,1024]{1,0:T(8,128)(2,1)S(1)}, bf16[128,1024]{1,0:T(8,128)(2,1)S(1)}, u32[]{:S(2)}, u32[]{:S(2)}) collective-permute-start(bf16[128,1024]{1,0:T(8,128)(2,1)S(1)} %collective-permute-done.3.refs_2_), channel_id=1, source_target_pairs={{0,1},{1,0},{2,3},{3,2},{4,5},{5,4},{6,7},{7,6},{8,9},{9,8},{10,11... | collective-permute-start | bytes 786440 | tf_op jit(solution)/shard_map/ppermute | solution.py:534
  48.2 18.7 %collective-permute-start.36 = (bf16[256,512]{1,0:T(8,128)(2,1)S(1)}, bf16[256,512]{1,0:T(8,128)(2,1)S(1)}, u32[]{:S(2)}, u32[]{:S(2)}) collective-permute-start(bf16[256,512]{1,0:T(8,128)(2,1)S(1)} %get-tuple-element.49.refs_11_.refs_0_), channel_id=1, source_target_pairs={{0,8},{1,9},{2,10},{3,11},{4,12},{5,13},{6,14},{7,15},{8,0},{9,1},... | collective-permute-start | bytes 786440 | tf_op jit(solution)/shard_map/ppermute | solution.py:534
  48.2 20.6 %collective-permute-start.35 = (bf16[256,512]{1,0:T(8,128)(2,1)S(1)}, bf16[256,512]{1,0:T(8,128)(2,1)S(1)}, u32[]{:S(2)}, u32[]{:S(2)}) collective-permute-start(bf16[256,512]{1,0:T(8,128)(2,1)S(1)} %get-tuple-element.49.refs_11_.refs_0_), channel_id=1, source_target_pairs={{0,4},{1,5},{2,6},{3,7},{4,0},{5,1},{6,2},{7,3},{8,12},{9,13},{10,... | collective-permute-start | bytes 786440 | tf_op jit(solution)/shard_map/ppermute | solution.py:534
  48.2 18.6 %collective-permute-start.25 = (bf16[256,384]{1,0:T(8,128)(2,1)S(1)}, bf16[256,384]{1,0:T(8,128)(2,1)S(1)}, u32[]{:S(2)}, u32[]{:S(2)}) collective-permute-start(bf16[256,384]{1,0:T(8,128)(2,1)S(1)} %get-tuple-element.48.refs_2_), channel_id=1, source_target_pairs={{0,4},{1,5},{2,6},{3,7},{4,0},{5,1},{6,2},{7,3},{8,12},{9,13},{10,... | collective-permute-start | bytes 589832 | tf_op jit(solution)/shard_map/ppermute | solution.py:534
  50.3 20.1 %collective-permute-start.27 = (bf16[256,384]{1,0:T(8,128)(2,1)S(1)}, bf16[256,384]{1,0:T(8,128)(2,1)S(1)}, u32[]{:S(2)}, u32[]{:S(2)}) collective-permute-start(bf16[256,384]{1,0:T(8,128)(2,1)S(1)} %collective-permute-done.26.refs_4_), channel_id=1, source_target_pairs={{0,4},{1,5},{2,6},{3,7},{4,0},{5,1},{6,2},{7,3},{8,12},{9,13},{10,... | collective-permute-start | bytes 589832 | tf_op jit(solution)/shard_map/ppermute | solution.py:534
  50.4 43.3 %collective-permute-start.17 = (bf16[256,1024]{1,0:T(8,128)(2,1)S(1)}, bf16[256,1024]{1,0:T(8,128)(2,1)S(1)}, u32[]{:S(2)}, u32[]{:S(2)}) collective-permute-start(bf16[256,1024]{1,0:T(8,128)(2,1)S(1)} %shard_map.59.refs_2_), channel_id=1, source_target_pairs={{0,1},{1,0},{2,3},{3,2},{4,5},{5,4},{6,7},{7,6},{8,9},{9,8},{10,11... | collective-permute-start | bytes 1572872 | tf_op jit(solution)/shard_map/ppermute | solution.py:534
  66.9 15.7 %collective-permute-start.16 = (bf16[256,1024]{1,0:T(8,128)(2,1)S(1)}, bf16[256,1024]{1,0:T(8,128)(2,1)S(1)}, u32[]{:S(2)}, u32[]{:S(2)}) collective-permute-start(bf16[256,1024]{1,0:T(8,128)(2,1)S(1)} %shard_map.59.refs_2_), channel_id=1, source_target_pairs={{0,18},{1,19},{2,16},{3,17},{4,22},{5,23},{6,20},{7,21},{8,26},{9,... | collective-permute-start | bytes 1572872 | tf_op jit(solution)/shard_map/ppermute | solution.py:534
  66.9 24.1 %collective-permute-start.15 = (bf16[256,1024]{1,0:T(8,128)(2,1)S(1)}, bf16[256,1024]{1,0:T(8,128)(2,1)S(1)}, u32[]{:S(2)}, u32[]{:S(2)}) collective-permute-start(bf16[256,1024]{1,0:T(8,128)(2,1)S(1)} %shard_map.59.refs_2_), channel_id=1, source_target_pairs={{0,16},{1,17},{2,18},{3,19},{4,20},{5,21},{6,22},{7,23},{8,24},{9,... | collective-permute-start | bytes 1572872 | tf_op jit(solution)/shard_map/ppermute | solution.py:534
  68.9 24.9 %collective-permute-start.14 = (bf16[256,1024]{1,0:T(8,128)(2,1)S(1)}, bf16[256,1024]{1,0:T(8,128)(2,1)S(1)}, u32[]{:S(2)}, u32[]{:S(2)}) collective-permute-start(bf16[256,1024]{1,0:T(8,128)(2,1)S(1)} %shard_map.59.refs_2_), channel_id=1, source_target_pairs={{0,2},{1,3},{2,0},{3,1},{4,6},{5,7},{6,4},{7,5},{8,10},{9,11},{10,... | collective-permute-start | bytes 1572872 | tf_op jit(solution)/shard_map/ppermute | solution.py:534
  77.4 19.2 %collective-permute-start.30 = (bf16[1024,128]{1,0:T(8,128)(2,1)S(1)}, bf16[1024,128]{1,0:T(8,128)(2,1)S(1)}, u32[]{:S(2)}, u32[]{:S(2)}) collective-permute-start(bf16[1024,128]{1,0:T(8,128)(2,1)S(1)} %shard_map.63.refs_3_), channel_id=1, source_target_pairs={{0,18},{1,19},{2,16},{3,17},{4,22},{5,23},{6,20},{7,21},{8,26},{9,... | collective-permute-start | bytes 786440 | tf_op jit(solution)/shard_map/ppermute | solution.py:534
  82.6 20.7 %collective-permute-start.20 = (bf16[256,1024]{1,0:T(8,128)(2,1)S(1)}, bf16[256,1024]{1,0:T(8,128)(2,1)S(1)}, u32[]{:S(2)}, u32[]{:S(2)}) collective-permute-start(bf16[256,1024]{1,0:T(8,128)(2,1)S(1)} %collective-permute-done.16.refs_5_), channel_id=1, source_target_pairs={{0,1},{1,0},{2,3},{3,2},{4,5},{5,4},{6,7},{7,6},{8,9},{9,8},{10,11... | collective-permute-start | bytes 1572872 | tf_op jit(solution)/shard_map/ppermute | solution.py:534
  91.0 12.4 %collective-permute-start.19 = (bf16[256,1024]{1,0:T(8,128)(2,1)S(1)}, bf16[256,1024]{1,0:T(8,128)(2,1)S(1)}, u32[]{:S(2)}, u32[]{:S(2)}) collective-permute-start(bf16[256,1024]{1,0:T(8,128)(2,1)S(1)} %collective-permute-done.15.refs_4_), channel_id=1, source_target_pairs={{0,1},{1,0},{2,3},{3,2},{4,5},{5,4},{6,7},{7,6},{8,9},{9,8},{10,11... | collective-permute-start | bytes 1572872 | tf_op jit(solution)/shard_map/ppermute | solution.py:534
  93.7 10.1 %collective-permute-start.18 = (bf16[256,1024]{1,0:T(8,128)(2,1)S(1)}, bf16[256,1024]{1,0:T(8,128)(2,1)S(1)}, u32[]{:S(2)}, u32[]{:S(2)}) collective-permute-start(bf16[256,1024]{1,0:T(8,128)(2,1)S(1)} %collective-permute-done.14.refs_3_), channel_id=1, source_target_pairs={{0,1},{1,0},{2,3},{3,2},{4,5},{5,4},{6,7},{7,6},{8,9},{9,8},{10,11... | collective-permute-start | bytes 1572872 | tf_op jit(solution)/shard_map/ppermute | solution.py:534
  93.7 8.7 %collective-permute-start.29 = (bf16[1024,128]{1,0:T(8,128)(2,1)S(1)}, bf16[1024,128]{1,0:T(8,128)(2,1)S(1)}, u32[]{:S(2)}, u32[]{:S(2)}) collective-permute-start(bf16[1024,128]{1,0:T(8,128)(2,1)S(1)} %shard_map.63.refs_3_), channel_id=1, source_target_pairs={{0,16},{1,17},{2,18},{3,19},{4,20},{5,21},{6,22},{7,23},{8,24},{9,... | collective-permute-start | bytes 786440 | tf_op jit(solution)/shard_map/ppermute | solution.py:534
  103.0 20.2 %collective-permute-start.42 = (bf16[256,512]{1,0:T(8,128)(2,1)S(1)}, bf16[256,512]{1,0:T(8,128)(2,1)S(1)}, u32[]{:S(2)}, u32[]{:S(2)}) collective-permute-start(bf16[256,512]{1,0:T(8,128)(2,1)S(1)} %shard_map.67.refs_7_), channel_id=1, source_target_pairs={{0,2},{1,3},{2,0},{3,1},{4,6},{5,7},{6,4},{7,5},{8,10},{9,11},{10,... | collective-permute-start | bytes 786440 | tf_op jit(solution)/shard_map/ppermute | solution.py:534
  121.3 8.3 %collective-permute-start.40 = (bf16[512,128]{1,0:T(8,128)(2,1)S(1)}, bf16[512,128]{1,0:T(8,128)(2,1)S(1)}, u32[]{:S(2)}, u32[]{:S(2)}) collective-permute-start(bf16[512,128]{1,0:T(8,128)(2,1)S(1)} %get-tuple-element.52), channel_id=1, source_target_pairs={{0,18},{1,19},{2,16},{3,17},{4,22},{5,23},{6,20},{7,21},{8,26},{9,... | collective-permute-start | bytes 393224 | tf_op jit(solution)/shard_map/ppermute | solution.py:534
  122.9 8.1 %collective-permute-start.38 = (bf16[512,128]{1,0:T(8,128)(2,1)S(1)}, bf16[512,128]{1,0:T(8,128)(2,1)S(1)}, u32[]{:S(2)}, u32[]{:S(2)}) collective-permute-start(bf16[512,128]{1,0:T(8,128)(2,1)S(1)} %get-tuple-element.52), channel_id=1, source_target_pairs={{0,2},{1,3},{2,0},{3,1},{4,6},{5,7},{6,4},{7,5},{8,10},{9,11},{10,... | collective-permute-start | bytes 393224 | tf_op jit(solution)/shard_map/ppermute | solution.py:534
  134.2 8.3 %collective-permute-start.46 = (bf16[64,512]{1,0:T(8,128)(2,1)S(1)}, bf16[64,512]{1,0:T(8,128)(2,1)S(1)}, u32[]{:S(2)}, u32[]{:S(2)}) collective-permute-start(bf16[64,512]{1,0:T(8,128)(2,1)S(1)} %get-tuple-element.55), channel_id=1, source_target_pairs={{0,8},{1,9},{2,10},{3,11},{4,12},{5,13},{6,14},{7,15},{8,0},{9,1},... | collective-permute-start | bytes 196616 | tf_op jit(solution)/shard_map/ppermute | solution.py:534
  (16 other events, 100.0 us)
